TPU v7x, 32 devices: a whole 2x2x4 slice. The times are simulated.
32 devices in a mesh: group: 1, ctx: 32 (over z, y, x, core).
Axes of the slice: x: 2, y: 2, z: 4, core: 2. Of those that a mesh axis runs over, the one named last changes fastest.
Arguments:
- history: bfloat16 [2, 1024, 8192], P('group', 'ctx'), may hold values from -6 to 6
- lengths: int32 [2], P('group'), may hold values from 256 to 1024
- token_ids: int32 [2, 512], P('group'), may hold values from 0 to 511
- embed: bfloat16 [512, 8192], P('ctx'), may hold values from -6 to 6
- residue: float32 [16, 8192], replicated, may hold values from -0.046875 to 0.046875
- decay: float32 [16, 8192], replicated, may hold values from 0.1 to 400
- skip: float32 [8192], replicated, may hold values from 0.5 to 1.5
Outputs:
- mixed: bfloat16 [2, 512, 8192], P('group', 'ctx')
Inputs may be any that keep to these rules, and one draw needn't show every extreme that they name: `lengths`: history positions at or past a sequence's length are ignored.
All inputs are finite; a program needn't handle non-finite values.
Results may differ from a plain program's by a relative error of at most 0.0005.
Values may be sent and summed in bfloat16 or wider, within the bound.
No kernel may reach another device: no remote copies, remote signals or barrier semaphores. Data moves between devices by JAX's collectives and lax.ppermute only.
A program may use at most 128 MiB of HBM per device.

v0:
```python
import jax
import jax.numpy as jnp
from jax import lax
from jax.sharding import PartitionSpec as P

STEP_LEN = 128


def body(history, lengths, token_ids, embed, residue, decay, skip):
    devices = lax.axis_size("ctx")
    myself = lax.axis_index("ctx")
    seqs, tile, width = history.shape
    narrow = width // devices
    total_len = tile * devices
    rates = decay / total_len
    start = myself * tile
    places = start + jnp.arange(tile, dtype=jnp.int32)
    inside = places[None, :] < lengths[:, None]
    masked = jnp.where(inside[:, :, None], history, jnp.zeros_like(history))
    ends = start + tile
    lift = jnp.maximum(lengths - ends, -tile).astype(jnp.float32)
    spans = (ends - places).astype(jnp.float32)

    def per_mode(rate_row):
        local = jnp.exp(-rate_row[None, :] * spans[:, None])
        part = jnp.sum(local[None, :, :] * masked, axis=1)
        return part * jnp.exp(-rate_row[None, :] * lift[:, None])

    partial_states = lax.map(per_mode, rates)
    summed = lax.psum(partial_states, "ctx")
    mine = lax.dynamic_slice_in_dim(summed, myself * narrow, narrow, 2)
    full_table = lax.all_gather(embed, "ctx", axis=0, tiled=True)
    columns = lax.dynamic_slice_in_dim(full_table, myself * narrow, narrow, 1)
    vocab = columns.shape[0]
    onehot = (token_ids[:, :, None] == jnp.arange(vocab, dtype=jnp.int32)[None, None, :]).astype(
        jnp.bfloat16
    )
    fresh = jnp.einsum("btv,vc->btc", onehot, columns, preferred_element_type=jnp.float32).astype(
        jnp.bfloat16
    )
    my_rates = lax.dynamic_slice_in_dim(rates, myself * narrow, narrow, 1)
    my_residue = lax.dynamic_slice_in_dim(residue, myself * narrow, narrow, 1)
    my_skip = lax.dynamic_slice_in_dim(skip, myself * narrow, narrow, 0)
    generated = token_ids.shape[1]
    steps_count = generated // STEP_LEN
    times = jnp.arange(generated, dtype=jnp.int32).astype(jnp.float32)
    decays = jnp.exp(-my_rates[:, None, :] * times[None, :, None])
    weighted = my_residue[:, None, :] * decays
    history_part = jnp.einsum("ktc,kbc->btc", weighted, mine, precision=lax.Precision.HIGHEST)
    fresh_wide = fresh.astype(jnp.float32)
    pieces = fresh_wide.reshape(seqs, steps_count, STEP_LEN, narrow)
    ladder = jnp.arange(STEP_LEN, dtype=jnp.int32)
    offset = ladder[:, None] - ladder[None, :]
    below = (offset >= 0)[:, :, None]
    gaps = jnp.maximum(offset, 0).astype(jnp.float32)

    def add_mode(index, block):
        rate_row = my_rates[index]
        return block + my_residue[index][None, None, :] * jnp.exp(
            -rate_row[None, None, :] * gaps[:, :, None]
        )

    toeplitz = lax.fori_loop(
        0, my_rates.shape[0], add_mode, jnp.zeros((STEP_LEN, STEP_LEN, narrow), jnp.float32)
    )
    toeplitz = jnp.where(below, toeplitz, 0.0)
    near_part = jnp.einsum("tsc,bjsc->bjtc", toeplitz, pieces, precision=lax.Precision.HIGHEST)
    ladder_f = ladder.astype(jnp.float32)
    into_step = my_residue[:, None, :] * jnp.exp(-my_rates[:, None, :] * ladder_f[None, :, None])
    out_of_step = jnp.exp(-my_rates[:, None, :] * (STEP_LEN - ladder_f)[None, :, None])
    step_decay = jnp.exp(-my_rates * STEP_LEN)
    carry = jnp.zeros((my_rates.shape[0], seqs, narrow), jnp.float32)
    far_blocks = []
    for index in range(steps_count):
        far_blocks.append(
            jnp.einsum("kuc,kbc->buc", into_step, carry, precision=lax.Precision.HIGHEST)
        )
        step_state = jnp.einsum(
            "ksc,bsc->kbc", out_of_step, pieces[:, index], precision=lax.Precision.HIGHEST
        )
        carry = step_decay[:, None, :] * carry + step_state
    far_part = jnp.stack(far_blocks, axis=1)
    conv_part = (near_part + far_part).reshape(seqs, generated, narrow)
    mixed = (history_part + conv_part + my_skip[None, None, :] * fresh_wide).astype(jnp.bfloat16)
    return lax.all_to_all(mixed, "ctx", split_axis=1, concat_axis=2, tiled=True)


def solution(mesh):
    placed = (P("group", "ctx", None), P("group"), P("group", None), P("ctx", None), P(), P(), P())
    return jax.shard_map(
        body, mesh=mesh, in_specs=placed, out_specs=P("group", "ctx", None), check_vma=False
    )
```

profile of v0, /device:TPU:0, one launch (start us, length us, event | category | flops | bytes accessed | tf_op | source)
XLA Modules:
  0.0 337.1 jit_solution(2049569387925838529)
XLA Ops:
  11.2 12.9 %while.25 = (s32[]{:T(128)}, f32[16,2,8192]{2,1,0:T(2,128)S(1)}, f32[16,8192]{1,0:T(8,128)S(1)}, bf16[2,32,8192]{2,1,0:T(8,128)(2,1)S(1)}, f32[2]{0:T(128)S(1)}, /*index=5*/s32[]{:T(128)}, s32[]{:T(128)}, s32[]{:T(128)}) while((s32[]{:T(128)}, f32[16,2,8192]{2,1,0:T(2,128)S(1)}, f32[16,8192]{1,0:T(8,128)S(1)}, ...), condition=%wide.region_2.3_spmd.clone, body=%wide.region_0.2_spmd.clone.sunk | while | flops 1859682 | bytes 3474285 | solution.py:29
  24.1 7.8 %copy.64 = f32[16,2,8192]{0,1,2:T(2,128)} copy(f32[16,2,8192]{2,1,0:T(2,128)S(1)} %get-tuple-element.131) | data formatting | bytes 2097152 | tf_op jit(solution)/shard_map/while | solution.py:29
  32.1 196.6 %while.26 = (s32[]{:T(128)}, f32[128,128,256]{2,1,0:T(8,128)}, f32[16,256]{1,0:T(8,128)S(1)}, f32[16,256]{1,0:T(8,128)S(1)}, s32[]{:T(128)}, /*index=5*/s32[]{:T(128)}) while((s32[]{:T(128)}, f32[128,128,256]{2,1,0:T(8,128)}, f32[16,256]{1,0:T(8,128)S(1)}, f32[16,256]{1,0:T(8,128)S(1)}, s32[]{:T(128)}, /*index=5*/s32[]{:T(128)}) %tuple.55), condition=%wide.region_5.6_spmd.clone, body=%wide.region_4.5_spmd.clone.sunk | while | flops 16826628 | bytes 33691736 | solution.py:63
  32.2 7.0 %select_add_fusion.2 = f32[128,128,256]{2,1,0:T(8,128)} fusion(f32[128,128,256]{2,1,0:T(8,128)} %get-tuple-element.278, f32[128,128]{1,0:T(8,128)S(1)} %maximum_convert_fusion.3, f32[256]{0:T(256)S(1)} %bitcast.86, f32[256]{0:T(256)S(1)} %bitcast.87, pred[]{:T(512)S(6)} %compare.3), kind=kLoop, calls=%fused_computation.8.clone.1 | loop fusion | flops 16777216 | bytes 33622016 | tf_op jit(solution)/shard_map/while/body/eval_jaxpr/add | solution.py:59
  39.3 12.5 %select_add_fusion.2 = f32[128,128,256]{2,1,0:T(8,128)} fusion(f32[128,128,256]{2,1,0:T(8,128)} %get-tuple-element.278, f32[128,128]{1,0:T(8,128)S(1)} %maximum_convert_fusion.3, f32[256]{0:T(256)S(1)} %bitcast.86, f32[256]{0:T(256)S(1)} %bitcast.87, pred[]{:T(512)S(6)} %compare.3), kind=kLoop, calls=%fused_computation.8.clone.1 | loop fusion | flops 16777216 | bytes 33622016 | tf_op jit(solution)/shard_map/while/body/eval_jaxpr/add | solution.py:59
  51.8 12.8 %select_add_fusion.2 = f32[128,128,256]{2,1,0:T(8,128)} fusion(f32[128,128,256]{2,1,0:T(8,128)} %get-tuple-element.278, f32[128,128]{1,0:T(8,128)S(1)} %maximum_convert_fusion.3, f32[256]{0:T(256)S(1)} %bitcast.86, f32[256]{0:T(256)S(1)} %bitcast.87, pred[]{:T(512)S(6)} %compare.3), kind=kLoop, calls=%fused_computation.8.clone.1 | loop fusion | flops 16777216 | bytes 33622016 | tf_op jit(solution)/shard_map/while/body/eval_jaxpr/add | solution.py:59
  64.6 12.5 %select_add_fusion.2 = f32[128,128,256]{2,1,0:T(8,128)} fusion(f32[128,128,256]{2,1,0:T(8,128)} %get-tuple-element.278, f32[128,128]{1,0:T(8,128)S(1)} %maximum_convert_fusion.3, f32[256]{0:T(256)S(1)} %bitcast.86, f32[256]{0:T(256)S(1)} %bitcast.87, pred[]{:T(512)S(6)} %compare.3), kind=kLoop, calls=%fused_computation.8.clone.1 | loop fusion | flops 16777216 | bytes 33622016 | tf_op jit(solution)/shard_map/while/body/eval_jaxpr/add | solution.py:59
  77.2 12.7 %select_add_fusion.2 = f32[128,128,256]{2,1,0:T(8,128)} fusion(f32[128,128,256]{2,1,0:T(8,128)} %get-tuple-element.278, f32[128,128]{1,0:T(8,128)S(1)} %maximum_convert_fusion.3, f32[256]{0:T(256)S(1)} %bitcast.86, f32[256]{0:T(256)S(1)} %bitcast.87, pred[]{:T(512)S(6)} %compare.3), kind=kLoop, calls=%fused_computation.8.clone.1 | loop fusion | flops 16777216 | bytes 33622016 | tf_op jit(solution)/shard_map/while/body/eval_jaxpr/add | solution.py:59
  89.9 12.8 %select_add_fusion.2 = f32[128,128,256]{2,1,0:T(8,128)} fusion(f32[128,128,256]{2,1,0:T(8,128)} %get-tuple-element.278, f32[128,128]{1,0:T(8,128)S(1)} %maximum_convert_fusion.3, f32[256]{0:T(256)S(1)} %bitcast.86, f32[256]{0:T(256)S(1)} %bitcast.87, pred[]{:T(512)S(6)} %compare.3), kind=kLoop, calls=%fused_computation.8.clone.1 | loop fusion | flops 16777216 | bytes 33622016 | tf_op jit(solution)/shard_map/while/body/eval_jaxpr/add | solution.py:59
  102.7 12.6 %select_add_fusion.2 = f32[128,128,256]{2,1,0:T(8,128)} fusion(f32[128,128,256]{2,1,0:T(8,128)} %get-tuple-element.278, f32[128,128]{1,0:T(8,128)S(1)} %maximum_convert_fusion.3, f32[256]{0:T(256)S(1)} %bitcast.86, f32[256]{0:T(256)S(1)} %bitcast.87, pred[]{:T(512)S(6)} %compare.3), kind=kLoop, calls=%fused_computation.8.clone.1 | loop fusion | flops 16777216 | bytes 33622016 | tf_op jit(solution)/shard_map/while/body/eval_jaxpr/add | solution.py:59
  115.4 12.7 %select_add_fusion.2 = f32[128,128,256]{2,1,0:T(8,128)} fusion(f32[128,128,256]{2,1,0:T(8,128)} %get-tuple-element.278, f32[128,128]{1,0:T(8,128)S(1)} %maximum_convert_fusion.3, f32[256]{0:T(256)S(1)} %bitcast.86, f32[256]{0:T(256)S(1)} %bitcast.87, pred[]{:T(512)S(6)} %compare.3), kind=kLoop, calls=%fused_computation.8.clone.1 | loop fusion | flops 16777216 | bytes 33622016 | tf_op jit(solution)/shard_map/while/body/eval_jaxpr/add | solution.py:59
  128.1 12.6 %select_add_fusion.2 = f32[128,128,256]{2,1,0:T(8,128)} fusion(f32[128,128,256]{2,1,0:T(8,128)} %get-tuple-element.278, f32[128,128]{1,0:T(8,128)S(1)} %maximum_convert_fusion.3, f32[256]{0:T(256)S(1)} %bitcast.86, f32[256]{0:T(256)S(1)} %bitcast.87, pred[]{:T(512)S(6)} %compare.3), kind=kLoop, calls=%fused_computation.8.clone.1 | loop fusion | flops 16777216 | bytes 33622016 | tf_op jit(solution)/shard_map/while/body/eval_jaxpr/add | solution.py:59
  140.8 12.5 %select_add_fusion.2 = f32[128,128,256]{2,1,0:T(8,128)} fusion(f32[128,128,256]{2,1,0:T(8,128)} %get-tuple-element.278, f32[128,128]{1,0:T(8,128)S(1)} %maximum_convert_fusion.3, f32[256]{0:T(256)S(1)} %bitcast.86, f32[256]{0:T(256)S(1)} %bitcast.87, pred[]{:T(512)S(6)} %compare.3), kind=kLoop, calls=%fused_computation.8.clone.1 | loop fusion | flops 16777216 | bytes 33622016 | tf_op jit(solution)/shard_map/while/body/eval_jaxpr/add | solution.py:59
  153.4 12.5 %select_add_fusion.2 = f32[128,128,256]{2,1,0:T(8,128)} fusion(f32[128,128,256]{2,1,0:T(8,128)} %get-tuple-element.278, f32[128,128]{1,0:T(8,128)S(1)} %maximum_convert_fusion.3, f32[256]{0:T(256)S(1)} %bitcast.86, f32[256]{0:T(256)S(1)} %bitcast.87, pred[]{:T(512)S(6)} %compare.3), kind=kLoop, calls=%fused_computation.8.clone.1 | loop fusion | flops 16777216 | bytes 33622016 | tf_op jit(solution)/shard_map/while/body/eval_jaxpr/add | solution.py:59
  166.0 12.5 %select_add_fusion.2 = f32[128,128,256]{2,1,0:T(8,128)} fusion(f32[128,128,256]{2,1,0:T(8,128)} %get-tuple-element.278, f32[128,128]{1,0:T(8,128)S(1)} %maximum_convert_fusion.3, f32[256]{0:T(256)S(1)} %bitcast.86, f32[256]{0:T(256)S(1)} %bitcast.87, pred[]{:T(512)S(6)} %compare.3), kind=kLoop, calls=%fused_computation.8.clone.1 | loop fusion | flops 16777216 | bytes 33622016 | tf_op jit(solution)/shard_map/while/body/eval_jaxpr/add | solution.py:59
  178.5 12.6 %select_add_fusion.2 = f32[128,128,256]{2,1,0:T(8,128)} fusion(f32[128,128,256]{2,1,0:T(8,128)} %get-tuple-element.278, f32[128,128]{1,0:T(8,128)S(1)} %maximum_convert_fusion.3, f32[256]{0:T(256)S(1)} %bitcast.86, f32[256]{0:T(256)S(1)} %bitcast.87, pred[]{:T(512)S(6)} %compare.3), kind=kLoop, calls=%fused_computation.8.clone.1 | loop fusion | flops 16777216 | bytes 33622016 | tf_op jit(solution)/shard_map/while/body/eval_jaxpr/add | solution.py:59
  191.1 12.4 %select_add_fusion.2 = f32[128,128,256]{2,1,0:T(8,128)} fusion(f32[128,128,256]{2,1,0:T(8,128)} %get-tuple-element.278, f32[128,128]{1,0:T(8,128)S(1)} %maximum_convert_fusion.3, f32[256]{0:T(256)S(1)} %bitcast.86, f32[256]{0:T(256)S(1)} %bitcast.87, pred[]{:T(512)S(6)} %compare.3), kind=kLoop, calls=%fused_computation.8.clone.1 | loop fusion | flops 16777216 | bytes 33622016 | tf_op jit(solution)/shard_map/while/body/eval_jaxpr/add | solution.py:59
  203.6 12.7 %select_add_fusion.2 = f32[128,128,256]{2,1,0:T(8,128)} fusion(f32[128,128,256]{2,1,0:T(8,128)} %get-tuple-element.278, f32[128,128]{1,0:T(8,128)S(1)} %maximum_convert_fusion.3, f32[256]{0:T(256)S(1)} %bitcast.86, f32[256]{0:T(256)S(1)} %bitcast.87, pred[]{:T(512)S(6)} %compare.3), kind=kLoop, calls=%fused_computation.8.clone.1 | loop fusion | flops 16777216 | bytes 33622016 | tf_op jit(solution)/shard_map/while/body/eval_jaxpr/add | solution.py:59
  216.3 12.5 %select_add_fusion.2 = f32[128,128,256]{2,1,0:T(8,128)} fusion(f32[128,128,256]{2,1,0:T(8,128)} %get-tuple-element.278, f32[128,128]{1,0:T(8,128)S(1)} %maximum_convert_fusion.3, f32[256]{0:T(256)S(1)} %bitcast.86, f32[256]{0:T(256)S(1)} %bitcast.87, pred[]{:T(512)S(6)} %compare.3), kind=kLoop, calls=%fused_computation.8.clone.1 | loop fusion | flops 16777216 | bytes 33622016 | tf_op jit(solution)/shard_map/while/body/eval_jaxpr/add | solution.py:59
  228.7 13.4 %select_bitcast_fusion = f32[128,128,256,1]{2,1,0,3:T(8,128)} fusion(f32[128,128,256]{2,1,0:T(8,128)} %get-tuple-element.132, pred[128,128]{1,0:T(8,128)(4,1)S(1)} %subtract_compare_fusion), kind=kLoop, calls=%fused_computation.12 | loop fusion | flops 4194304 | bytes 33570816 | tf_op jit(solution)/shard_map/jit(_where)/select_n | solution.py:66
  242.2 18.1 %copy.80 = f32[128,128,256,1]{1,0,3,2:T(8,128)} copy(f32[128,128,256,1]{2,1,0,3:T(8,128)} %select_bitcast_fusion) | data formatting | bytes 33554432 | tf_op jit(solution)/shard_map/jit(_where)/select_n | solution.py:66
  261.3 2.8 fusion.18
  264.2 1.5 fusion.19
  267.3 2.2 fusion.34
  269.6 2.8 fusion.17
  272.4 2.2 fusion.36
  274.6 2.8 fusion.16
  277.5 2.2 fusion.38
  279.7 3.0 fusion.15
  282.7 13.1 %fusion.23 = f32[2,4,128,256]{2,1,0,3:T(4,128)S(1)} fusion(bf16[2,4,128,256]{2,1,0,3:T(4,128)(2,1)S(1)} %reshape.164, f32[128,128,256,1]{1,0,3,2:T(8,128)S(1)} %copy-done.2, f32[2,1,128,256]{2,1,0,3:T(1,128)S(1)} %bitcast.85, f32[2,1,128,256]{2,1,0,3:T(1,128)S(1)} %bitcast.84, f32[2,1,128,256]{2,1,0,3:T(1,128)S(1)} %bitcast.83, ...), kind=kOutput, calls=%fused_computation.33 | convolution fusion | flops 403701760 | bytes 19398656 | tf_op jit(solution)/shard_map/tsc,bjsc->bjtc/dot_general | solution.py:67
  296.7 8.1 %fusion.30 = bf16[2,512,256]{1,0,2:T(2,128)(2,1)S(1)} fusion(f32[2,512,256]{1,0,2:T(2,128)S(1)} %reshape.165, f32[512]{0:T(512)S(1)} %iota_convert_fusion, f32[16,256]{0,1:T(8,128)S(1)} %copy.66, f32[16,256]{0,1:T(8,128)S(1)} %copy.65, bf16[2,512,256]{1,0,2:T(2,128)(2,1)S(1)} %copy.67, f32[256]{0:T(256)S(1)} %dynamic_slice.37, ...), kind=kOutput, calls=%fused_computation.36 | convolution fusion | flops 55836672 | bytes 2395140 | tf_op jit(solution)/shard_map/ktc,kbc->btc/dot_general | solution.py:49
  305.8 23.6 %all_to_all.18 = bf16[2,512,256]{2,0,1:T(2,128)(2,1)S(1)} all-to-all(bf16[2,512,256]{2,0,1:T(2,128)(2,1)S(1)} %copy.77), channel_id=1, replica_groups=mesh['group'=1,'ctx'=32] {'ctx'}, dimensions={1} | all-to-all | bytes 1048576 | tf_op jit(solution)/shard_map/all_to_all | solution.py:85
  (154 shorter events, 23.1 us)
Async XLA Ops:
  6.5 25.4 %copy-start = (f32[16,8192]{1,0:T(8,128)S(1)}, f32[16,8192]{1,0:T(8,128)}, u32[]{:S(2)}) copy-start(f32[16,8192]{1,0:T(8,128)} %param.15) | copy-start | bytes 1572868
  6.5 257.6 %all-gather.2.cloned.1.call-start = ((), (), s32[]{:S(2)}) async-start(), calls=%async_computation.2 | async-start | bytes 8650752 | tf_op jit(solution)/shard_map/all_gather | solution.py:32
  7.3 289.4 %all-reduce.2.cloned.1.call-start = ((), (), s32[]{:S(2)}) async-start(), calls=%async_computation.1 | async-start | bytes 16777216 | tf_op jit(solution)/shard_map/psum | solution.py:30
  260.4 3.7 %copy-start.3 = (s32[2,512]{1,0:T(2,128)S(1)}, s32[2,512]{1,0:T(2,128)}, u32[]{:S(2)}) copy-start(s32[2,512]{1,0:T(2,128)} %param.13) | copy-start | bytes 12292
  269.6 13.2 %copy-start.2 = (f32[128,128,256,1]{1,0,3,2:T(8,128)S(1)}, f32[128,128,256,1]{1,0,3,2:T(8,128)}, u32[]{:S(2)}) copy-start(f32[128,128,256,1]{1,0,3,2:T(8,128)} %copy.80) | copy-start | bytes 50331652
  296.7 33.6 %copy-start.1 = (f32[16,8192]{1,0:T(8,128)S(1)}, f32[16,8192]{1,0:T(8,128)}, u32[]{:S(2)}) copy-start(f32[16,8192]{1,0:T(8,128)} %param.15) | copy-start | bytes 1572868
Sparse Core Ops, SparseCore 0:
  10.2 79.7 all-gather.1
  95.7 177.6 all-reduce.1
where the time goes:
time: 338 us; the launch traced here: 337 us
  other arithmetic  226 us (67%)
  matrix products  40.8 us (12%)
  local copies, waits for them, and re-layouts  31.4 us (9%)
  blocking collectives  23.6 us (7%)
  between operations  13.7 us (4%)
    add x16, other arithmetic, add_mode(): block + my_residue[index][None, None, :] * jnp.exp(-rate_row[None, None,...  196 us
    all_to_all x1, blocking collectives, body(): return lax.all_to_all(mixed, 'ctx', split_axis=1, concat_axis=2, tiled=True)  23.6 us
    select_n x1, local copies, waits for them, and re-layouts, body(): toeplitz = jnp.where(below, toeplitz, 0.0)  18.1 us
    select_n x1, other arithmetic, body(): toeplitz = jnp.where(below, toeplitz, 0.0)  13.4 us
    dot_general x1, matrix products, body(): jnp.einsum('tsc,bjsc->bjtc', toeplitz, pieces, precision=lax.Precision.HI...  13.1 us
    dot_general x4, matrix products, body(): jnp.einsum('kuc,kbc->buc', into_step, carry, precision=lax.Precision.HIGH...  11.5 us
    dot_general x1, matrix products, body(): jnp.einsum('ktc,kbc->btc', weighted, mine, precision=lax.Precision.HIGHEST)  8.11 us
    while x1, local copies, waits for them, and re-layouts, body(): partial_states = lax.map(per_mode, rates)  7.76 us
  transfers between devices with their start and end apart: 2, of which 0 were waited for; matrix products, arithmetic and copies ran while one was open for 85% of the time, Pallas kernels for 0%

commit v1 on v0

v1 whole, which is shorter than its diff:
```python
import jax
import jax.numpy as jnp
from jax import lax
from jax.experimental import pallas as pl
from jax.experimental.pallas import tpu as pltpu
from jax.sharding import PartitionSpec as P

ROWS = 8


def lanes_of(block):
    return 256 if block % 256 == 0 else block


def lost(rate):
    series = jnp.ones_like(rate)
    for k in range(12, 1, -1):
        series = 1.0 - rate * series * (1.0 / k)
    return jnp.where(rate < 0.5, rate * series, 1.0 - jnp.exp(-rate))


def merge_rows(parts):
    shape = parts[0].shape
    row = lax.broadcasted_iota(jnp.int32, shape, 0)
    low = row < 4
    level = [
        jnp.where(low, parts[i], parts[i + 4]) + pltpu.roll(jnp.where(low, parts[i + 4], parts[i]), 4, 0)
        for i in range(4)
    ]
    for gap in (2, 1):
        first = (row & gap) == 0
        level = [
            jnp.where(first, level[i], level[i + gap])
            + jnp.where(first, pltpu.roll(level[i], 8 - gap, 0), pltpu.roll(level[i + gap], gap, 0))
            for i in range(gap)
        ]
    return level[0]


def fold(x):
    total = x[:ROWS]
    for start in range(ROWS, x.shape[0], ROWS):
        total = total + x[start : start + ROWS]
    return total


def history_kernel(total_len, where_ref, lengths_ref, own_ref, other_ref, decay_ref, out_ref, wide):
    seqs, tile, block = own_ref.shape
    me = where_ref[0]
    partner = me + 1 - 2 * lax.rem(me, 2)
    row = lax.broadcasted_iota(jnp.int32, (tile, block), 0)
    for side, (ref, owner) in enumerate(((own_ref, me), (other_ref, partner))):
        for b in range(seqs):
            left = lengths_ref[b] - owner * tile
            wide[side, b] = jnp.where(row < left, ref[b].astype(jnp.float32), 0.0)
    lanes = lanes_of(block)
    for start in range(0, block, lanes):
        at = slice(start, start + lanes)
        rate = decay_ref[:, at] / total_len
        keep = jnp.exp(-rate)
        chains = [(side, b) for side in range(2) for b in range(seqs)]

        def step(s, sums):
            return tuple(
                keep * total + wide[side, b, pl.ds(s, 1), at] for (side, b), total in zip(chains, sums)
            )

        zero = jnp.zeros(rate.shape, jnp.float32)
        sums = lax.fori_loop(0, tile, step, (zero,) * len(chains), unroll=8)
        for b in range(seqs):
            total = zero
            for side, owner in enumerate((me, partner)):
                after = jnp.maximum(lengths_ref[b] - (owner + 1) * tile, -tile) + 1
                total = total + sums[side * seqs + b] * jnp.exp(-rate * after.astype(jnp.float32))
            out_ref[0, b, :, at] = total


def fresh_kernel(total_len, where_ref, tokens_ref, table_ref, decay_ref, residue_ref, skip_ref, out_ref, fresh):
    seqs, gen = tokens_ref.shape
    span = out_ref.shape[1]
    vocab, lanes = table_ref.shape
    table = table_ref[...]
    entry = lax.broadcasted_iota(jnp.int32, (vocab, gen), 0)
    for b in range(seqs):
        chosen = jnp.where(entry == tokens_ref[b : b + 1, :], 1.0, 0.0).astype(jnp.bfloat16)
        fresh[b] = lax.dot_general(
            chosen, table, (((0,), (0,)), ((), ())), preferred_element_type=jnp.float32
        )
    rate = decay_ref[...] / total_len
    gone = lost(rate)
    residue = residue_ref[...]
    skip = skip_ref[...]
    skipped = where_ref[1] * span

    def advance(total, b, t):
        return (total + fresh[b, pl.ds(t, 1), :]) - total * gone

    def before(index, sums):
        sums = list(sums)
        for j in range(ROWS):
            sums = [advance(sums[b], b, index * ROWS + j) for b in range(seqs)]
        return tuple(sums)

    def after(index, sums):
        sums = list(sums)
        parts = [[] for _ in range(seqs)]
        first = pl.multiple_of(skipped + index * ROWS, ROWS)
        for j in range(ROWS):
            for b in range(seqs):
                sums[b] = advance(sums[b], b, first + j)
                parts[b].append(fold(residue * sums[b]))
        for b in range(seqs):
            rows = pl.ds(pl.multiple_of(index * ROWS, ROWS), ROWS)
            out_ref[b, rows, :] = merge_rows(parts[b]) + skip * fresh[b, pl.ds(first, ROWS), :]
        return tuple(sums)

    zero = jnp.zeros(rate.shape, jnp.float32)
    sums = lax.fori_loop(0, lax.div(skipped, ROWS), before, (zero,) * seqs)
    lax.fori_loop(0, span // ROWS, after, sums)


def mix_kernel(total_len, where_ref, near_ref, far_ref, fresh_ref, decay_ref, residue_ref, out_ref):
    seqs, span, lanes = fresh_ref.shape
    rate = decay_ref[...] / total_len
    keep = jnp.exp(-rate)
    states = [residue_ref[...] * (near_ref[b] + far_ref[b]) for b in range(seqs)]
    skipped = where_ref[1] * span
    chunk = 2 * ROWS

    def step(index, _):
        first = pl.multiple_of(index * chunk, chunk)
        scale = jnp.exp(-rate * (skipped + first).astype(jnp.float32))
        terms = [states[b] * scale for b in range(seqs)]
        done = [[] for _ in range(seqs)]
        for _ in range(chunk // ROWS):
            parts = [[] for _ in range(seqs)]
            for _ in range(ROWS):
                for b in range(seqs):
                    parts[b].append(fold(terms[b]))
                    terms[b] = terms[b] * keep
            for b in range(seqs):
                done[b].append(merge_rows(parts[b]))
        for b in range(seqs):
            mixed = jnp.concatenate(done[b], axis=0) + fresh_ref[b, pl.ds(first, chunk), :]
            if len(out_ref.shape) == 4:
                own = out_ref.shape[2]
                spot = pl.ds(pl.multiple_of(lax.rem(first, own), chunk), chunk)
                out_ref[lax.div(first, own), b, spot, :] = mixed.astype(jnp.bfloat16)
            else:
                out_ref[b, pl.ds(first, chunk), :] = mixed.astype(jnp.bfloat16)
        return 0

    lax.fori_loop(0, span // chunk, step, 0)


def body(history, lengths, token_ids, embed, residue, decay, skip):
    devices = lax.axis_size("ctx")
    me = lax.axis_index("ctx")
    seqs, tile, width = history.shape
    modes = decay.shape[0]
    gen = token_ids.shape[1]
    total_len = float(tile * devices)
    team = devices // 2
    chips = team // 2
    block = width // team
    lanes = lanes_of(block)
    pieces = block // lanes
    span = gen // 2
    own = gen // devices
    half = me // team
    mine = lax.rem(me, 2) * chips + lax.rem(me, team) // 2
    where = jnp.stack([me, half, mine]).astype(jnp.int32)
    f32 = jnp.float32

    swapped = lax.ppermute(history, "ctx", [(j, j ^ 1) for j in range(devices)])

    rows = embed.shape[0]
    columns = embed.reshape(rows, 2, chips, block).transpose(2, 1, 0, 3).reshape(team, rows, block)
    table = lax.all_to_all(jnp.concatenate([columns, columns]), "ctx", 0, 0, tiled=True)
    table = table.reshape(devices * rows, block)

    part = lambda g, at, ln: (0, 0, lax.rem(at[0], 2) * chips + g)
    partial = pl.pallas_call(
        lambda *refs: history_kernel(total_len, *refs),
        grid_spec=pltpu.PrefetchScalarGridSpec(
            num_scalar_prefetch=2,
            grid=(chips,),
            in_specs=[
                pl.BlockSpec((seqs, tile, block), part),
                pl.BlockSpec((seqs, tile, block), part),
                pl.BlockSpec((modes, block), lambda g, at, ln: part(g, at, ln)[1:]),
            ],
            out_specs=pl.BlockSpec((1, seqs, modes, block), lambda g, at, ln: (g, 0, 0, 0)),
            scratch_shapes=[pltpu.VMEM((2, seqs, tile, block), f32)],
        ),
        out_shape=jax.ShapeDtypeStruct((chips, seqs, modes, block), f32),
        cost_estimate=pl.CostEstimate(
            flops=4 * seqs * tile * modes * block * chips, bytes_accessed=3 * 2**20, transcendentals=0
        ),
        name="history_states",
    )(where, lengths, history, swapped, decay)
    sides = [[h * team + 2 * q + c for q in range(chips)] for h in range(2) for c in range(2)]
    gathered = lax.all_to_all(partial, "ctx", 0, 0, tiled=True, axis_index_groups=sides)
    near = jnp.sum(gathered, axis=0)
    far = lax.ppermute(near, "ctx", [(j, (j + team) % devices) for j in range(devices)])

    strip = lambda g, at: (0, at[2] * pieces + g)
    fresh = pl.pallas_call(
        lambda *refs: fresh_kernel(total_len, *refs),
        grid_spec=pltpu.PrefetchScalarGridSpec(
            num_scalar_prefetch=1,
            grid=(pieces,),
            in_specs=[
                pl.BlockSpec((seqs, gen), lambda g, at: (0, 0)),
                pl.BlockSpec((devices * rows, lanes), lambda g, at: (0, g)),
                pl.BlockSpec((modes, lanes), strip),
                pl.BlockSpec((modes, lanes), strip),
                pl.BlockSpec((1, lanes), strip),
            ],
            out_specs=pl.BlockSpec((seqs, span, lanes), lambda g, at: (0, 0, g)),
            scratch_shapes=[pltpu.VMEM((seqs, gen, lanes), f32)],
        ),
        out_shape=jax.ShapeDtypeStruct((seqs, span, block), f32),
        cost_estimate=pl.CostEstimate(
            flops=6 * seqs * span * modes * block, bytes_accessed=2**21, transcendentals=0
        ),
        name="fresh_scan",
    )(where, token_ids, table, decay, residue, skip.reshape(1, width))

    direct = own % (2 * ROWS) == 0
    state = pl.BlockSpec((seqs, modes, lanes), lambda g, at: (0, 0, g))
    if direct:
        out_shape = (team, seqs, own, block)
        out_spec = pl.BlockSpec((team, seqs, own, lanes), lambda g, at: (0, 0, 0, g))
    else:
        out_shape = (seqs, span, block)
        out_spec = pl.BlockSpec((seqs, span, lanes), lambda g, at: (0, 0, g))
    mixed = pl.pallas_call(
        lambda *refs: mix_kernel(total_len, *refs),
        grid_spec=pltpu.PrefetchScalarGridSpec(
            num_scalar_prefetch=1,
            grid=(pieces,),
            in_specs=[
                state,
                state,
                pl.BlockSpec((seqs, span, lanes), lambda g, at: (0, 0, g)),
                pl.BlockSpec((modes, lanes), strip),
                pl.BlockSpec((modes, lanes), strip),
            ],
            out_specs=out_spec,
        ),
        out_shape=jax.ShapeDtypeStruct(out_shape, jnp.bfloat16),
        cost_estimate=pl.CostEstimate(
            flops=3 * seqs * span * modes * block, bytes_accessed=2**21, transcendentals=0
        ),
        name="mix_states",
    )(where, near, far, fresh, decay, residue)
    if not direct:
        mixed = mixed.reshape(seqs, team, own, block).transpose(1, 0, 2, 3)
    halves = [[h * team + p for p in range(team)] for h in range(2)]
    result = lax.all_to_all(mixed, "ctx", 0, 0, tiled=True, axis_index_groups=halves)
    result = result.reshape(chips, 2, seqs, own, block).transpose(2, 3, 1, 0, 4)
    return result.reshape(seqs, own, width)


def solution(mesh):
    placed = (P("group", "ctx", None), P("group"), P("group", None), P("ctx", None), P(), P(), P())
    return jax.shard_map(
        body, mesh=mesh, in_specs=placed, out_specs=P("group", "ctx", None), check_vma=False
    )
```

time: 338 us -> 78 us (0.23)
  other arithmetic: 226 us -> 1.48 us
  matrix products: 40.8 us -> 0 us
  local copies, waits for them, and re-layouts: 31.4 us -> 3.95 us
  waiting for transfers between devices: 0.77 us -> 24.4 us
  Pallas kernels: 0 us -> 19.9 us
  between operations: 13.7 us -> 0.06 us
  starting transfers between devices: 0.04 us -> 13.2 us
  blocking collectives: 23.6 us -> 14.2 us
    add x17 -> x0, other arithmetic: 196 us -> none  [the longest x16 196 us: add_mode(): block + my_residue[index][None, None, :] * jnp.exp(-rate_row[None, None,...]
    dot_general x10 -> x0, matrix products: 40.8 us -> none  [the longest x1 13.1 us: body(): jnp.einsum('tsc,bjsc->bjtc', toeplitz, pieces, precision=lax.Precision.HI...]
    all_to_all x0 -> x2, waiting for transfers between devices: none -> 22.5 us  [the longest x1 14.2 us: body(): lax.all_to_all(jnp.concatenate([columns, columns]), 'ctx', 0, 0, tiled=True)]
    pallas_call x0 -> x3, Pallas kernels: none -> 19.9 us  [the longest x1 7.88 us: body(): pl.pallas_call(lambda *refs: fresh_kernel(total_len, *refs), grid_spec=pl...]
    select_n x1 -> x0, local copies, waits for them, and re-layouts: 18.1 us -> none  [body(): toeplitz = jnp.where(below, toeplitz, 0.0)]
    select_n x2 -> x0, other arithmetic: 14.8 us -> none  [the longest x1 13.4 us: body(): toeplitz = jnp.where(below, toeplitz, 0.0)]
    all_to_all x0 -> x2, starting transfers between devices: none -> 9.94 us  [the longest x1 6.22 us: body(): lax.all_to_all(partial, 'ctx', 0, 0, tiled=True, axis_index_groups=sides)]
    all_to_all x1, blocking collectives: 23.6 us -> 14.2 us  [body(): lax.all_to_all(mixed, 'ctx', 0, 0, tiled=True, axis_index_groups=halves)]
  transfers between devices with their start and end apart: 2 -> 4, of which waited for: 0 -> 3; matrix products, arithmetic and copies ran while one was open for 85% -> 2% of each run, Pallas kernels for 0% -> 10%
where the time goes in v1:
time: 78 us; the launch traced here: 77.2 us
  waiting for transfers between devices  24.4 us (31%)
  Pallas kernels  19.9 us (26%)
  blocking collectives  14.2 us (18%)
  starting transfers between devices  13.2 us (17%)
  local copies, waits for them, and re-layouts  3.95 us (5%)
  other arithmetic  1.48 us (2%)
    all_to_all x1, waiting for transfers between devices, body(): lax.all_to_all(jnp.concatenate([columns, columns]), 'ctx', 0, 0, tiled=True)  14.2 us
    all_to_all x1, blocking collectives, body(): lax.all_to_all(mixed, 'ctx', 0, 0, tiled=True, axis_index_groups=halves)  14.2 us
    all_to_all x1, waiting for transfers between devices, body(): lax.all_to_all(partial, 'ctx', 0, 0, tiled=True, axis_index_groups=sides)  8.28 us
    pallas_call x1, Pallas kernels, body(): pl.pallas_call(lambda *refs: fresh_kernel(total_len, *refs), grid_spec=pl...  7.88 us
    pallas_call x1, Pallas kernels, body(): pl.pallas_call(lambda *refs: history_kernel(total_len, *refs), grid_spec=...  7.05 us
    all_to_all x1, starting transfers between devices, body(): lax.all_to_all(partial, 'ctx', 0, 0, tiled=True, axis_index_groups=sides)  6.22 us
    pallas_call x1, Pallas kernels, body(): pl.pallas_call(lambda *refs: mix_kernel(total_len, *refs), grid_spec=pltp...  4.98 us
    all_to_all x1, starting transfers between devices, body(): lax.all_to_all(jnp.concatenate([columns, columns]), 'ctx', 0, 0, tiled=True)  3.71 us
  transfers between devices with their start and end apart: 4, of which 3 were waited for; matrix products, arithmetic and copies ran while one was open for 2% of the time, Pallas kernels for 10%

profile of v1, /device:TPU:0, one launch (start us, length us, event | category | flops | bytes accessed | tf_op | source)
XLA Modules:
  0.0 77.2 jit_solution(15081460810628379822)
XLA Ops:
  0.0 0.5 collective-permute-start
  0.5 0.6 pad_add_fusion.refs_0_
  1.1 1.9 %collective-permute-done.refs_3_ = bf16[2,32,8192]{2,1,0:T(8,128)(2,1)S(1)} collective-permute-done((bf16[2,32,8192]{2,1,0:T(8,128)(2,1)}, bf16[2,32,8192]{2,1,0:T(8,128)(2,1)S(1)}, u32[]{:S(2)}, u32[]{:S(2)}) %collective-permute-start) | collective-permute-done | bytes 1048608 | tf_op jit(solution)/shard_map/ppermute | solution.py:175
  3.0 0.0 copy-start.1
  3.0 1.0 %copy-done.1 = bf16[2,32,8192]{2,1,0:T(8,128)(2,1)} copy-done((bf16[2,32,8192]{2,1,0:T(8,128)(2,1)}, bf16[2,32,8192]{2,1,0:T(8,128)(2,1)S(1)}, u32[]{:S(2)}) %copy-start.1) | copy-done | bytes 1048600
  4.0 7.1 %history_states.1 = f32[8,2,16,512]{3,2,1,0:T(8,128)} custom-call(s32[3]{0:T(128)} %pad_add_fusion.refs_0_, s32[2]{0:T(128)} %refs_1_.2, bf16[2,32,8192]{2,1,0:T(8,128)(2,1)} %refs_2_.1, bf16[2,32,8192]{2,1,0:T(8,128)(2,1)} %copy-done.1, f32[16,8192]{1,0:T(8,128)} %refs_4_.5), custom_call_target="tpu_custom_call" | custom-call | flops 16777216 | bytes 3145728 | tf_op jit(solution)/shard_map/history_states/pallas_call | solution.py:183
  11.0 0.0 copy-start.2
  11.0 6.2 %all-to-all-start = ((f32[8,2,16,512]{3,2,1,0:T(8,128)}), f32[8,2,16,512]{3,2,1,0:T(8,128)S(1)}, u32[]{:S(2)}, u32[]{:S(2)}) async-start(f32[8,2,16,512]{3,2,1,0:T(8,128)} %history_states.1), calls=%async_computation | async-start | bytes 1048576 | tf_op jit(solution)/shard_map/all_to_all | solution.py:203
  17.2 0.0 copy-done.2
  17.2 0.1 copy.10
  17.3 0.2 copy.8
  17.5 0.8 %pad_maximum_fusion = bf16[32,16,512]{2,1,0:T(8,128)(2,1)} fusion(bf16[16,16,512]{2,1,0:T(8,128)(2,1)S(1)} %bitcast.18), kind=kLoop, calls=%fused_computation | loop fusion | flops 262144 | bytes 786432 | tf_op jit(solution)/shard_map/concatenate | solution.py:179
  18.3 8.3 %all-to-all-done = f32[8,2,16,512]{3,2,1,0:T(8,128)S(1)} async-done(((f32[8,2,16,512]{3,2,1,0:T(8,128)}), f32[8,2,16,512]{3,2,1,0:T(8,128)S(1)}, u32[]{:S(2)}, u32[]{:S(2)}) %all-to-all-start) | async-done | bytes 524320 | tf_op jit(solution)/shard_map/all_to_all | solution.py:203
  26.6 3.7 %all-to-all-start.1 = ((bf16[32,16,512]{2,1,0:T(8,128)(2,1)}), bf16[32,16,512]{2,1,0:T(8,128)(2,1)S(1)}, u32[]{:S(2)}, u32[]{:S(2)}) async-start(bf16[32,16,512]{2,1,0:T(8,128)(2,1)} %pad_maximum_fusion), calls=%async_computation.1 | async-start | bytes 1048576 | tf_op jit(solution)/shard_map/all_to_all | solution.py:179
  30.4 0.0 copy-start.3
  30.4 2.7 %collective-permute-start.1 = (f32[2,16,512]{2,1,0:T(8,128)S(1)}, f32[2,16,512]{2,1,0:T(8,128)S(1)}, u32[]{:S(2)}, u32[]{:S(2)}) collective-permute-start(f32[2,16,512]{2,1,0:T(8,128)S(1)} %reduce_sum.9.refs_1_), channel_id=1, source_target_pairs={{0,16},{1,17},{2,18},{3,19},{4,20},{5,21},{6,22},{7,23},{8,24},{9,... | collective-permute-start | bytes 196616 | tf_op jit(solution)/shard_map/ppermute | solution.py:205
  33.1 14.2 %all-to-all-done.1 = bf16[32,16,512]{2,1,0:T(8,128)(2,1)S(1)} async-done(((bf16[32,16,512]{2,1,0:T(8,128)(2,1)}), bf16[32,16,512]{2,1,0:T(8,128)(2,1)S(1)}, u32[]{:S(2)}, u32[]{:S(2)}) %all-to-all-start.1) | async-done | bytes 524320 | tf_op jit(solution)/shard_map/all_to_all | solution.py:179
  47.3 0.0 copy-start
  47.3 0.8 %copy-done = bf16[32,16,512]{2,1,0:T(8,128)(2,1)} copy-done((bf16[32,16,512]{2,1,0:T(8,128)(2,1)}, bf16[32,16,512]{2,1,0:T(8,128)(2,1)S(1)}, u32[]{:S(2)}) %copy-start) | copy-done | bytes 524312
  48.1 7.9 %fresh_scan.1.refs_3_ = f32[2,256,512]{2,1,0:T(8,128)} custom-call(s32[3]{0:T(128)} %pad_add_fusion.refs_0_, s32[2,512]{1,0:T(2,128)} %refs_1_.3, bf16[512,512]{1,0:T(8,128)(2,1)} %bitcast.17, f32[16,8192]{1,0:T(8,128)} %refs_4_.5, f32[16,8192]{1,0:T(8,128)} %refs_5_.1, f32[1,8192]{1,0:T(1,128)} %bitcast.21), custom_call_target="tpu_custom_call" | custom-call | flops 25165824 | bytes 2097152 | tf_op jit(solution)/shard_map/fresh_scan/pallas_call | solution.py:208
  56.0 0.0 copy-done.3
  56.0 0.0 collective-permute-done.1.refs_2_
  56.0 0.0 copy-start.4
  56.0 0.6 copy-done.4
  56.7 5.0 %mix_states.1 = bf16[16,2,16,512]{3,2,1,0:T(8,128)(2,1)} custom-call(s32[3]{0:T(128)} %pad_add_fusion.refs_0_, f32[2,16,512]{2,1,0:T(8,128)} %copy-done.3, f32[2,16,512]{2,1,0:T(8,128)} %copy-done.4, f32[2,256,512]{2,1,0:T(8,128)} %fresh_scan.1.refs_3_, f32[16,8192]{1,0:T(8,128)} %refs_4_.5, f32[16,8192]{1,0:T(8,128)} %refs_5_.1), custom_call_target="tpu_custom_call" | custom-call | flops 12582912 | bytes 2097152 | tf_op jit(solution)/shard_map/mix_states/pallas_call | solution.py:238
  61.6 14.2 %all_to_all.15 = bf16[16,2,16,512]{3,2,1,0:T(8,128)(2,1)S(1)} all-to-all(bf16[16,2,16,512]{3,2,1,0:T(8,128)(2,1)} %mix_states.1), channel_id=1, replica_groups={{0,1,2,3,4,5,6,7,8,9,10,11,12,13,14,15},{16,17,18,19,20,21,22,23,24,25,..., dimensions={0} | all-to-all | bytes 1048576 | tf_op jit(solution)/shard_map/all_to_all | solution.py:261
  75.9 0.3 copy.9
  76.1 1.0 %reshape.23 = bf16[2,16,8192]{2,1,0:T(8,128)(2,1)} reshape(bf16[2,16,2,8,512]{4,3,2,1,0:T(8,128)(2,1)S(1)} %copy.9) | data formatting | bytes 1048576 | tf_op jit(solution)/shard_map/reshape | solution.py:263
  (1 shorter events, 0.0 us)
Async XLA Ops:
  0.0 3.0 %collective-permute-start = (bf16[2,32,8192]{2,1,0:T(8,128)(2,1)}, bf16[2,32,8192]{2,1,0:T(8,128)(2,1)S(1)}, u32[]{:S(2)}, u32[]{:S(2)}) collective-permute-start(bf16[2,32,8192]{2,1,0:T(8,128)(2,1)} %refs_2_.1), channel_id=1, source_target_pairs={{0,1},{1,0},{2,3},{3,2},{4,5},{5,4},{6,7},{7,6},{8,9},{9,8},{10,11... | collective-permute-start | bytes 3145736 | tf_op jit(solution)/shard_map/ppermute | solution.py:175
  3.0 1.0 %copy-start.1 = (bf16[2,32,8192]{2,1,0:T(8,128)(2,1)}, bf16[2,32,8192]{2,1,0:T(8,128)(2,1)S(1)}, u32[]{:S(2)}) copy-start(bf16[2,32,8192]{2,1,0:T(8,128)(2,1)S(1)} %collective-permute-done.refs_3_) | copy-start | bytes 3145732
  11.0 6.2 %copy-start.2 = (bf16[16,8192]{1,0:T(8,128)(2,1)S(1)}, bf16[16,8192]{1,0:T(8,128)(2,1)}, u32[]{:S(2)}) copy-start(bf16[16,8192]{1,0:T(8,128)(2,1)} %param.10) | copy-start | bytes 786436
  11.0 15.6 %all-to-all-start = ((f32[8,2,16,512]{3,2,1,0:T(8,128)}), f32[8,2,16,512]{3,2,1,0:T(8,128)S(1)}, u32[]{:S(2)}, u32[]{:S(2)}) async-start(f32[8,2,16,512]{3,2,1,0:T(8,128)} %history_states.1), calls=%async_computation | async-start | bytes 1048576 | tf_op jit(solution)/shard_map/all_to_all | solution.py:203
  26.6 20.7 %all-to-all-start.1 = ((bf16[32,16,512]{2,1,0:T(8,128)(2,1)}), bf16[32,16,512]{2,1,0:T(8,128)(2,1)S(1)}, u32[]{:S(2)}, u32[]{:S(2)}) async-start(bf16[32,16,512]{2,1,0:T(8,128)(2,1)} %pad_maximum_fusion), calls=%async_computation.1 | async-start | bytes 1048576 | tf_op jit(solution)/shard_map/all_to_all | solution.py:179
  30.4 25.7 %copy-start.3 = (f32[2,16,512]{2,1,0:T(8,128)}, f32[2,16,512]{2,1,0:T(8,128)S(1)}, u32[]{:S(2)}) copy-start(f32[2,16,512]{2,1,0:T(8,128)S(1)} %reduce_sum.9.refs_1_) | copy-start | bytes 196612
  30.4 25.6 %collective-permute-start.1 = (f32[2,16,512]{2,1,0:T(8,128)S(1)}, f32[2,16,512]{2,1,0:T(8,128)S(1)}, u32[]{:S(2)}, u32[]{:S(2)}) collective-permute-start(f32[2,16,512]{2,1,0:T(8,128)S(1)} %reduce_sum.9.refs_1_), channel_id=1, source_target_pairs={{0,16},{1,17},{2,18},{3,19},{4,20},{5,21},{6,22},{7,23},{8,24},{9,... | collective-permute-start | bytes 196616 | tf_op jit(solution)/shard_map/ppermute | solution.py:205
  47.3 0.8 %copy-start = (bf16[32,16,512]{2,1,0:T(8,128)(2,1)}, bf16[32,16,512]{2,1,0:T(8,128)(2,1)S(1)}, u32[]{:S(2)}) copy-start(bf16[32,16,512]{2,1,0:T(8,128)(2,1)S(1)} %all-to-all-done.1) | copy-start | bytes 1572868
  56.0 0.6 copy-start.4

commit v2 on v1

--- a/solution.py
+++ b/solution.py
@@ -75,17 +75,19 @@
             out_ref[0, b, :, at] = total
 
 
-def fresh_kernel(total_len, where_ref, tokens_ref, table_ref, decay_ref, residue_ref, skip_ref, out_ref, fresh):
+def fresh_kernel(total_len, where_ref, tokens_ref, table_ref, far_ref, decay_ref, residue_ref, skip_ref, out_ref, fresh):
     seqs, gen = tokens_ref.shape
     span = out_ref.shape[1]
-    vocab, lanes = table_ref.shape
-    table = table_ref[...]
+    vocab = table_ref.shape[0]
     entry = lax.broadcasted_iota(jnp.int32, (vocab, gen), 0)
     for b in range(seqs):
-        chosen = jnp.where(entry == tokens_ref[b : b + 1, :], 1.0, 0.0).astype(jnp.bfloat16)
-        fresh[b] = lax.dot_general(
-            chosen, table, (((0,), (0,)), ((), ())), preferred_element_type=jnp.float32
-        )
+        found = 0.0
+        for ref, side in ((table_ref, where_ref[1]), (far_ref, 1 - where_ref[1])):
+            chosen = jnp.where(entry == tokens_ref[b : b + 1, :] - side * vocab, 1.0, 0.0).astype(jnp.bfloat16)
+            found = found + lax.dot_general(
+                chosen, ref[...], (((0,), (0,)), ((), ())), preferred_element_type=jnp.float32
+            )
+        fresh[b] = found
     rate = decay_ref[...] / total_len
     gone = lost(rate)
     residue = residue_ref[...]
@@ -120,7 +122,7 @@
 
 
 def mix_kernel(total_len, where_ref, near_ref, far_ref, fresh_ref, decay_ref, residue_ref, out_ref):
-    seqs, span, lanes = fresh_ref.shape
+    seqs, span, _ = fresh_ref.shape
     rate = decay_ref[...] / total_len
     keep = jnp.exp(-rate)
     states = [residue_ref[...] * (near_ref[b] + far_ref[b]) for b in range(seqs)]
@@ -175,9 +177,12 @@
     swapped = lax.ppermute(history, "ctx", [(j, j ^ 1) for j in range(devices)])
 
     rows = embed.shape[0]
+    halves = [[h * team + p for p in range(team)] for h in range(2)]
+    opposite = [(j, (j + team) % devices) for j in range(devices)]
     columns = embed.reshape(rows, 2, chips, block).transpose(2, 1, 0, 3).reshape(team, rows, block)
-    table = lax.all_to_all(jnp.concatenate([columns, columns]), "ctx", 0, 0, tiled=True)
-    table = table.reshape(devices * rows, block)
+    table = lax.all_to_all(columns, "ctx", 0, 0, tiled=True, axis_index_groups=halves)
+    table = table.reshape(team * rows, block)
+    table_far = lax.ppermute(table, "ctx", opposite)
 
     part = lambda g, at, ln: (0, 0, lax.rem(at[0], 2) * chips + g)
     partial = pl.pallas_call(
@@ -197,12 +202,13 @@
         cost_estimate=pl.CostEstimate(
             flops=4 * seqs * tile * modes * block * chips, bytes_accessed=3 * 2**20, transcendentals=0
         ),
+        compiler_params=pltpu.CompilerParams(vmem_limit_bytes=16 * 2**20),
         name="history_states",
     )(where, lengths, history, swapped, decay)
     sides = [[h * team + 2 * q + c for q in range(chips)] for h in range(2) for c in range(2)]
     gathered = lax.all_to_all(partial, "ctx", 0, 0, tiled=True, axis_index_groups=sides)
     near = jnp.sum(gathered, axis=0)
-    far = lax.ppermute(near, "ctx", [(j, (j + team) % devices) for j in range(devices)])
+    far = lax.ppermute(near, "ctx", opposite)
 
     strip = lambda g, at: (0, at[2] * pieces + g)
     fresh = pl.pallas_call(
@@ -212,7 +218,8 @@
             grid=(pieces,),
             in_specs=[
                 pl.BlockSpec((seqs, gen), lambda g, at: (0, 0)),
-                pl.BlockSpec((devices * rows, lanes), lambda g, at: (0, g)),
+                pl.BlockSpec((team * rows, lanes), lambda g, at: (0, g)),
+                pl.BlockSpec((team * rows, lanes), lambda g, at: (0, g)),
                 pl.BlockSpec((modes, lanes), strip),
                 pl.BlockSpec((modes, lanes), strip),
                 pl.BlockSpec((1, lanes), strip),
@@ -224,8 +231,9 @@
         cost_estimate=pl.CostEstimate(
             flops=6 * seqs * span * modes * block, bytes_accessed=2**21, transcendentals=0
         ),
+        compiler_params=pltpu.CompilerParams(vmem_limit_bytes=16 * 2**20),
         name="fresh_scan",
-    )(where, token_ids, table, decay, residue, skip.reshape(1, width))
+    )(where, token_ids, table, table_far, decay, residue, skip.reshape(1, width))
 
     direct = own % (2 * ROWS) == 0
     state = pl.BlockSpec((seqs, modes, lanes), lambda g, at: (0, 0, g))
@@ -253,11 +261,11 @@
         cost_estimate=pl.CostEstimate(
             flops=3 * seqs * span * modes * block, bytes_accessed=2**21, transcendentals=0
         ),
+        compiler_params=pltpu.CompilerParams(vmem_limit_bytes=16 * 2**20),
         name="mix_states",
     )(where, near, far, fresh, decay, residue)
     if not direct:
         mixed = mixed.reshape(seqs, team, own, block).transpose(1, 0, 2, 3)
-    halves = [[h * team + p for p in range(team)] for h in range(2)]
     result = lax.all_to_all(mixed, "ctx", 0, 0, tiled=True, axis_index_groups=halves)
     result = result.reshape(chips, 2, seqs, own, block).transpose(2, 3, 1, 0, 4)
     return result.reshape(seqs, own, width)

time: 78 us -> 62.6 us (0.80)
  the two profiles are of different devices: /device:TPU:0 before, /device:TPU:16 now
where the time goes in v2:
time: 62.6 us; the launch traced here: 62.2 us
  blocking collectives  16.5 us (26%)
  Pallas kernels  16.3 us (26%)
  starting transfers between devices  14 us (22%)
  waiting for transfers between devices  11.2 us (18%)
  local copies, waits for them, and re-layouts  3.89 us (6%)
    all_to_all x1, blocking collectives, body(): lax.all_to_all(mixed, 'ctx', 0, 0, tiled=True, axis_index_groups=halves)  16.5 us
    all_to_all x1, waiting for transfers between devices, body(): lax.all_to_all(partial, 'ctx', 0, 0, tiled=True, axis_index_groups=sides)  9.34 us
    pallas_call x1, Pallas kernels, body(): pl.pallas_call(lambda *refs: fresh_kernel(total_len, *refs), grid_spec=pl...  7.96 us
    ppermute x1, starting transfers between devices, body(): far = lax.ppermute(near, 'ctx', opposite)  5.2 us
    pallas_call x1, Pallas kernels, body(): pl.pallas_call(lambda *refs: history_kernel(total_len, *refs), grid_spec=...  5.13 us
    all_to_all x1, starting transfers between devices, body(): lax.all_to_all(columns, 'ctx', 0, 0, tiled=True, axis_index_groups=halves)  4.86 us
    all_to_all x1, starting transfers between devices, body(): lax.all_to_all(partial, 'ctx', 0, 0, tiled=True, axis_index_groups=sides)  3.49 us
    pallas_call x1, Pallas kernels, body(): pl.pallas_call(lambda *refs: mix_kernel(total_len, *refs), grid_spec=pltp...  3.22 us
  transfers between devices with their start and end apart: 5, of which 2 were waited for; matrix products, arithmetic and copies ran while one was open for 3% of the time, Pallas kernels for 21%

profile of v2, /device:TPU:16, one launch (start us, length us, event | category | flops | bytes accessed | tf_op | source)
XLA Modules:
  0.0 62.2 jit_solution(6820391925600949695)
XLA Ops:
  0.0 0.0 copy-start.2
  0.0 0.0 collective-permute-start
  0.0 1.1 %copy.10 = bf16[2,8,16,512]{3,2,1,0:T(8,128)(2,1)S(1)} copy(bf16[2,8,16,512]{3,1,2,0:T(8,128)(2,1)} %bitcast.21) | data formatting | bytes 524288
  1.1 0.0 copy-start
  1.1 0.9 %copy.8 = bf16[8,2,16,512]{3,2,1,0:T(8,128)(2,1)} copy(bf16[8,2,16,512]{3,0,1,2:T(8,128)(2,1)S(1)} %bitcast.20) | data formatting | bytes 524288 | tf_op jit(solution)/shard_map/transpose | solution.py:182
  2.0 4.9 %all-to-all-start.1 = ((bf16[16,16,512]{2,1,0:T(8,128)(2,1)}), bf16[16,16,512]{2,1,0:T(8,128)(2,1)S(1)}, u32[]{:S(2)}, u32[]{:S(2)}) async-start(bf16[16,16,512]{2,1,0:T(8,128)(2,1)} %bitcast.4), calls=%async_computation.1 | async-start | bytes 524288 | tf_op jit(solution)/shard_map/all_to_all | solution.py:183
  6.9 0.0 copy-start.5
  6.9 0.1 pad_add_fusion.refs_0_
  7.0 0.0 collective-permute-done.refs_3_
  7.0 0.0 copy-done.2
  7.0 0.0 copy-done
  7.0 0.6 copy-done.5
  7.6 5.1 %history_states.1 = f32[8,2,16,512]{3,2,1,0:T(8,128)} custom-call(s32[3]{0:T(128)S(1)} %pad_add_fusion.refs_0_, s32[2]{0:T(128)S(1)} %copy-done.5, bf16[2,32,8192]{2,1,0:T(8,128)(2,1)S(1)} %copy-done.2, bf16[2,32,8192]{2,1,0:T(8,128)(2,1)S(1)} %collective-permute-done.refs_3_, f32[16,8192]{1,0:T(8,128)S(1)} %copy-done), custom_call_target="tpu_custom_call" | custom-call | flops 16777216 | bytes 3145728 | tf_op jit(solution)/shard_map/history_states/pallas_call | solution.py:188
  12.7 1.9 %all-to-all-done.1 = bf16[16,16,512]{2,1,0:T(8,128)(2,1)S(1)} async-done(((bf16[16,16,512]{2,1,0:T(8,128)(2,1)}), bf16[16,16,512]{2,1,0:T(8,128)(2,1)S(1)}, u32[]{:S(2)}, u32[]{:S(2)}) %all-to-all-start.1) | async-done | bytes 262176 | tf_op jit(solution)/shard_map/all_to_all | solution.py:183
  14.6 3.5 %all-to-all-start = ((f32[8,2,16,512]{3,2,1,0:T(8,128)}), f32[8,2,16,512]{3,2,1,0:T(8,128)S(1)}, u32[]{:S(2)}, u32[]{:S(2)}) async-start(f32[8,2,16,512]{3,2,1,0:T(8,128)} %history_states.1), calls=%async_computation | async-start | bytes 1048576 | tf_op jit(solution)/shard_map/all_to_all | solution.py:209
  18.1 0.0 copy-start.1
  18.1 0.0 copy-start.3
  18.1 0.4 collective-permute-start.2
  18.5 9.3 %all-to-all-done = f32[8,2,16,512]{3,2,1,0:T(8,128)S(1)} async-done(((f32[8,2,16,512]{3,2,1,0:T(8,128)}), f32[8,2,16,512]{3,2,1,0:T(8,128)S(1)}, u32[]{:S(2)}, u32[]{:S(2)}) %all-to-all-start) | async-done | bytes 524320 | tf_op jit(solution)/shard_map/all_to_all | solution.py:209
  27.8 0.0 copy-start.4
  27.9 5.2 %collective-permute-start.1 = (f32[2,16,512]{2,1,0:T(8,128)S(1)}, f32[2,16,512]{2,1,0:T(8,128)S(1)}, u32[]{:S(2)}, u32[]{:S(2)}) collective-permute-start(f32[2,16,512]{2,1,0:T(8,128)S(1)} %reduce_sum.9.refs_1_), channel_id=1, source_target_pairs={{0,16},{1,17},{2,18},{3,19},{4,20},{5,21},{6,22},{7,23},{8,24},{9,... | collective-permute-start | bytes 196616 | tf_op jit(solution)/shard_map/ppermute | solution.py:211
  33.1 0.0 collective-permute-done.2.refs_3_
  33.1 0.0 copy-done.1
  33.1 0.0 copy-done.3
  33.1 0.0 copy-done.4
  33.1 8.0 %fresh_scan.1.refs_3_ = f32[2,256,512]{2,1,0:T(8,128)S(1)} custom-call(s32[3]{0:T(128)S(1)} %pad_add_fusion.refs_0_, s32[2,512]{1,0:T(2,128)S(1)} %copy-done.4, bf16[256,512]{1,0:T(8,128)(2,1)S(1)} %bitcast.17, bf16[256,512]{1,0:T(8,128)(2,1)S(1)} %collective-permute-done.2.refs_3_, f32[16,8192]{1,0:T(8,128)S(1)} %copy-done, f32[16,8192]{1,0:T(8,128)S(1)} %copy-done.1, ...), custom_call_target="tpu_custom_call" | custom-call | flops 25165824 | bytes 2097152 | tf_op jit(solution)/shard_map/fresh_scan/pallas_call | solution.py:214
  41.1 0.0 collective-permute-done.1.refs_2_
  41.1 3.2 %mix_states.1 = bf16[16,2,16,512]{3,2,1,0:T(8,128)(2,1)S(1)} custom-call(s32[3]{0:T(128)S(1)} %pad_add_fusion.refs_0_, f32[2,16,512]{2,1,0:T(8,128)S(1)} %reduce_sum.9.refs_1_, f32[2,16,512]{2,1,0:T(8,128)S(1)} %collective-permute-done.1.refs_2_, f32[2,256,512]{2,1,0:T(8,128)S(1)} %fresh_scan.1.refs_3_, f32[16,8192]{1,0:T(8,128)S(1)} %copy-done, ...), custom_call_target="tpu_custom_call" | custom-call | flops 12582912 | bytes 2097152 | tf_op jit(solution)/shard_map/mix_states/pallas_call | solution.py:246
  44.3 16.5 %all_to_all.15 = bf16[16,2,16,512]{3,2,1,0:T(8,128)(2,1)S(1)} all-to-all(bf16[16,2,16,512]{3,2,1,0:T(8,128)(2,1)S(1)} %mix_states.1), channel_id=1, replica_groups={{0,1,2,3,4,5,6,7,8,9,10,11,12,13,14,15},{16,17,18,19,20,21,22,23,24,25,..., dimensions={0} | all-to-all | bytes 1048576 | tf_op jit(solution)/shard_map/all_to_all | solution.py:269
  60.9 0.3 copy.9
  61.1 1.0 %reshape.23 = bf16[2,16,8192]{2,1,0:T(8,128)(2,1)} reshape(bf16[2,16,2,8,512]{4,3,2,1,0:T(8,128)(2,1)S(1)} %copy.9) | data formatting | bytes 1048576 | tf_op jit(solution)/shard_map/reshape | solution.py:271
  (1 shorter events, 0.0 us)
Async XLA Ops:
  0.0 7.0 %copy-start.2 = (bf16[2,32,8192]{2,1,0:T(8,128)(2,1)S(1)}, bf16[2,32,8192]{2,1,0:T(8,128)(2,1)}, u32[]{:S(2)}) copy-start(bf16[2,32,8192]{2,1,0:T(8,128)(2,1)} %refs_2_.1) | copy-start | bytes 3145732
  0.0 7.0 %collective-permute-start = (bf16[2,32,8192]{2,1,0:T(8,128)(2,1)}, bf16[2,32,8192]{2,1,0:T(8,128)(2,1)S(1)}, u32[]{:S(2)}, u32[]{:S(2)}) collective-permute-start(bf16[2,32,8192]{2,1,0:T(8,128)(2,1)} %refs_2_.1), channel_id=1, source_target_pairs={{0,1},{1,0},{2,3},{3,2},{4,5},{5,4},{6,7},{7,6},{8,9},{9,8},{10,11... | collective-permute-start | bytes 3145736 | tf_op jit(solution)/shard_map/ppermute | solution.py:177
  1.1 5.9 %copy-start = (f32[16,8192]{1,0:T(8,128)S(1)}, f32[16,8192]{1,0:T(8,128)}, u32[]{:S(2)}) copy-start(f32[16,8192]{1,0:T(8,128)} %refs_4_.5) | copy-start | bytes 1572868
  2.0 12.6 %all-to-all-start.1 = ((bf16[16,16,512]{2,1,0:T(8,128)(2,1)}), bf16[16,16,512]{2,1,0:T(8,128)(2,1)S(1)}, u32[]{:S(2)}, u32[]{:S(2)}) async-start(bf16[16,16,512]{2,1,0:T(8,128)(2,1)} %bitcast.4), calls=%async_computation.1 | async-start | bytes 524288 | tf_op jit(solution)/shard_map/all_to_all | solution.py:183
  6.9 0.7 %copy-start.5 = (s32[2]{0:T(128)S(1)}, s32[2]{0:T(128)}, u32[]{:S(2)}) copy-start(s32[2]{0:T(128)} %refs_1_.2) | copy-start | bytes 28
  14.6 13.3 %all-to-all-start = ((f32[8,2,16,512]{3,2,1,0:T(8,128)}), f32[8,2,16,512]{3,2,1,0:T(8,128)S(1)}, u32[]{:S(2)}, u32[]{:S(2)}) async-start(f32[8,2,16,512]{3,2,1,0:T(8,128)} %history_states.1), calls=%async_computation | async-start | bytes 1048576 | tf_op jit(solution)/shard_map/all_to_all | solution.py:209
  18.1 15.0 %copy-start.1 = (f32[16,8192]{1,0:T(8,128)S(1)}, f32[16,8192]{1,0:T(8,128)}, u32[]{:S(2)}) copy-start(f32[16,8192]{1,0:T(8,128)} %refs_5_.3) | copy-start | bytes 1572868
  18.1 15.0 %copy-start.3 = (f32[8192]{0:T(1024)S(1)}, f32[8192]{0:T(1024)}, u32[]{:S(2)}) copy-start(f32[8192]{0:T(1024)} %param.13) | copy-start | bytes 98308
  18.1 15.0 %collective-permute-start.2 = (bf16[256,512]{1,0:T(8,128)(2,1)S(1)}, bf16[256,512]{1,0:T(8,128)(2,1)S(1)}, u32[]{:S(2)}, u32[]{:S(2)}) collective-permute-start(bf16[256,512]{1,0:T(8,128)(2,1)S(1)} %bitcast.16), channel_id=1, source_target_pairs={{0,16},{1,17},{2,18},{3,19},{4,20},{5,21},{6,22},{7,23},{8,24},{9,... | collective-permute-start | bytes 786440 | tf_op jit(solution)/shard_map/ppermute | solution.py:185
  27.8 5.3 %copy-start.4 = (s32[2,512]{1,0:T(2,128)S(1)}, s32[2,512]{1,0:T(2,128)}, u32[]{:S(2)}) copy-start(s32[2,512]{1,0:T(2,128)} %refs_1_.3) | copy-start | bytes 12292
  27.9 13.2 %collective-permute-start.1 = (f32[2,16,512]{2,1,0:T(8,128)S(1)}, f32[2,16,512]{2,1,0:T(8,128)S(1)}, u32[]{:S(2)}, u32[]{:S(2)}) collective-permute-start(f32[2,16,512]{2,1,0:T(8,128)S(1)} %reduce_sum.9.refs_1_), channel_id=1, source_target_pairs={{0,16},{1,17},{2,18},{3,19},{4,20},{5,21},{6,22},{7,23},{8,24},{9,... | collective-permute-start | bytes 196616 | tf_op jit(solution)/shard_map/ppermute | solution.py:211

commit v3 on v1

v3 whole, which is shorter than its diff:
```python
import jax
import jax.numpy as jnp
from jax import lax
from jax.experimental import pallas as pl
from jax.experimental.pallas import tpu as pltpu
from jax.sharding import PartitionSpec as P

ROWS = 8
CHUNK = 16
VMEM = 16 * 2**20
f32 = jnp.float32


def lanes_of(block):
    return 256 if block % 256 == 0 else block


def lost(rate):
    series = jnp.ones_like(rate)
    for k in range(12, 1, -1):
        series = 1.0 - rate * series * (1.0 / k)
    return jnp.where(rate < 0.5, rate * series, 1.0 - jnp.exp(-rate))


def merge_rows(parts):
    row = lax.broadcasted_iota(jnp.int32, parts[0].shape, 0)
    low = row < 4
    level = [
        jnp.where(low, parts[i], parts[i + 4]) + pltpu.roll(jnp.where(low, parts[i + 4], parts[i]), 4, 0)
        for i in range(4)
    ]
    for gap in (2, 1):
        first = (row & gap) == 0
        level = [
            jnp.where(first, level[i], level[i + gap])
            + jnp.where(first, pltpu.roll(level[i], 8 - gap, 0), pltpu.roll(level[i + gap], gap, 0))
            for i in range(gap)
        ]
    return level[0]


def fold(x):
    total = x[:ROWS]
    for start in range(ROWS, x.shape[0], ROWS):
        total = total + x[start : start + ROWS]
    return total


def spread_kernel(total_len, me_ref, embed_ref, decay_ref, residue_ref, skip_ref, columns_ref, coef_ref, gain_ref):
    count, _, block = columns_ref.shape
    team = count // 2
    for p in range(team):
        piece = embed_ref[:, p * block : (p + 1) * block]
        columns_ref[p] = piece
        columns_ref[team + p] = piece
    rate = decay_ref[...] / total_len
    keep = jnp.exp(-rate)
    square = keep * keep
    fourth = square * square
    power = fourth * fourth * fourth * square * keep
    coef_ref[0] = rate
    coef_ref[1] = keep
    coef_ref[2] = -float(CHUNK) * ((keep - 1.0) + lost(rate)) * power
    coef_ref[3] = residue_ref[...]
    gain_ref[...] = skip_ref[...]


def history_kernel(total_len, me_ref, lengths_ref, own_ref, other_ref, decay_ref, out_ref, wide):
    seqs, tile, block = own_ref.shape
    me = me_ref[0]
    partner = me + 1 - 2 * lax.rem(me, 2)
    row = lax.broadcasted_iota(jnp.int32, (tile, block), 0)
    for side, (ref, owner) in enumerate(((own_ref, me), (other_ref, partner))):
        for b in range(seqs):
            left = lengths_ref[b] - owner * tile
            wide[side, b] = jnp.where(row < left, ref[b].astype(f32), 0.0)
    lanes = lanes_of(block)
    for start in range(0, block, lanes):
        at = slice(start, start + lanes)
        rate = decay_ref[:, at] / total_len
        keep = jnp.exp(-rate)
        chains = [(side, b) for side in range(2) for b in range(seqs)]

        def step(s, sums):
            return tuple(
                keep * total + wide[side, b, pl.ds(s, 1), at] for (side, b), total in zip(chains, sums)
            )

        zero = jnp.zeros(rate.shape, f32)
        sums = lax.fori_loop(0, tile, step, (zero,) * len(chains), unroll=8)
        for b in range(seqs):
            total = zero
            for side, owner in enumerate((me, partner)):
                after = jnp.maximum(lengths_ref[b] - (owner + 1) * tile, -tile) + 1
                total = total + sums[side * seqs + b] * jnp.exp(-rate * after.astype(f32))
            out_ref[0, b, :, at] = total


def fresh_kernel(team, me_ref, tokens_ref, table_ref, coef_ref, skip_ref, out_ref, fresh):
    seqs, gen = tokens_ref.shape
    span = out_ref.shape[1]
    entry = lax.broadcasted_iota(jnp.int32, (table_ref.shape[0], gen), 0)
    for b in range(seqs):
        chosen = jnp.where(entry == tokens_ref[b : b + 1, :], 1.0, 0.0).astype(jnp.bfloat16)
        fresh[b] = lax.dot_general(
            chosen, table_ref[...], (((0,), (0,)), ((), ())), preferred_element_type=f32
        )
    keep, missed, residue = coef_ref[1], coef_ref[2], coef_ref[3]
    skip = skip_ref[...]
    skipped = lax.div(me_ref[0], team) * span

    def before(index, sums):
        ends = []
        for b, begun in enumerate(sums):
            total = begun
            for j in range(CHUNK):
                total = keep * total + fresh[b, pl.ds(index * CHUNK + j, 1), :]
            ends.append(total + missed * begun)
        return tuple(ends)

    def after(index, sums):
        first = pl.multiple_of(skipped + index * CHUNK, CHUNK)
        local = pl.multiple_of(index * CHUNK, CHUNK)
        ends = []
        for b, begun in enumerate(sums):
            total = begun
            for start in range(0, CHUNK, ROWS):
                parts = []
                for j in range(start, start + ROWS):
                    total = keep * total + fresh[b, pl.ds(first + j, 1), :]
                    parts.append(fold(residue * total))
                direct = skip * fresh[b, pl.ds(first + start, ROWS), :]
                out_ref[b, pl.ds(local + start, ROWS), :] = merge_rows(parts) + direct
            ends.append(total + missed * begun)
        return tuple(ends)

    zero = jnp.zeros(keep.shape, f32)
    sums = lax.fori_loop(0, lax.div(skipped, CHUNK), before, (zero,) * seqs)
    lax.fori_loop(0, span // CHUNK, after, sums)


def mix_kernel(team, me_ref, near_ref, far_ref, fresh_ref, coef_ref, out_ref):
    seqs, span, _ = fresh_ref.shape
    rate, keep, residue = coef_ref[0], coef_ref[1], coef_ref[3]
    states = [residue * (near_ref[b] + far_ref[b]) for b in range(seqs)]
    skipped = lax.div(me_ref[0], team) * span

    def step(index, _):
        first = pl.multiple_of(index * CHUNK, CHUNK)
        scale = jnp.exp(-rate * (skipped + first).astype(f32))
        for b in range(seqs):
            terms = states[b] * scale
            done = []
            for start in range(0, CHUNK, ROWS):
                parts = []
                for j in range(start, start + ROWS):
                    parts.append(fold(terms))
                    if j < CHUNK - 1:
                        terms = terms * keep
                done.append(merge_rows(parts))
            mixed = (jnp.concatenate(done, axis=0) + fresh_ref[b, pl.ds(first, CHUNK), :]).astype(jnp.bfloat16)
            if len(out_ref.shape) == 4:
                own = out_ref.shape[2]
                spot = pl.ds(pl.multiple_of(lax.rem(first, own), CHUNK), CHUNK)
                out_ref[lax.div(first, own), b, spot, :] = mixed
            else:
                out_ref[b, pl.ds(first, CHUNK), :] = mixed
        return 0

    lax.fori_loop(0, span // CHUNK, step, 0)


def join_kernel(mixed_ref, out_ref):
    count, seqs, _, block = mixed_ref.shape
    for p in range(count):
        for b in range(seqs):
            out_ref[b, :, p * block : (p + 1) * block] = mixed_ref[p, b]


def call(kernel, grid, scalars, in_specs, out_specs, out_shape, flops, moved, scratch=()):
    return pl.pallas_call(
        kernel,
        grid_spec=pltpu.PrefetchScalarGridSpec(
            num_scalar_prefetch=scalars,
            grid=grid,
            in_specs=in_specs,
            out_specs=out_specs,
            scratch_shapes=scratch,
        ),
        out_shape=out_shape,
        cost_estimate=pl.CostEstimate(flops=flops, bytes_accessed=moved, transcendentals=0),
        compiler_params=pltpu.CompilerParams(vmem_limit_bytes=VMEM),
    )


def reverse_bits(value, bits):
    result = 0
    for k in range(bits):
        result = result + lax.rem(lax.div(value, 2**k), 2) * 2 ** (bits - 1 - k)
    return result


def body(history, lengths, token_ids, embed, residue, decay, skip):
    devices = lax.axis_size("ctx")
    me = lax.axis_index("ctx")
    seqs, tile, width = history.shape
    modes = decay.shape[0]
    rows = embed.shape[0]
    gen = token_ids.shape[1]
    total_len = float(tile * devices)
    team = devices // 2
    chips = team // 2
    bits = chips.bit_length() - 1
    assert devices == 4 * 2**bits
    block = width // team
    lanes = lanes_of(block)
    pieces = block // lanes
    span = gen // 2
    own = gen // devices
    place = me.astype(jnp.int32).reshape(1)
    chip = lax.rem(me, team) // 2
    opposite = [(j, (j + team) % devices) for j in range(devices)]
    shape = jax.ShapeDtypeStruct

    def paired(x, distance):
        return lax.ppermute(x, "ctx", [(j, j ^ distance) for j in range(devices)])

    swapped = paired(history, 1)

    strip = lambda g, at: (0, lax.rem(at[0], team))
    columns, coef, gain = call(
        lambda *refs: spread_kernel(total_len, *refs),
        (1,),
        1,
        [
            pl.BlockSpec((rows, width), lambda g, at: (0, 0)),
            pl.BlockSpec((modes, block), strip),
            pl.BlockSpec((modes, block), strip),
            pl.BlockSpec((1, block), strip),
        ],
        [
            pl.BlockSpec((devices, rows, block), lambda g, at: (0, 0, 0)),
            pl.BlockSpec((4, modes, block), lambda g, at: (0, 0, 0)),
            pl.BlockSpec((1, block), lambda g, at: (0, 0)),
        ],
        [
            shape((devices, rows, block), jnp.bfloat16),
            shape((4, modes, block), f32),
            shape((1, block), f32),
        ],
        10**5,
        2**20,
    )(place, embed, decay, residue, skip.reshape(1, width))
    table = lax.all_to_all(columns, "ctx", 0, 0, tiled=True)
    table = table.reshape(devices * rows, block)

    def states_for(flip):
        def part(g, at, ln):
            low = lax.rem(at[0], 4)
            if flip:
                low = lax.rem(low + 2, 4)
            return 0, 0, 4 * g + low

        return call(
            lambda *refs: history_kernel(total_len, *refs),
            (chips // 2,),
            2,
            [
                pl.BlockSpec((seqs, tile, block), part),
                pl.BlockSpec((seqs, tile, block), part),
                pl.BlockSpec((modes, block), lambda g, at, ln: part(g, at, ln)[1:]),
            ],
            pl.BlockSpec((1, seqs, modes, block), lambda g, at, ln: (reverse_bits(g, bits - 1), 0, 0, 0)),
            shape((chips // 2, seqs, modes, block), f32),
            2 * seqs * tile * modes * block * chips,
            2**20,
            [pltpu.VMEM((2, seqs, tile, block), f32)],
        )(place, lengths, history, swapped, decay)

    sent = states_for(True)
    came = paired(sent, 2)
    states = states_for(False) + came
    for k in range(1, bits):
        bit = lax.rem(lax.div(chip, 2**k), 2)
        size = states.shape[0] // 2
        sent = lax.dynamic_slice_in_dim(states, (1 - bit) * size, size, 0)
        came = paired(sent, 2 << k)
        states = lax.dynamic_slice_in_dim(states, bit * size, size, 0) + came
    near = states[0]
    far = lax.ppermute(near, "ctx", opposite)

    piece2 = lambda g, at: (0, g)
    piece3 = lambda g, at: (0, 0, g)
    fresh = call(
        lambda *refs: fresh_kernel(team, *refs),
        (pieces,),
        1,
        [
            pl.BlockSpec((seqs, gen), lambda g, at: (0, 0)),
            pl.BlockSpec((devices * rows, lanes), piece2),
            pl.BlockSpec((4, modes, lanes), piece3),
            pl.BlockSpec((1, lanes), piece2),
        ],
        pl.BlockSpec((seqs, span, lanes), piece3),
        shape((seqs, span, block), f32),
        6 * seqs * span * modes * block,
        2**21,
        [pltpu.VMEM((seqs, gen, lanes), f32)],
    )(place, token_ids, table, coef, gain)

    direct = own % CHUNK == 0
    if direct:
        mixed_shape = (team, seqs, own, block)
        mixed_spec = pl.BlockSpec((team, seqs, own, lanes), lambda g, at: (0, 0, 0, g))
    else:
        mixed_shape = (seqs, span, block)
        mixed_spec = pl.BlockSpec((seqs, span, lanes), piece3)
    mixed = call(
        lambda *refs: mix_kernel(team, *refs),
        (pieces,),
        1,
        [
            pl.BlockSpec((seqs, modes, lanes), piece3),
            pl.BlockSpec((seqs, modes, lanes), piece3),
            pl.BlockSpec((seqs, span, lanes), piece3),
            pl.BlockSpec((4, modes, lanes), piece3),
        ],
        mixed_spec,
        shape(mixed_shape, jnp.bfloat16),
        3 * seqs * span * modes * block,
        2**21,
    )(place, near, far, fresh, coef)
    if not direct:
        mixed = mixed.reshape(seqs, team, own, block).transpose(1, 0, 2, 3)
    halves = [[h * team + p for p in range(team)] for h in range(2)]
    result = lax.all_to_all(mixed, "ctx", 0, 0, tiled=True, axis_index_groups=halves)
    parts = 4
    return call(
        join_kernel,
        (parts,),
        0,
        [pl.BlockSpec((team // parts, seqs, own, block), lambda g: (g, 0, 0, 0))],
        pl.BlockSpec((seqs, own, width // parts), lambda g: (0, 0, g)),
        shape((seqs, own, width), jnp.bfloat16),
        10**5,
        2**20,
    )(result)


def solution(mesh):
    placed = (P("group", "ctx", None), P("group"), P("group", None), P("ctx", None), P(), P(), P())
    return jax.shard_map(
        body, mesh=mesh, in_specs=placed, out_specs=P("group", "ctx", None), check_vma=False
    )
```

time: 78 us -> 57.6 us (0.74)
  waiting for transfers between devices: 24.4 us -> 11.2 us
  Pallas kernels: 19.9 us -> 13.5 us
  starting transfers between devices: 13.2 us -> 14.1 us
  local copies, waits for them, and re-layouts: 3.95 us -> 3.11 us
    all_to_all x2 -> x1, waiting for transfers between devices: 22.5 us -> 0.01 us  [body(): table = lax.all_to_all(columns, 'ctx', 0, 0, tiled=True)]
    ppermute x2 -> x5, waiting for transfers between devices: 1.9 us -> 11.2 us  [the longest x4 11.2 us: paired(): return lax.ppermute(x, 'ctx', [(j, j ^ distance) for j in range(devices)])]
    pallas_call x3 -> x6, Pallas kernels: 19.9 us -> 13.5 us  [the longest x1 4.7 us: body(): call(lambda *refs: fresh_kernel(team, *refs), (pieces,), 1, [pl.BlockSpec...]
    ppermute x2 -> x5, starting transfers between devices: 3.23 us -> 9.17 us  [the longest x4 7.01 us: paired(): return lax.ppermute(x, 'ctx', [(j, j ^ distance) for j in range(devices)])]
    all_to_all x2 -> x1, starting transfers between devices: 9.94 us -> 4.92 us  [body(): table = lax.all_to_all(columns, 'ctx', 0, 0, tiled=True)]
    reshape x1 -> x0, local copies, waits for them, and re-layouts: 1.03 us -> none  [body(): return result.reshape(seqs, own, width)]
    add x0 -> x2, other arithmetic: none -> 1 us  [the longest x1 0.99 us: body(): states = states_for(False) + came]
    concatenate x1 -> x0, other arithmetic: 0.84 us -> none  [body(): jnp.concatenate([columns, columns])]
  transfers between devices with their start and end apart: 4 -> 6, of which waited for: 3 -> 3; matrix products, arithmetic and copies ran while one was open for 2% -> 2% of each run, Pallas kernels for 10% -> 12%
where the time goes in v3:
time: 57.6 us; the launch traced here: 57.3 us
  blocking collectives  14.2 us (25%)
  starting transfers between devices  14.1 us (24%)
  Pallas kernels  13.5 us (23%)
  waiting for transfers between devices  11.2 us (19%)
  local copies, waits for them, and re-layouts  3.11 us (5%)
  other arithmetic  1.01 us (2%)
    all_to_all x1, blocking collectives, body(): lax.all_to_all(mixed, 'ctx', 0, 0, tiled=True, axis_index_groups=halves)  14.2 us
    ppermute x4, waiting for transfers between devices, paired(): return lax.ppermute(x, 'ctx', [(j, j ^ distance) for j in range(devices)])  11.2 us
    ppermute x4, starting transfers between devices, paired(): return lax.ppermute(x, 'ctx', [(j, j ^ distance) for j in range(devices)])  7.01 us
    all_to_all x1, starting transfers between devices, body(): table = lax.all_to_all(columns, 'ctx', 0, 0, tiled=True)  4.92 us
    pallas_call x1, Pallas kernels, body(): call(lambda *refs: fresh_kernel(team, *refs), (pieces,), 1, [pl.BlockSpec...  4.7 us
    pallas_call x2, Pallas kernels, states_for(): call(lambda *refs: history_kernel(total_len, *refs), (chips // 2,), 2, [p...  4.65 us
    unnamed x20, local copies, waits for them, and re-layouts  3.08 us
    pallas_call x1, Pallas kernels, body(): call(lambda *refs: mix_kernel(team, *refs), (pieces,), 1, [pl.BlockSpec((...  2.64 us
  transfers between devices with their start and end apart: 6, of which 3 were waited for; matrix products, arithmetic and copies ran while one was open for 2% of the time, Pallas kernels for 12%

profile of v3, /device:TPU:0, one launch (start us, length us, event | category | flops | bytes accessed | tf_op | source)
XLA Modules:
  0.0 57.3 jit_solution(2588554863869821930)
XLA Ops:
  0.0 0.5 collective-permute-start
  0.5 2.5 %collective-permute-done.refs_3_ = bf16[2,32,8192]{2,1,0:T(8,128)(2,1)S(1)} collective-permute-done((bf16[2,32,8192]{2,1,0:T(8,128)(2,1)}, bf16[2,32,8192]{2,1,0:T(8,128)(2,1)S(1)}, u32[]{:S(2)}, u32[]{:S(2)}) %collective-permute-start) | collective-permute-done | bytes 1048608 | tf_op jit(solution)/shard_map/ppermute | solution.py:226
  3.0 0.0 copy-done.9
  3.0 1.0 %copy-done = f32[16,8192]{1,0:T(8,128)S(1)} copy-done((f32[16,8192]{1,0:T(8,128)S(1)}, f32[16,8192]{1,0:T(8,128)}, u32[]{:S(2)}) %copy-start) | copy-done | bytes 524312
  4.0 1.2 %copy-done.2 = bf16[2,32,8192]{2,1,0:T(8,128)(2,1)S(1)} copy-done((bf16[2,32,8192]{2,1,0:T(8,128)(2,1)S(1)}, bf16[2,32,8192]{2,1,0:T(8,128)(2,1)}, u32[]{:S(2)}) %copy-start.2) | copy-done | bytes 1048600
  5.3 2.4 %shard_map.74 = f32[4,2,16,512]{3,2,1,0:T(8,128)S(1)} custom-call(s32[1]{0:T(128)} %bitcast.refs_0_, s32[2]{0:T(128)S(1)} %copy-done.9, bf16[2,32,8192]{2,1,0:T(8,128)(2,1)S(1)} %copy-done.2, bf16[2,32,8192]{2,1,0:T(8,128)(2,1)S(1)} %collective-permute-done.refs_3_, f32[16,8192]{1,0:T(8,128)S(1)} %copy-done), custom_call_target="tpu_custom_call" | custom-call | flops 8388608 | bytes 1048576 | tf_op jit(solution)/shard_map/pallas_call | solution.py:264
  7.6 2.9 %collective-permute-start.1 = (f32[4,2,16,512]{3,2,1,0:T(8,128)S(1)}, f32[4,2,16,512]{3,2,1,0:T(8,128)}, u32[]{:S(2)}, u32[]{:S(2)}) collective-permute-start(f32[4,2,16,512]{3,2,1,0:T(8,128)S(1)} %shard_map.74), channel_id=1, source_target_pairs={{0,2},{1,3},{2,0},{3,1},{4,6},{5,7},{6,4},{7,5},{8,10},{9,11},{10,... | collective-permute-start | bytes 786440 | tf_op jit(solution)/shard_map/ppermute | solution.py:226
  10.5 0.0 copy-done.4
  10.6 0.0 copy-done.6
  10.6 0.0 copy-done.7
  10.6 0.1 shard_map.75
  10.7 0.0 copy-start.5
  10.7 0.8 %copy-done.5 = bf16[32,16,512]{2,1,0:T(8,128)(2,1)} copy-done((bf16[32,16,512]{2,1,0:T(8,128)(2,1)}, bf16[32,16,512]{2,1,0:T(8,128)(2,1)S(1)}, u32[]{:S(2)}) %copy-start.5) | copy-done | bytes 524312
  11.5 4.9 %all-to-all-start = ((bf16[32,16,512]{2,1,0:T(8,128)(2,1)}), bf16[32,16,512]{2,1,0:T(8,128)(2,1)S(1)}, u32[]{:S(2)}, u32[]{:S(2)}) async-start(bf16[32,16,512]{2,1,0:T(8,128)(2,1)} %copy-done.5), calls=%async_computation | async-start | bytes 1048576 | tf_op jit(solution)/shard_map/all_to_all | solution.py:254
  16.4 0.0 copy-done.3
  16.4 0.0 copy-done.1
  16.5 2.3 %shard_map.73 = f32[4,2,16,512]{3,2,1,0:T(8,128)S(1)} custom-call(s32[1]{0:T(128)} %bitcast.refs_0_, s32[2]{0:T(128)S(1)} %copy-done.9, bf16[2,32,8192]{2,1,0:T(8,128)(2,1)S(1)} %copy-done.3, bf16[2,32,8192]{2,1,0:T(8,128)(2,1)S(1)} %collective-permute-done.refs_3_, f32[16,8192]{1,0:T(8,128)S(1)} %copy-done.1), custom_call_target="tpu_custom_call" | custom-call | flops 8388608 | bytes 1048576 | tf_op jit(solution)/shard_map/pallas_call | solution.py:264
  18.8 0.0 collective-permute-done.1
  18.8 1.0 %add.23 = f32[4,2,16,512]{3,2,1,0:T(8,128)S(1)} add(f32[4,2,16,512]{3,2,1,0:T(8,128)S(1)} %shard_map.73, f32[4,2,16,512]{3,2,1,0:T(8,128)} %collective-permute-done.1) | non-fusion elementwise | flops 65536 | bytes 786432 | tf_op jit(solution)/shard_map/add | solution.py:282
  19.8 1.8 %collective-permute-start.2 = (f32[2,2,16,512]{3,2,1,0:T(8,128)S(1)}, f32[2,2,16,512]{3,2,1,0:T(8,128)S(1)}, u32[]{:S(2)}, u32[]{:S(2)}) collective-permute-start(f32[2,2,16,512]{3,2,1,0:T(8,128)S(1)} %constant_dynamic-slice_fusion.1), channel_id=1, source_target_pairs={{0,4},{1,5},{2,6},{3,7},{4,0},{5,1},{6,2},{7,3},{8,12},{9,13},{10,... | collective-permute-start | bytes 393224 | tf_op jit(solution)/shard_map/ppermute | solution.py:226
  21.6 5.8 %collective-permute-done.2 = f32[2,2,16,512]{3,2,1,0:T(8,128)S(1)} collective-permute-done((f32[2,2,16,512]{3,2,1,0:T(8,128)S(1)}, f32[2,2,16,512]{3,2,1,0:T(8,128)S(1)}, u32[]{:S(2)}, u32[]{:S(2)}) %collective-permute-start.2) | collective-permute-done | bytes 131104 | tf_op jit(solution)/shard_map/ppermute | solution.py:226
  27.5 1.8 %collective-permute-start.3 = (f32[1,2,16,512]{3,2,1,0:T(8,128)S(1)}, f32[1,2,16,512]{3,2,1,0:T(8,128)S(1)}, u32[]{:S(2)}, u32[]{:S(2)}) collective-permute-start(f32[1,2,16,512]{3,2,1,0:T(8,128)S(1)} %constant_dynamic-slice_fusion), channel_id=1, source_target_pairs={{0,8},{1,9},{2,10},{3,11},{4,12},{5,13},{6,14},{7,15},{8,0},{9,1},... | collective-permute-start | bytes 196616 | tf_op jit(solution)/shard_map/ppermute | solution.py:226
  29.3 2.9 %collective-permute-done.3 = f32[1,2,16,512]{3,2,1,0:T(8,128)S(1)} collective-permute-done((f32[1,2,16,512]{3,2,1,0:T(8,128)S(1)}, f32[1,2,16,512]{3,2,1,0:T(8,128)S(1)}, u32[]{:S(2)}, u32[]{:S(2)}) %collective-permute-start.3) | collective-permute-done | bytes 65568 | tf_op jit(solution)/shard_map/ppermute | solution.py:226
  32.2 0.0 copy-start.8
  32.2 2.2 %collective-permute-start.4 = (f32[2,16,512]{2,1,0:T(8,128)S(1)}, f32[2,16,512]{2,1,0:T(8,128)S(1)}, u32[]{:S(2)}, u32[]{:S(2)}) collective-permute-start(f32[2,16,512]{2,1,0:T(8,128)S(1)} %add_bitcast_fusion.refs_1_), channel_id=1, source_target_pairs={{0,16},{1,17},{2,18},{3,19},{4,20},{5,21},{6,22},{7,23},{8,24},{9,... | collective-permute-start | bytes 196616 | tf_op jit(solution)/shard_map/ppermute | solution.py:290
  34.4 0.0 all-to-all-done
  34.4 0.0 copy-done.8
  34.4 4.7 %shard_map.76.refs_3_ = f32[2,256,512]{2,1,0:T(8,128)S(1)} custom-call(s32[1]{0:T(128)} %bitcast.refs_0_, s32[2,512]{1,0:T(2,128)S(1)} %copy-done.8, bf16[512,512]{1,0:T(8,128)(2,1)S(1)} %bitcast.5, f32[4,16,512]{2,1,0:T(8,128)S(1)} %get-tuple-element.9.refs_3_.refs_4_, f32[1,512]{1,0:T(1,128)S(1)} %get-tuple-element.10.refs_4_), custom_call_target="tpu_custom_call" | custom-call | flops 25165824 | bytes 2097152 | tf_op jit(solution)/shard_map/pallas_call | solution.py:294
  39.1 0.0 collective-permute-done.4.refs_2_
  39.1 2.6 %shard_map.77 = bf16[16,2,16,512]{3,2,1,0:T(8,128)(2,1)S(1)} custom-call(s32[1]{0:T(128)} %bitcast.refs_0_, f32[2,16,512]{2,1,0:T(8,128)S(1)} %add_bitcast_fusion.refs_1_, f32[2,16,512]{2,1,0:T(8,128)S(1)} %collective-permute-done.4.refs_2_, f32[2,256,512]{2,1,0:T(8,128)S(1)} %shard_map.76.refs_3_, f32[4,16,512]{2,1,0:T(8,128)S(1)} %get-tuple-element.9.refs_3_.refs_4_), custom_call_target="tpu_custom_call" | custom-call | flops 12582912 | bytes 2097152 | tf_op jit(solution)/shard_map/pallas_call | solution.py:318
  41.7 14.2 %all_to_all.10.mixed_ref = bf16[16,2,16,512]{3,2,1,0:T(8,128)(2,1)S(1)} all-to-all(bf16[16,2,16,512]{3,2,1,0:T(8,128)(2,1)S(1)} %shard_map.77), channel_id=1, replica_groups={{0,1,2,3,4,5,6,7,8,9,10,11,12,13,14,15},{16,17,18,19,20,21,22,23,24,25,..., dimensions={0} | all-to-all | bytes 1048576 | tf_op jit(solution)/shard_map/all_to_all | solution.py:336
  55.9 1.4 %shard_map.78 = bf16[2,16,8192]{2,1,0:T(8,128)(2,1)} custom-call(bf16[16,2,16,512]{3,2,1,0:T(8,128)(2,1)S(1)} %all_to_all.10.mixed_ref), custom_call_target="tpu_custom_call" | custom-call | flops 100000 | bytes 1048576 | tf_op jit(solution)/shard_map/pallas_call | solution.py:338
  (12 shorter events, 0.1 us)
Async XLA Ops:
  0.0 3.0 %collective-permute-start = (bf16[2,32,8192]{2,1,0:T(8,128)(2,1)}, bf16[2,32,8192]{2,1,0:T(8,128)(2,1)S(1)}, u32[]{:S(2)}, u32[]{:S(2)}) collective-permute-start(bf16[2,32,8192]{2,1,0:T(8,128)(2,1)} %refs_2_.4), channel_id=1, source_target_pairs={{0,1},{1,0},{2,3},{3,2},{4,5},{5,4},{6,7},{7,6},{8,9},{9,8},{10,11... | collective-permute-start | bytes 3145736 | tf_op jit(solution)/shard_map/ppermute | solution.py:226
  0.5 2.5 %copy-start.9 = (s32[2]{0:T(128)S(1)}, s32[2]{0:T(128)}, u32[]{:S(2)}) copy-start(s32[2]{0:T(128)} %refs_1_.5) | copy-start | bytes 28
  3.0 1.0 %copy-start = (f32[16,8192]{1,0:T(8,128)S(1)}, f32[16,8192]{1,0:T(8,128)}, u32[]{:S(2)}) copy-start(f32[16,8192]{1,0:T(8,128)} %refs_2_.5) | copy-start | bytes 1572868
  4.0 1.2 %copy-start.2 = (bf16[2,32,8192]{2,1,0:T(8,128)(2,1)S(1)}, bf16[2,32,8192]{2,1,0:T(8,128)(2,1)}, u32[]{:S(2)}) copy-start(bf16[2,32,8192]{2,1,0:T(8,128)(2,1)} %refs_2_.4) | copy-start | bytes 3145732
  5.3 5.3 %copy-start.4 = (f32[16,8192]{1,0:T(8,128)S(1)}, f32[16,8192]{1,0:T(8,128)}, u32[]{:S(2)}) copy-start(f32[16,8192]{1,0:T(8,128)} %refs_3_.1) | copy-start | bytes 1572868
  5.3 5.3 %copy-start.6 = (bf16[16,8192]{1,0:T(8,128)(2,1)S(1)}, bf16[16,8192]{1,0:T(8,128)(2,1)}, u32[]{:S(2)}) copy-start(bf16[16,8192]{1,0:T(8,128)(2,1)} %refs_1_.6) | copy-start | bytes 786436
  5.3 5.3 %copy-start.7 = (f32[8192]{0:T(1024)S(1)}, f32[8192]{0:T(1024)}, u32[]{:S(2)}) copy-start(f32[8192]{0:T(1024)} %param.13) | copy-start | bytes 98308
  7.6 11.1 %collective-permute-start.1 = (f32[4,2,16,512]{3,2,1,0:T(8,128)S(1)}, f32[4,2,16,512]{3,2,1,0:T(8,128)}, u32[]{:S(2)}, u32[]{:S(2)}) collective-permute-start(f32[4,2,16,512]{3,2,1,0:T(8,128)S(1)} %shard_map.74), channel_id=1, source_target_pairs={{0,2},{1,3},{2,0},{3,1},{4,6},{5,7},{6,4},{7,5},{8,10},{9,11},{10,... | collective-permute-start | bytes 786440 | tf_op jit(solution)/shard_map/ppermute | solution.py:226
  10.6 5.9 %copy-start.3 = (bf16[2,32,8192]{2,1,0:T(8,128)(2,1)S(1)}, bf16[2,32,8192]{2,1,0:T(8,128)(2,1)}, u32[]{:S(2)}) copy-start(bf16[2,32,8192]{2,1,0:T(8,128)(2,1)} %refs_2_.4) | copy-start | bytes 3145732
  10.7 0.8 %copy-start.5 = (bf16[32,16,512]{2,1,0:T(8,128)(2,1)}, bf16[32,16,512]{2,1,0:T(8,128)(2,1)S(1)}, u32[]{:S(2)}) copy-start(bf16[32,16,512]{2,1,0:T(8,128)(2,1)S(1)} %get-tuple-element.8) | copy-start | bytes 1572868
  11.5 5.0 %copy-start.1 = (f32[16,8192]{1,0:T(8,128)S(1)}, f32[16,8192]{1,0:T(8,128)}, u32[]{:S(2)}) copy-start(f32[16,8192]{1,0:T(8,128)} %refs_2_.5) | copy-start | bytes 1572868
  11.5 22.9 %all-to-all-start = ((bf16[32,16,512]{2,1,0:T(8,128)(2,1)}), bf16[32,16,512]{2,1,0:T(8,128)(2,1)S(1)}, u32[]{:S(2)}, u32[]{:S(2)}) async-start(bf16[32,16,512]{2,1,0:T(8,128)(2,1)} %copy-done.5), calls=%async_computation | async-start | bytes 1048576 | tf_op jit(solution)/shard_map/all_to_all | solution.py:254
  19.8 7.7 %collective-permute-start.2 = (f32[2,2,16,512]{3,2,1,0:T(8,128)S(1)}, f32[2,2,16,512]{3,2,1,0:T(8,128)S(1)}, u32[]{:S(2)}, u32[]{:S(2)}) collective-permute-start(f32[2,2,16,512]{3,2,1,0:T(8,128)S(1)} %constant_dynamic-slice_fusion.1), channel_id=1, source_target_pairs={{0,4},{1,5},{2,6},{3,7},{4,0},{5,1},{6,2},{7,3},{8,12},{9,13},{10,... | collective-permute-start | bytes 393224 | tf_op jit(solution)/shard_map/ppermute | solution.py:226
  27.5 4.7 %collective-permute-start.3 = (f32[1,2,16,512]{3,2,1,0:T(8,128)S(1)}, f32[1,2,16,512]{3,2,1,0:T(8,128)S(1)}, u32[]{:S(2)}, u32[]{:S(2)}) collective-permute-start(f32[1,2,16,512]{3,2,1,0:T(8,128)S(1)} %constant_dynamic-slice_fusion), channel_id=1, source_target_pairs={{0,8},{1,9},{2,10},{3,11},{4,12},{5,13},{6,14},{7,15},{8,0},{9,1},... | collective-permute-start | bytes 196616 | tf_op jit(solution)/shard_map/ppermute | solution.py:226
  32.2 2.2 %copy-start.8 = (s32[2,512]{1,0:T(2,128)S(1)}, s32[2,512]{1,0:T(2,128)}, u32[]{:S(2)}) copy-start(s32[2,512]{1,0:T(2,128)} %refs_1_.7) | copy-start | bytes 12292
  32.2 6.9 %collective-permute-start.4 = (f32[2,16,512]{2,1,0:T(8,128)S(1)}, f32[2,16,512]{2,1,0:T(8,128)S(1)}, u32[]{:S(2)}, u32[]{:S(2)}) collective-permute-start(f32[2,16,512]{2,1,0:T(8,128)S(1)} %add_bitcast_fusion.refs_1_), channel_id=1, source_target_pairs={{0,16},{1,17},{2,18},{3,19},{4,20},{5,21},{6,22},{7,23},{8,24},{9,... | collective-permute-start | bytes 196616 | tf_op jit(solution)/shard_map/ppermute | solution.py:290

commit v4 on v3

--- a/solution.py
+++ b/solution.py
@@ -218,6 +218,10 @@
     span = gen // 2
     own = gen // devices
     place = me.astype(jnp.int32).reshape(1)
+    history, embed, residue, decay, skip = (
+        pltpu.with_memory_space_constraint(x, pltpu.HBM)
+        for x in (history, embed, residue, decay, skip.reshape(1, width))
+    )
     chip = lax.rem(me, team) // 2
     opposite = [(j, (j + team) % devices) for j in range(devices)]
     shape = jax.ShapeDtypeStruct
@@ -225,7 +229,7 @@
     def paired(x, distance):
         return lax.ppermute(x, "ctx", [(j, j ^ distance) for j in range(devices)])
 
-    swapped = paired(history, 1)
+    swapped = pltpu.with_memory_space_constraint(paired(history, 1), pltpu.VMEM)
 
     strip = lambda g, at: (0, lax.rem(at[0], team))
     columns, coef, gain = call(
@@ -250,7 +254,7 @@
         ],
         10**5,
         2**20,
-    )(place, embed, decay, residue, skip.reshape(1, width))
+    )(place, embed, decay, residue, skip)
     table = lax.all_to_all(columns, "ctx", 0, 0, tiled=True)
     table = table.reshape(devices * rows, block)
 

time: 57.6 us -> 57.8 us (level)
  Pallas kernels: 13.5 us -> 17.5 us
  local copies, waits for them, and re-layouts: 3.11 us -> 0.04 us
  other arithmetic: 1.01 us -> 0.06 us
    unnamed x20 -> x4, local copies, waits for them, and re-layouts: 3.08 us -> 0.01 us
    pallas_call x2, Pallas kernels: 4.65 us -> 6.97 us  [states_for(): call(lambda *refs: history_kernel(total_len, *refs), (chips // 2,), 2, [p...]
    pallas_call x1, Pallas kernels: 0.11 us -> 1.81 us  [body(): call(lambda *refs: spread_kernel(total_len, *refs), (1,), 1, [pl.BlockSpe...]
    add x1, other arithmetic: 0.99 us -> 0.04 us  [body(): states = states_for(False) + came]
  transfers between devices with their start and end apart: 6 -> 6, of which waited for: 3 -> 3; matrix products, arithmetic and copies ran while one was open for 2% -> 0% of each run, Pallas kernels for 12% -> 17%
where the time goes in v4:
time: 57.8 us; the launch traced here: 57.3 us
  Pallas kernels  17.5 us (30%)
  blocking collectives  14.4 us (25%)
  starting transfers between devices  14.1 us (24%)
  waiting for transfers between devices  11 us (19%)
    all_to_all x1, blocking collectives, body(): lax.all_to_all(mixed, 'ctx', 0, 0, tiled=True, axis_index_groups=halves)  14.4 us
    ppermute x4, waiting for transfers between devices, paired(): return lax.ppermute(x, 'ctx', [(j, j ^ distance) for j in range(devices)])  11 us
    ppermute x4, starting transfers between devices, paired(): return lax.ppermute(x, 'ctx', [(j, j ^ distance) for j in range(devices)])  7 us
    pallas_call x2, Pallas kernels, states_for(): call(lambda *refs: history_kernel(total_len, *refs), (chips // 2,), 2, [p...  6.97 us
    all_to_all x1, starting transfers between devices, body(): table = lax.all_to_all(columns, 'ctx', 0, 0, tiled=True)  4.92 us
    pallas_call x1, Pallas kernels, body(): call(lambda *refs: fresh_kernel(team, *refs), (pieces,), 1, [pl.BlockSpec...  4.7 us
    pallas_call x1, Pallas kernels, body(): call(lambda *refs: mix_kernel(team, *refs), (pieces,), 1, [pl.BlockSpec((...  2.64 us
    ppermute x1, starting transfers between devices, body(): far = lax.ppermute(near, 'ctx', opposite)  2.19 us
  transfers between devices with their start and end apart: 6, of which 3 were waited for; matrix products, arithmetic and copies ran while one was open for 0% of the time, Pallas kernels for 17%

profile of v4, /device:TPU:0, one launch (start us, length us, event | category | flops | bytes accessed | tf_op | source)
XLA Modules:
  0.0 57.3 jit_solution(11198170882294036792)
XLA Ops:
  0.0 0.5 collective-permute-start
  0.5 0.0 copy-start.1
  0.5 2.5 %collective-permute-done.refs_3_ = bf16[2,32,8192]{2,1,0:T(8,128)(2,1)S(1)} collective-permute-done((bf16[2,32,8192]{2,1,0:T(8,128)(2,1)}, bf16[2,32,8192]{2,1,0:T(8,128)(2,1)S(1)}, u32[]{:S(2)}, u32[]{:S(2)}) %collective-permute-start) | collective-permute-done | bytes 1048608 | tf_op jit(solution)/shard_map/ppermute | solution.py:230
  3.0 0.0 copy-done.1
  3.0 3.5 %shard_map.74 = f32[4,2,16,512]{3,2,1,0:T(8,128)S(1)} custom-call(s32[1]{0:T(128)} %bitcast.refs_0_, s32[2]{0:T(128)S(1)} %copy-done.1, bf16[2,32,8192]{2,1,0:T(8,128)(2,1)} %refs_2_.4, bf16[2,32,8192]{2,1,0:T(8,128)(2,1)S(1)} %collective-permute-done.refs_3_, f32[16,8192]{1,0:T(8,128)} %refs_2_.5), custom_call_target="tpu_custom_call" | custom-call | flops 8388608 | bytes 1048576 | tf_op jit(solution)/shard_map/pallas_call | solution.py:268
  6.5 2.9 %collective-permute-start.1 = (f32[4,2,16,512]{3,2,1,0:T(8,128)S(1)}, f32[4,2,16,512]{3,2,1,0:T(8,128)S(1)}, u32[]{:S(2)}, u32[]{:S(2)}) collective-permute-start(f32[4,2,16,512]{3,2,1,0:T(8,128)S(1)} %shard_map.74), channel_id=1, source_target_pairs={{0,2},{1,3},{2,0},{3,1},{4,6},{5,7},{6,4},{7,5},{8,10},{9,11},{10,... | collective-permute-start | bytes 786440 | tf_op jit(solution)/shard_map/ppermute | solution.py:230
  9.4 1.8 %shard_map.75 = (bf16[32,16,512]{2,1,0:T(8,128)(2,1)}, f32[4,16,512]{2,1,0:T(8,128)S(1)}, f32[1,512]{1,0:T(1,128)S(1)}) custom-call(s32[1]{0:T(128)} %bitcast.refs_0_, bf16[16,8192]{1,0:T(8,128)(2,1)} %refs_1_.6, f32[16,8192]{1,0:T(8,128)} %refs_2_.5, f32[16,8192]{1,0:T(8,128)} %refs_3_.1, f32[1,8192]{1,0:T(1,128)} %bitcast.6), custom_call_target="tpu_custom_call" | custom-call | flops 100000 | bytes 1048576 | tf_op jit(solution)/shard_map/pallas_call | solution.py:235
  11.2 4.9 %all-to-all-start = ((bf16[32,16,512]{2,1,0:T(8,128)(2,1)}), bf16[32,16,512]{2,1,0:T(8,128)(2,1)S(1)}, u32[]{:S(2)}, u32[]{:S(2)}) async-start(bf16[32,16,512]{2,1,0:T(8,128)(2,1)} %get-tuple-element.8), calls=%async_computation | async-start | bytes 1048576 | tf_op jit(solution)/shard_map/all_to_all | solution.py:258
  16.2 3.5 %shard_map.73 = f32[4,2,16,512]{3,2,1,0:T(8,128)S(1)} custom-call(s32[1]{0:T(128)} %bitcast.refs_0_, s32[2]{0:T(128)S(1)} %copy-done.1, bf16[2,32,8192]{2,1,0:T(8,128)(2,1)} %refs_2_.4, bf16[2,32,8192]{2,1,0:T(8,128)(2,1)S(1)} %collective-permute-done.refs_3_, f32[16,8192]{1,0:T(8,128)} %refs_2_.5), custom_call_target="tpu_custom_call" | custom-call | flops 8388608 | bytes 1048576 | tf_op jit(solution)/shard_map/pallas_call | solution.py:268
  19.7 0.0 collective-permute-done.1
  19.8 1.8 %collective-permute-start.2 = (f32[2,2,16,512]{3,2,1,0:T(8,128)S(1)}, f32[2,2,16,512]{3,2,1,0:T(8,128)S(1)}, u32[]{:S(2)}, u32[]{:S(2)}) collective-permute-start(f32[2,2,16,512]{3,2,1,0:T(8,128)S(1)} %constant_dynamic-slice_fusion.1), channel_id=1, source_target_pairs={{0,4},{1,5},{2,6},{3,7},{4,0},{5,1},{6,2},{7,3},{8,12},{9,13},{10,... | collective-permute-start | bytes 393224 | tf_op jit(solution)/shard_map/ppermute | solution.py:230
  21.6 5.7 %collective-permute-done.2 = f32[2,2,16,512]{3,2,1,0:T(8,128)S(1)} collective-permute-done((f32[2,2,16,512]{3,2,1,0:T(8,128)S(1)}, f32[2,2,16,512]{3,2,1,0:T(8,128)S(1)}, u32[]{:S(2)}, u32[]{:S(2)}) %collective-permute-start.2) | collective-permute-done | bytes 131104 | tf_op jit(solution)/shard_map/ppermute | solution.py:230
  27.3 1.8 %collective-permute-start.3 = (f32[1,2,16,512]{3,2,1,0:T(8,128)S(1)}, f32[1,2,16,512]{3,2,1,0:T(8,128)S(1)}, u32[]{:S(2)}, u32[]{:S(2)}) collective-permute-start(f32[1,2,16,512]{3,2,1,0:T(8,128)S(1)} %constant_dynamic-slice_fusion), channel_id=1, source_target_pairs={{0,8},{1,9},{2,10},{3,11},{4,12},{5,13},{6,14},{7,15},{8,0},{9,1},... | collective-permute-start | bytes 196616 | tf_op jit(solution)/shard_map/ppermute | solution.py:230
  29.1 2.8 %collective-permute-done.3 = f32[1,2,16,512]{3,2,1,0:T(8,128)S(1)} collective-permute-done((f32[1,2,16,512]{3,2,1,0:T(8,128)S(1)}, f32[1,2,16,512]{3,2,1,0:T(8,128)S(1)}, u32[]{:S(2)}, u32[]{:S(2)}) %collective-permute-start.3) | collective-permute-done | bytes 65568 | tf_op jit(solution)/shard_map/ppermute | solution.py:230
  32.0 0.0 copy-start
  32.0 2.2 %collective-permute-start.4 = (f32[2,16,512]{2,1,0:T(8,128)S(1)}, f32[2,16,512]{2,1,0:T(8,128)S(1)}, u32[]{:S(2)}, u32[]{:S(2)}) collective-permute-start(f32[2,16,512]{2,1,0:T(8,128)S(1)} %add_bitcast_fusion.refs_1_), channel_id=1, source_target_pairs={{0,16},{1,17},{2,18},{3,19},{4,20},{5,21},{6,22},{7,23},{8,24},{9,... | collective-permute-start | bytes 196616 | tf_op jit(solution)/shard_map/ppermute | solution.py:294
  34.2 0.0 all-to-all-done
  34.2 0.0 copy-done
  34.2 4.7 %shard_map.76.refs_3_ = f32[2,256,512]{2,1,0:T(8,128)S(1)} custom-call(s32[1]{0:T(128)} %bitcast.refs_0_, s32[2,512]{1,0:T(2,128)S(1)} %copy-done, bf16[512,512]{1,0:T(8,128)(2,1)S(1)} %bitcast.5, f32[4,16,512]{2,1,0:T(8,128)S(1)} %get-tuple-element.9.refs_3_.refs_4_, f32[1,512]{1,0:T(1,128)S(1)} %get-tuple-element.10.refs_4_), custom_call_target="tpu_custom_call" | custom-call | flops 25165824 | bytes 2097152 | tf_op jit(solution)/shard_map/pallas_call | solution.py:298
  38.9 0.0 collective-permute-done.4.refs_2_
  38.9 2.6 %shard_map.77 = bf16[16,2,16,512]{3,2,1,0:T(8,128)(2,1)S(1)} custom-call(s32[1]{0:T(128)} %bitcast.refs_0_, f32[2,16,512]{2,1,0:T(8,128)S(1)} %add_bitcast_fusion.refs_1_, f32[2,16,512]{2,1,0:T(8,128)S(1)} %collective-permute-done.4.refs_2_, f32[2,256,512]{2,1,0:T(8,128)S(1)} %shard_map.76.refs_3_, f32[4,16,512]{2,1,0:T(8,128)S(1)} %get-tuple-element.9.refs_3_.refs_4_), custom_call_target="tpu_custom_call" | custom-call | flops 12582912 | bytes 2097152 | tf_op jit(solution)/shard_map/pallas_call | solution.py:322
  41.5 14.4 %all_to_all.10.mixed_ref = bf16[16,2,16,512]{3,2,1,0:T(8,128)(2,1)S(1)} all-to-all(bf16[16,2,16,512]{3,2,1,0:T(8,128)(2,1)S(1)} %shard_map.77), channel_id=1, replica_groups={{0,1,2,3,4,5,6,7,8,9,10,11,12,13,14,15},{16,17,18,19,20,21,22,23,24,25,..., dimensions={0} | all-to-all | bytes 1048576 | tf_op jit(solution)/shard_map/all_to_all | solution.py:340
  55.9 1.4 %shard_map.78 = bf16[2,16,8192]{2,1,0:T(8,128)(2,1)} custom-call(bf16[16,2,16,512]{3,2,1,0:T(8,128)(2,1)S(1)} %all_to_all.10.mixed_ref), custom_call_target="tpu_custom_call" | custom-call | flops 100000 | bytes 1048576 | tf_op jit(solution)/shard_map/pallas_call | solution.py:342
  (5 shorter events, 0.1 us)
Async XLA Ops:
  0.0 3.0 %collective-permute-start = (bf16[2,32,8192]{2,1,0:T(8,128)(2,1)}, bf16[2,32,8192]{2,1,0:T(8,128)(2,1)S(1)}, u32[]{:S(2)}, u32[]{:S(2)}) collective-permute-start(bf16[2,32,8192]{2,1,0:T(8,128)(2,1)} %refs_2_.4), channel_id=1, source_target_pairs={{0,1},{1,0},{2,3},{3,2},{4,5},{5,4},{6,7},{7,6},{8,9},{9,8},{10,11... | collective-permute-start | bytes 3145736 | tf_op jit(solution)/shard_map/ppermute | solution.py:230
  0.5 2.5 %copy-start.1 = (s32[2]{0:T(128)S(1)}, s32[2]{0:T(128)}, u32[]{:S(2)}) copy-start(s32[2]{0:T(128)} %refs_1_.5) | copy-start | bytes 28
  6.5 13.2 %collective-permute-start.1 = (f32[4,2,16,512]{3,2,1,0:T(8,128)S(1)}, f32[4,2,16,512]{3,2,1,0:T(8,128)S(1)}, u32[]{:S(2)}, u32[]{:S(2)}) collective-permute-start(f32[4,2,16,512]{3,2,1,0:T(8,128)S(1)} %shard_map.74), channel_id=1, source_target_pairs={{0,2},{1,3},{2,0},{3,1},{4,6},{5,7},{6,4},{7,5},{8,10},{9,11},{10,... | collective-permute-start | bytes 786440 | tf_op jit(solution)/shard_map/ppermute | solution.py:230
  11.2 22.9 %all-to-all-start = ((bf16[32,16,512]{2,1,0:T(8,128)(2,1)}), bf16[32,16,512]{2,1,0:T(8,128)(2,1)S(1)}, u32[]{:S(2)}, u32[]{:S(2)}) async-start(bf16[32,16,512]{2,1,0:T(8,128)(2,1)} %get-tuple-element.8), calls=%async_computation | async-start | bytes 1048576 | tf_op jit(solution)/shard_map/all_to_all | solution.py:258
  19.8 7.5 %collective-permute-start.2 = (f32[2,2,16,512]{3,2,1,0:T(8,128)S(1)}, f32[2,2,16,512]{3,2,1,0:T(8,128)S(1)}, u32[]{:S(2)}, u32[]{:S(2)}) collective-permute-start(f32[2,2,16,512]{3,2,1,0:T(8,128)S(1)} %constant_dynamic-slice_fusion.1), channel_id=1, source_target_pairs={{0,4},{1,5},{2,6},{3,7},{4,0},{5,1},{6,2},{7,3},{8,12},{9,13},{10,... | collective-permute-start | bytes 393224 | tf_op jit(solution)/shard_map/ppermute | solution.py:230
  27.3 4.6 %collective-permute-start.3 = (f32[1,2,16,512]{3,2,1,0:T(8,128)S(1)}, f32[1,2,16,512]{3,2,1,0:T(8,128)S(1)}, u32[]{:S(2)}, u32[]{:S(2)}) collective-permute-start(f32[1,2,16,512]{3,2,1,0:T(8,128)S(1)} %constant_dynamic-slice_fusion), channel_id=1, source_target_pairs={{0,8},{1,9},{2,10},{3,11},{4,12},{5,13},{6,14},{7,15},{8,0},{9,1},... | collective-permute-start | bytes 196616 | tf_op jit(solution)/shard_map/ppermute | solution.py:230
  32.0 2.2 %copy-start = (s32[2,512]{1,0:T(2,128)S(1)}, s32[2,512]{1,0:T(2,128)}, u32[]{:S(2)}) copy-start(s32[2,512]{1,0:T(2,128)} %refs_1_.7) | copy-start | bytes 12292
  32.0 6.9 %collective-permute-start.4 = (f32[2,16,512]{2,1,0:T(8,128)S(1)}, f32[2,16,512]{2,1,0:T(8,128)S(1)}, u32[]{:S(2)}, u32[]{:S(2)}) collective-permute-start(f32[2,16,512]{2,1,0:T(8,128)S(1)} %add_bitcast_fusion.refs_1_), channel_id=1, source_target_pairs={{0,16},{1,17},{2,18},{3,19},{4,20},{5,21},{6,22},{7,23},{8,24},{9,... | collective-permute-start | bytes 196616 | tf_op jit(solution)/shard_map/ppermute | solution.py:294

commit v5 on v4

--- a/solution.py
+++ b/solution.py
@@ -20,6 +20,13 @@
     for k in range(12, 1, -1):
         series = 1.0 - rate * series * (1.0 / k)
     return jnp.where(rate < 0.5, rate * series, 1.0 - jnp.exp(-rate))
+
+
+def reverse_bits(value, bits):
+    result = 0
+    for k in range(bits):
+        result = result + lax.rem(lax.div(value, 2**k), 2) * 2 ** (bits - 1 - k)
+    return result
 
 
 def merge_rows(parts):
@@ -46,13 +53,57 @@
     return total
 
 
-def spread_kernel(total_len, me_ref, embed_ref, decay_ref, residue_ref, skip_ref, columns_ref, coef_ref, gain_ref):
+def horner(keep, rows_of, count, tile):
+    def step(s, sums):
+        return tuple(keep * total + rows_of(i, s) for i, total in enumerate(sums))
+
+    return lax.fori_loop(0, tile, step, (jnp.zeros(keep.shape, f32),) * count, unroll=16)
+
+
+def low_bits(me, flip):
+    low = lax.rem(me, 4)
+    return lax.rem(low + 2, 4) if flip else low
+
+
+def masked(value, length, start):
+    row = lax.broadcasted_iota(jnp.int32, value.shape, 0)
+    return jnp.where(row < length - start, value.astype(f32), 0.0)
+
+
+def lift(rate, length, end, tile):
+    return jnp.exp(-rate * (jnp.maximum(length - end, -tile) + 1).astype(f32))
+
+
+def prepare_kernel(
+    total_len, bits, me_ref, lengths_ref, embed_ref, history_ref, all_decay_ref, decay_ref, residue_ref, skip_ref,
+    columns_ref, coef_ref, gain_ref, states_ref, rates_ref,
+    entries, pieces, wide, load_sem, piece_sem, rate_sem, store_sem,
+):
     count, _, block = columns_ref.shape
     team = count // 2
-    for p in range(team):
-        piece = embed_ref[:, p * block : (p + 1) * block]
-        columns_ref[p] = piece
-        columns_ref[team + p] = piece
+    chips = team // 2
+    seqs, tile, _ = history_ref.shape
+    me = me_ref[0]
+
+    def origin(spot):
+        low = lax.rem(lax.rem(me, 4) + lax.select(spot < chips // 2, 2, 0), 4)
+        return 4 * reverse_bits(lax.rem(spot, chips // 2), bits - 1) + low
+
+    def piece_copies(spot):
+        at = pl.ds(pl.multiple_of(origin(spot) * block, block), block)
+        return (
+            pltpu.make_async_copy(history_ref.at[:, :, at], pieces.at[spot], piece_sem.at[spot]),
+            pltpu.make_async_copy(all_decay_ref.at[:, at], rates_ref.at[spot], rate_sem.at[spot]),
+        )
+
+    load = pltpu.make_async_copy(embed_ref, entries, load_sem)
+    load.start()
+
+    @pl.loop(0, chips)
+    def _(spot):
+        for copy in piece_copies(spot):
+            copy.start()
+
     rate = decay_ref[...] / total_len
     keep = jnp.exp(-rate)
     square = keep * keep
@@ -64,47 +115,61 @@
     coef_ref[3] = residue_ref[...]
     gain_ref[...] = skip_ref[...]
 
-
-def history_kernel(total_len, me_ref, lengths_ref, own_ref, other_ref, decay_ref, out_ref, wide):
-    seqs, tile, block = own_ref.shape
+    def store(p):
+        at = pl.ds(pl.multiple_of(lax.rem(p, team) * block, block), block)
+        return pltpu.make_async_copy(entries.at[:, at], columns_ref.at[p], store_sem.at[p])
+
+    load.wait()
+
+    @pl.loop(0, count)
+    def _(p):
+        store(p).start()
+
+    @pl.loop(0, chips)
+    def _(spot):
+        for copy in piece_copies(spot):
+            copy.wait()
+        rate = rates_ref[spot] / total_len
+        rates_ref[spot] = rate
+        keep = jnp.exp(-rate)
+        for b in range(seqs):
+            wide[b] = masked(pieces[spot, b], lengths_ref[b], me * tile)
+        sums = horner(keep, lambda b, s: wide[b, pl.ds(s, 1), :], seqs, tile)
+        for b in range(seqs):
+            states_ref[spot, b] = sums[b] * lift(rate, lengths_ref[b], (me + 1) * tile, tile)
+
+    @pl.loop(0, count)
+    def _(p):
+        store(p).wait()
+
+
+def partner_kernel(flip, bits, me_ref, lengths_ref, other_ref, states_ref, rates_ref, out_ref, wide):
+    seqs, tile, _ = other_ref.shape
+    half, _, _, block = out_ref.shape
     me = me_ref[0]
     partner = me + 1 - 2 * lax.rem(me, 2)
-    row = lax.broadcasted_iota(jnp.int32, (tile, block), 0)
-    for side, (ref, owner) in enumerate(((own_ref, me), (other_ref, partner))):
-        for b in range(seqs):
-            left = lengths_ref[b] - owner * tile
-            wide[side, b] = jnp.where(row < left, ref[b].astype(f32), 0.0)
-    lanes = lanes_of(block)
-    for start in range(0, block, lanes):
-        at = slice(start, start + lanes)
-        rate = decay_ref[:, at] / total_len
+    base = 0 if flip else half
+
+    @pl.loop(0, half)
+    def _(spot):
+        start = (4 * reverse_bits(spot, bits - 1) + low_bits(me, flip)) * block
+        at = pl.ds(pl.multiple_of(start, block), block)
+        rate = rates_ref[base + spot]
         keep = jnp.exp(-rate)
-        chains = [(side, b) for side in range(2) for b in range(seqs)]
-
-        def step(s, sums):
-            return tuple(
-                keep * total + wide[side, b, pl.ds(s, 1), at] for (side, b), total in zip(chains, sums)
+        for b in range(seqs):
+            wide[b] = masked(other_ref[b, :, at], lengths_ref[b], partner * tile)
+        sums = horner(keep, lambda b, s: wide[b, pl.ds(s, 1), :], seqs, tile)
+        for b in range(seqs):
+            out_ref[spot, b] = states_ref[base + spot, b] + sums[b] * lift(
+                rate, lengths_ref[b], (partner + 1) * tile, tile
             )
 
-        zero = jnp.zeros(rate.shape, f32)
-        sums = lax.fori_loop(0, tile, step, (zero,) * len(chains), unroll=8)
-        for b in range(seqs):
-            total = zero
-            for side, owner in enumerate((me, partner)):
-                after = jnp.maximum(lengths_ref[b] - (owner + 1) * tile, -tile) + 1
-                total = total + sums[side * seqs + b] * jnp.exp(-rate * after.astype(f32))
-            out_ref[0, b, :, at] = total
-
-
-def fresh_kernel(team, me_ref, tokens_ref, table_ref, coef_ref, skip_ref, out_ref, fresh):
-    seqs, gen = tokens_ref.shape
+
+def fresh_kernel(team, me_ref, chosen_ref, table_ref, coef_ref, skip_ref, out_ref, fresh):
+    seqs = chosen_ref.shape[0]
     span = out_ref.shape[1]
-    entry = lax.broadcasted_iota(jnp.int32, (table_ref.shape[0], gen), 0)
     for b in range(seqs):
-        chosen = jnp.where(entry == tokens_ref[b : b + 1, :], 1.0, 0.0).astype(jnp.bfloat16)
-        fresh[b] = lax.dot_general(
-            chosen, table_ref[...], (((0,), (0,)), ((), ())), preferred_element_type=f32
-        )
+        fresh[b] = jnp.dot(chosen_ref[b], table_ref[...], preferred_element_type=f32)
     keep, missed, residue = coef_ref[1], coef_ref[2], coef_ref[3]
     skip = skip_ref[...]
     skipped = lax.div(me_ref[0], team) * span
@@ -191,13 +256,6 @@
         cost_estimate=pl.CostEstimate(flops=flops, bytes_accessed=moved, transcendentals=0),
         compiler_params=pltpu.CompilerParams(vmem_limit_bytes=VMEM),
     )
-
-
-def reverse_bits(value, bits):
-    result = 0
-    for k in range(bits):
-        result = result + lax.rem(lax.div(value, 2**k), 2) * 2 ** (bits - 1 - k)
-    return result
 
 
 def body(history, lengths, token_ids, embed, residue, decay, skip):
@@ -218,9 +276,9 @@
     span = gen // 2
     own = gen // devices
     place = me.astype(jnp.int32).reshape(1)
-    history, embed, residue, decay, skip = (
+    history, embed, residue, decay, skip, lengths = (
         pltpu.with_memory_space_constraint(x, pltpu.HBM)
-        for x in (history, embed, residue, decay, skip.reshape(1, width))
+        for x in (history, embed, residue, decay, skip.reshape(1, width), lengths)
     )
     chip = lax.rem(me, team) // 2
     opposite = [(j, (j + team) % devices) for j in range(devices)]
@@ -231,68 +289,77 @@
 
     swapped = pltpu.with_memory_space_constraint(paired(history, 1), pltpu.VMEM)
 
-    strip = lambda g, at: (0, lax.rem(at[0], team))
-    columns, coef, gain = call(
-        lambda *refs: spread_kernel(total_len, *refs),
+    strip = lambda g, at, ln: (0, lax.rem(at[0], team))
+    hbm = pl.BlockSpec(memory_space=pltpu.HBM)
+    vmem = pl.BlockSpec(memory_space=pltpu.VMEM)
+    columns, coef, gain, states, rates = call(
+        lambda *refs: prepare_kernel(total_len, bits, *refs),
         (1,),
-        1,
+        2,
         [
-            pl.BlockSpec((rows, width), lambda g, at: (0, 0)),
+            hbm,
+            hbm,
+            hbm,
             pl.BlockSpec((modes, block), strip),
             pl.BlockSpec((modes, block), strip),
             pl.BlockSpec((1, block), strip),
         ],
-        [
-            pl.BlockSpec((devices, rows, block), lambda g, at: (0, 0, 0)),
-            pl.BlockSpec((4, modes, block), lambda g, at: (0, 0, 0)),
-            pl.BlockSpec((1, block), lambda g, at: (0, 0)),
-        ],
+        [hbm, vmem, vmem, vmem, vmem],
         [
             shape((devices, rows, block), jnp.bfloat16),
             shape((4, modes, block), f32),
             shape((1, block), f32),
+            shape((chips, seqs, modes, block), f32),
+            shape((chips, modes, block), f32),
         ],
-        10**5,
+        2 * seqs * tile * modes * block * chips,
         2**20,
-    )(place, embed, decay, residue, skip)
+        [
+            pltpu.VMEM((rows, width), jnp.bfloat16),
+            pltpu.VMEM((chips, seqs, tile, block), jnp.bfloat16),
+            pltpu.VMEM((seqs, tile, block), f32),
+            pltpu.SemaphoreType.DMA(()),
+            pltpu.SemaphoreType.DMA((chips,)),
+            pltpu.SemaphoreType.DMA((chips,)),
+            pltpu.SemaphoreType.DMA((devices,)),
+        ],
+    )(place, lengths, embed, history, decay, decay, residue, skip)
     table = lax.all_to_all(columns, "ctx", 0, 0, tiled=True)
     table = table.reshape(devices * rows, block)
 
-    def states_for(flip):
-        def part(g, at, ln):
-            low = lax.rem(at[0], 4)
-            if flip:
-                low = lax.rem(low + 2, 4)
-            return 0, 0, 4 * g + low
-
+    def finish(flip):
         return call(
-            lambda *refs: history_kernel(total_len, *refs),
-            (chips // 2,),
+            lambda *refs: partner_kernel(flip, bits, *refs),
+            (1,),
             2,
-            [
-                pl.BlockSpec((seqs, tile, block), part),
-                pl.BlockSpec((seqs, tile, block), part),
-                pl.BlockSpec((modes, block), lambda g, at, ln: part(g, at, ln)[1:]),
-            ],
-            pl.BlockSpec((1, seqs, modes, block), lambda g, at, ln: (reverse_bits(g, bits - 1), 0, 0, 0)),
+            [vmem] * 3,
+            vmem,
             shape((chips // 2, seqs, modes, block), f32),
-            2 * seqs * tile * modes * block * chips,
+            seqs * tile * modes * block * chips,
             2**20,
-            [pltpu.VMEM((2, seqs, tile, block), f32)],
-        )(place, lengths, history, swapped, decay)
-
-    sent = states_for(True)
+            [pltpu.VMEM((seqs, tile, block), f32)],
+        )(place, lengths, swapped, states, rates)
+
+    sent = finish(True)
     came = paired(sent, 2)
-    states = states_for(False) + came
-    for k in range(1, bits):
-        bit = lax.rem(lax.div(chip, 2**k), 2)
-        size = states.shape[0] // 2
-        sent = lax.dynamic_slice_in_dim(states, (1 - bit) * size, size, 0)
-        came = paired(sent, 2 << k)
-        states = lax.dynamic_slice_in_dim(states, bit * size, size, 0) + came
-    near = states[0]
+    mine = finish(False) + came
+    done = 1
+    while done < bits:
+        now = min(2, bits - done)
+        ways, size = 2**now, mine.shape[0] // 2**now
+        digit = lax.rem(lax.div(chip, 2**done), ways)
+        take = lambda x, d: lax.dynamic_slice_in_dim(x, reverse_bits(d, now) * size, size, 0)
+        total = take(mine, digit)
+        for d in range(1, ways):
+            flipped = digit ^ d
+            total = total + paired(take(mine, flipped), d << (done + 1))
+        mine = total
+        done += now
+    near = mine[0]
     far = lax.ppermute(near, "ctx", opposite)
 
+    entry = lax.broadcasted_iota(jnp.int32, (seqs, gen, devices * rows), 2)
+    chosen = (token_ids[:, :, None] == entry).astype(jnp.bfloat16)
     piece2 = lambda g, at: (0, g)
     piece3 = lambda g, at: (0, 0, g)
     fresh = call(
@@ -300,7 +367,7 @@
         (pieces,),
         1,
         [
-            pl.BlockSpec((seqs, gen), lambda g, at: (0, 0)),
+            pl.BlockSpec((seqs, gen, devices * rows), lambda g, at: (0, 0, 0)),
             pl.BlockSpec((devices * rows, lanes), piece2),
             pl.BlockSpec((4, modes, lanes), piece3),
             pl.BlockSpec((1, lanes), piece2),
@@ -310,7 +377,7 @@
         6 * seqs * span * modes * block,
         2**21,
         [pltpu.VMEM((seqs, gen, lanes), f32)],
-    )(place, token_ids, table, coef, gain)
+    )(place, chosen, table, coef, gain)
 
     direct = own % CHUNK == 0
     if direct:

time: 57.8 us -> 58.4 us (1.010)
  starting transfers between devices: 14.1 us -> 16 us
  waiting for transfers between devices: 11 us -> 12.4 us
  Pallas kernels: 17.5 us -> 16.1 us
  blocking collectives: 14.4 us -> 13.2 us
    all_to_all x1, starting transfers between devices: 4.92 us -> 6.95 us  [body(): table = lax.all_to_all(columns, 'ctx', 0, 0, tiled=True)]
    ppermute x4 -> x5, waiting for transfers between devices: 11 us -> 12.3 us  [paired(): return lax.ppermute(x, 'ctx', [(j, j ^ distance) for j in range(devices)])]
    pallas_call x3, Pallas kernels: 8.78 us -> 7.5 us  [the longest x1 4.65 us: body(): call(lambda *refs: prepare_kernel(total_len, bits, *refs), (1,), 2, [hbm,...]
    all_to_all x1, blocking collectives: 14.4 us -> 13.2 us  [body(): lax.all_to_all(mixed, 'ctx', 0, 0, tiled=True, axis_index_groups=halves)]
    ppermute x4 -> x5, starting transfers between devices: 7 us -> 5.88 us  [paired(): return lax.ppermute(x, 'ctx', [(j, j ^ distance) for j in range(devices)])]
    ppermute x1, starting transfers between devices: 2.19 us -> 3.17 us  [body(): far = lax.ppermute(near, 'ctx', opposite)]
  transfers between devices with their start and end apart: 6 -> 7, of which waited for: 3 -> 4; matrix products, arithmetic and copies ran while one was open for 0% -> 1% of each run, Pallas kernels for 17% -> 21%
where the time goes in v5:
time: 58.4 us; the launch traced here: 58.1 us
  Pallas kernels  16.1 us (28%)
  starting transfers between devices  16 us (27%)
  blocking collectives  13.2 us (23%)
  waiting for transfers between devices  12.4 us (21%)
    all_to_all x1, blocking collectives, body(): lax.all_to_all(mixed, 'ctx', 0, 0, tiled=True, axis_index_groups=halves)  13.2 us
    ppermute x5, waiting for transfers between devices, paired(): return lax.ppermute(x, 'ctx', [(j, j ^ distance) for j in range(devices)])  12.3 us
    all_to_all x1, starting transfers between devices, body(): table = lax.all_to_all(columns, 'ctx', 0, 0, tiled=True)  6.95 us
    ppermute x5, starting transfers between devices, paired(): return lax.ppermute(x, 'ctx', [(j, j ^ distance) for j in range(devices)])  5.88 us
    pallas_call x1, Pallas kernels, body(): call(lambda *refs: prepare_kernel(total_len, bits, *refs), (1,), 2, [hbm,...  4.65 us
    pallas_call x1, Pallas kernels, body(): call(lambda *refs: fresh_kernel(team, *refs), (pieces,), 1, [pl.BlockSpec...  4.6 us
    ppermute x1, starting transfers between devices, body(): far = lax.ppermute(near, 'ctx', opposite)  3.17 us
    pallas_call x2, Pallas kernels, finish(): call(lambda *refs: partner_kernel(flip, bits, *refs), (1,), 2, [vmem] * 3...  2.85 us
  transfers between devices with their start and end apart: 7, of which 4 were waited for; matrix products, arithmetic and copies ran while one was open for 1% of the time, Pallas kernels for 21%

profile of v5, /device:TPU:0, one launch (start us, length us, event | category | flops | bytes accessed | tf_op | source)
XLA Modules:
  0.0 58.1 jit_solution(15943837098012149949)
XLA Ops:
  0.0 0.5 collective-permute-start
  0.5 4.7 %shard_map.73 = (bf16[32,16,512]{2,1,0:T(8,128)(2,1)}, f32[4,16,512]{2,1,0:T(8,128)S(1)}, f32[1,512]{1,0:T(1,128)S(1)}, f32[8,2,16,512]{3,2,1,0:T(8,128)S(1)}, f32[8,16,512]{2,1,0:T(8,128)S(1)}) custom-call(s32[1]{0:T(128)} %bitcast.refs_0_, s32[2]{0:T(128)} %refs_1_.5, bf16[16,8192]{1,0:T(8,128)(2,1)} %refs_2_.1, bf16[2,32,8192]{2,1,0:T(8,128)(2,1)} %refs_3_.1, ...), custom_call_target="tpu_custom_call" | custom-call | flops 8388608 | bytes 1048576 | tf_op jit(solution)/shard_map/pallas_call | solution.py:295
  5.2 7.0 %all-to-all-start = ((bf16[32,16,512]{2,1,0:T(8,128)(2,1)}), bf16[32,16,512]{2,1,0:T(8,128)(2,1)S(1)}, u32[]{:S(2)}, u32[]{:S(2)}) async-start(bf16[32,16,512]{2,1,0:T(8,128)(2,1)} %get-tuple-element.12), calls=%async_computation | async-start | bytes 1048576 | tf_op jit(solution)/shard_map/all_to_all | solution.py:327
  12.1 0.0 collective-permute-done.refs_2_
  12.1 1.4 %shard_map.75 = f32[4,2,16,512]{3,2,1,0:T(8,128)S(1)} custom-call(s32[1]{0:T(128)} %bitcast.refs_0_, s32[2]{0:T(128)} %refs_1_.5, bf16[2,32,8192]{2,1,0:T(8,128)(2,1)S(1)} %collective-permute-done.refs_2_, f32[8,2,16,512]{3,2,1,0:T(8,128)S(1)} %get-tuple-element.10.refs_3_, f32[8,16,512]{2,1,0:T(8,128)S(1)} %get-tuple-element.11.refs_4_), custom_call_target="tpu_custom_call" | custom-call | flops 4194304 | bytes 1048576 | tf_op jit(solution)/shard_map/pallas_call | solution.py:331
  13.6 1.8 %collective-permute-start.1 = (f32[4,2,16,512]{3,2,1,0:T(8,128)S(1)}, f32[4,2,16,512]{3,2,1,0:T(8,128)S(1)}, u32[]{:S(2)}, u32[]{:S(2)}) collective-permute-start(f32[4,2,16,512]{3,2,1,0:T(8,128)S(1)} %shard_map.75), channel_id=1, source_target_pairs={{0,2},{1,3},{2,0},{3,1},{4,6},{5,7},{6,4},{7,5},{8,10},{9,11},{10,... | collective-permute-start | bytes 786440 | tf_op jit(solution)/shard_map/ppermute | solution.py:288
  15.4 1.4 %shard_map.74 = f32[4,2,16,512]{3,2,1,0:T(8,128)S(1)} custom-call(s32[1]{0:T(128)} %bitcast.refs_0_, s32[2]{0:T(128)} %refs_1_.5, bf16[2,32,8192]{2,1,0:T(8,128)(2,1)S(1)} %collective-permute-done.refs_2_, f32[8,2,16,512]{3,2,1,0:T(8,128)S(1)} %get-tuple-element.10.refs_3_, f32[8,16,512]{2,1,0:T(8,128)S(1)} %get-tuple-element.11.refs_4_), custom_call_target="tpu_custom_call" | custom-call | flops 4194304 | bytes 1048576 | tf_op jit(solution)/shard_map/pallas_call | solution.py:331
  16.8 0.0 copy-start
  16.8 8.9 %collective-permute-done.1 = f32[4,2,16,512]{3,2,1,0:T(8,128)S(1)} collective-permute-done((f32[4,2,16,512]{3,2,1,0:T(8,128)S(1)}, f32[4,2,16,512]{3,2,1,0:T(8,128)S(1)}, u32[]{:S(2)}, u32[]{:S(2)}) %collective-permute-start.1) | collective-permute-done | bytes 262176 | tf_op jit(solution)/shard_map/ppermute | solution.py:288
  25.8 2.3 %collective-permute-start.4 = (f32[1,2,16,512]{3,2,1,0:T(8,128)S(1)}, f32[1,2,16,512]{3,2,1,0:T(8,128)S(1)}, u32[]{:S(2)}, u32[]{:S(2)}) collective-permute-start(f32[1,2,16,512]{3,2,1,0:T(8,128)S(1)} %get-tuple-element.16), channel_id=1, source_target_pairs={{0,12},{1,13},{2,14},{3,15},{4,8},{5,9},{6,10},{7,11},{8,4},{9,5},... | collective-permute-start | bytes 196616 | tf_op jit(solution)/shard_map/ppermute | solution.py:288
  28.2 0.4 collective-permute-start.3
  28.5 0.8 %collective-permute-start.2 = (f32[1,2,16,512]{3,2,1,0:T(8,128)S(1)}, f32[1,2,16,512]{3,2,1,0:T(8,128)S(1)}, u32[]{:S(2)}, u32[]{:S(2)}) collective-permute-start(f32[1,2,16,512]{3,2,1,0:T(8,128)S(1)} %get-tuple-element.15), channel_id=1, source_target_pairs={{0,4},{1,5},{2,6},{3,7},{4,0},{5,1},{6,2},{7,3},{8,12},{9,13},{10,... | collective-permute-start | bytes 196616 | tf_op jit(solution)/shard_map/ppermute | solution.py:288
  29.4 2.3 %collective-permute-done.4 = f32[1,2,16,512]{3,2,1,0:T(8,128)S(1)} collective-permute-done((f32[1,2,16,512]{3,2,1,0:T(8,128)S(1)}, f32[1,2,16,512]{3,2,1,0:T(8,128)S(1)}, u32[]{:S(2)}, u32[]{:S(2)}) %collective-permute-start.4) | collective-permute-done | bytes 65568 | tf_op jit(solution)/shard_map/ppermute | solution.py:288
  31.6 0.8 %collective-permute-done.3 = f32[1,2,16,512]{3,2,1,0:T(8,128)S(1)} collective-permute-done((f32[1,2,16,512]{3,2,1,0:T(8,128)S(1)}, f32[1,2,16,512]{3,2,1,0:T(8,128)S(1)}, u32[]{:S(2)}, u32[]{:S(2)}) %collective-permute-start.3) | collective-permute-done | bytes 65568 | tf_op jit(solution)/shard_map/ppermute | solution.py:288
  32.4 0.4 collective-permute-done.2
  32.8 3.2 %collective-permute-start.5 = (f32[2,16,512]{2,1,0:T(8,128)S(1)}, f32[2,16,512]{2,1,0:T(8,128)S(1)}, u32[]{:S(2)}, u32[]{:S(2)}) collective-permute-start(f32[2,16,512]{2,1,0:T(8,128)S(1)} %add_bitcast_fusion.refs_1_), channel_id=1, source_target_pairs={{0,16},{1,17},{2,18},{3,19},{4,20},{5,21},{6,22},{7,23},{8,24},{9,... | collective-permute-start | bytes 196616 | tf_op jit(solution)/shard_map/ppermute | solution.py:359
  36.0 0.0 copy-done
  36.0 0.2 fusion.refs_1_
  36.2 0.0 all-to-all-done
  36.3 4.6 %shard_map.76.refs_3_ = f32[2,256,512]{2,1,0:T(8,128)S(1)} custom-call(s32[1]{0:T(128)} %bitcast.refs_0_, bf16[2,512,512]{2,1,0:T(8,128)(2,1)S(1)} %fusion.refs_1_, bf16[512,512]{1,0:T(8,128)(2,1)S(1)} %bitcast.5, f32[4,16,512]{2,1,0:T(8,128)S(1)} %get-tuple-element.13.refs_3_.refs_4_, f32[1,512]{1,0:T(1,128)S(1)} %get-tuple-element.14.refs_4_), custom_call_target="tpu_custom_call" | custom-call | flops 25165824 | bytes 2097152 | tf_op jit(solution)/shard_map/pallas_call | solution.py:365
  40.9 0.0 collective-permute-done.5.refs_2_
  40.9 2.6 %shard_map.77 = bf16[16,2,16,512]{3,2,1,0:T(8,128)(2,1)S(1)} custom-call(s32[1]{0:T(128)} %bitcast.refs_0_, f32[2,16,512]{2,1,0:T(8,128)S(1)} %add_bitcast_fusion.refs_1_, f32[2,16,512]{2,1,0:T(8,128)S(1)} %collective-permute-done.5.refs_2_, f32[2,256,512]{2,1,0:T(8,128)S(1)} %shard_map.76.refs_3_, f32[4,16,512]{2,1,0:T(8,128)S(1)} %get-tuple-element.13.refs_3_.refs_4_), custom_call_target="tpu_custom_call" | custom-call | flops 12582912 | bytes 2097152 | tf_op jit(solution)/shard_map/pallas_call | solution.py:389
  43.5 13.2 %all_to_all.10.mixed_ref = bf16[16,2,16,512]{3,2,1,0:T(8,128)(2,1)S(1)} all-to-all(bf16[16,2,16,512]{3,2,1,0:T(8,128)(2,1)S(1)} %shard_map.77), channel_id=1, replica_groups={{0,1,2,3,4,5,6,7,8,9,10,11,12,13,14,15},{16,17,18,19,20,21,22,23,24,25,..., dimensions={0} | all-to-all | bytes 1048576 | tf_op jit(solution)/shard_map/all_to_all | solution.py:407
  56.7 1.4 %shard_map.78 = bf16[2,16,8192]{2,1,0:T(8,128)(2,1)} custom-call(bf16[16,2,16,512]{3,2,1,0:T(8,128)(2,1)S(1)} %all_to_all.10.mixed_ref), custom_call_target="tpu_custom_call" | custom-call | flops 100000 | bytes 1048576 | tf_op jit(solution)/shard_map/pallas_call | solution.py:409
  (3 shorter events, 0.1 us)
Async XLA Ops:
  0.0 12.1 %collective-permute-start = (bf16[2,32,8192]{2,1,0:T(8,128)(2,1)}, bf16[2,32,8192]{2,1,0:T(8,128)(2,1)S(1)}, u32[]{:S(2)}, u32[]{:S(2)}) collective-permute-start(bf16[2,32,8192]{2,1,0:T(8,128)(2,1)} %refs_3_.1), channel_id=1, source_target_pairs={{0,1},{1,0},{2,3},{3,2},{4,5},{5,4},{6,7},{7,6},{8,9},{9,8},{10,11... | collective-permute-start | bytes 3145736 | tf_op jit(solution)/shard_map/ppermute | solution.py:288
  5.2 31.1 %all-to-all-start = ((bf16[32,16,512]{2,1,0:T(8,128)(2,1)}), bf16[32,16,512]{2,1,0:T(8,128)(2,1)S(1)}, u32[]{:S(2)}, u32[]{:S(2)}) async-start(bf16[32,16,512]{2,1,0:T(8,128)(2,1)} %get-tuple-element.12), calls=%async_computation | async-start | bytes 1048576 | tf_op jit(solution)/shard_map/all_to_all | solution.py:327
  13.6 12.2 %collective-permute-start.1 = (f32[4,2,16,512]{3,2,1,0:T(8,128)S(1)}, f32[4,2,16,512]{3,2,1,0:T(8,128)S(1)}, u32[]{:S(2)}, u32[]{:S(2)}) collective-permute-start(f32[4,2,16,512]{3,2,1,0:T(8,128)S(1)} %shard_map.75), channel_id=1, source_target_pairs={{0,2},{1,3},{2,0},{3,1},{4,6},{5,7},{6,4},{7,5},{8,10},{9,11},{10,... | collective-permute-start | bytes 786440 | tf_op jit(solution)/shard_map/ppermute | solution.py:288
  16.8 19.2 %copy-start = (s32[2,512]{1,0:T(2,128)S(1)}, s32[2,512]{1,0:T(2,128)}, u32[]{:S(2)}) copy-start(s32[2,512]{1,0:T(2,128)} %param.9) | copy-start | bytes 12292
  25.8 5.8 %collective-permute-start.4 = (f32[1,2,16,512]{3,2,1,0:T(8,128)S(1)}, f32[1,2,16,512]{3,2,1,0:T(8,128)S(1)}, u32[]{:S(2)}, u32[]{:S(2)}) collective-permute-start(f32[1,2,16,512]{3,2,1,0:T(8,128)S(1)} %get-tuple-element.16), channel_id=1, source_target_pairs={{0,12},{1,13},{2,14},{3,15},{4,8},{5,9},{6,10},{7,11},{8,4},{9,5},... | collective-permute-start | bytes 196616 | tf_op jit(solution)/shard_map/ppermute | solution.py:288
  28.2 4.3 %collective-permute-start.3 = (f32[1,2,16,512]{3,2,1,0:T(8,128)S(1)}, f32[1,2,16,512]{3,2,1,0:T(8,128)S(1)}, u32[]{:S(2)}, u32[]{:S(2)}) collective-permute-start(f32[1,2,16,512]{3,2,1,0:T(8,128)S(1)} %get-tuple-element.17), channel_id=1, source_target_pairs={{0,8},{1,9},{2,10},{3,11},{4,12},{5,13},{6,14},{7,15},{8,0},{9,1},... | collective-permute-start | bytes 196616 | tf_op jit(solution)/shard_map/ppermute | solution.py:288
  28.5 4.3 %collective-permute-start.2 = (f32[1,2,16,512]{3,2,1,0:T(8,128)S(1)}, f32[1,2,16,512]{3,2,1,0:T(8,128)S(1)}, u32[]{:S(2)}, u32[]{:S(2)}) collective-permute-start(f32[1,2,16,512]{3,2,1,0:T(8,128)S(1)} %get-tuple-element.15), channel_id=1, source_target_pairs={{0,4},{1,5},{2,6},{3,7},{4,0},{5,1},{6,2},{7,3},{8,12},{9,13},{10,... | collective-permute-start | bytes 196616 | tf_op jit(solution)/shard_map/ppermute | solution.py:288
  32.8 8.0 %collective-permute-start.5 = (f32[2,16,512]{2,1,0:T(8,128)S(1)}, f32[2,16,512]{2,1,0:T(8,128)S(1)}, u32[]{:S(2)}, u32[]{:S(2)}) collective-permute-start(f32[2,16,512]{2,1,0:T(8,128)S(1)} %add_bitcast_fusion.refs_1_), channel_id=1, source_target_pairs={{0,16},{1,17},{2,18},{3,19},{4,20},{5,21},{6,22},{7,23},{8,24},{9,... | collective-permute-start | bytes 196616 | tf_op jit(solution)/shard_map/ppermute | solution.py:359

commit v6 on v5

v6 whole, which is shorter than its diff:
```python
import jax
import jax.numpy as jnp
from jax import lax
from jax.experimental import pallas as pl
from jax.experimental.pallas import tpu as pltpu
from jax.sharding import PartitionSpec as P

ROWS = 8
CHUNK = 16
LANES = 128
VMEM = 16 * 2**20
f32 = jnp.float32


def reverse_bits(value, bits):
    result = 0
    for k in range(bits):
        result = result + lax.rem(lax.div(value, 2**k), 2) * 2 ** (bits - 1 - k)
    return result


def reversed_int(value, bits):
    return sum((value >> k & 1) << (bits - 1 - k) for k in range(bits))


def merge_rows(parts):
    row = lax.broadcasted_iota(jnp.int32, parts[0].shape, 0)
    low = row < 4
    level = [
        jnp.where(low, parts[i], parts[i + 4]) + pltpu.roll(jnp.where(low, parts[i + 4], parts[i]), 4, 0)
        for i in range(4)
    ]
    for gap in (2, 1):
        first = (row & gap) == 0
        level = [
            jnp.where(first, level[i], level[i + gap])
            + jnp.where(first, pltpu.roll(level[i], 8 - gap, 0), pltpu.roll(level[i + gap], gap, 0))
            for i in range(gap)
        ]
    return level[0]


def fold(x):
    total = x[:ROWS]
    for start in range(ROWS, x.shape[0], ROWS):
        total = total + x[start : start + ROWS]
    return total


def horner(keep, rows_of, count, tile):
    def step(s, sums):
        return tuple(keep * total + rows_of(i, s) for i, total in enumerate(sums))

    return lax.fori_loop(0, tile, step, (jnp.zeros(keep.shape, f32),) * count, unroll=16)


def low_bits(me, flip):
    low = lax.rem(me, 4)
    return lax.rem(low + 2, 4) if flip else low


def masked(value, length, start):
    row = lax.broadcasted_iota(jnp.int32, value.shape, 0)
    return jnp.where(row < length - start, value.astype(f32), 0.0)


def lift(rate, length, end, tile):
    return jnp.exp(-rate * (jnp.maximum(length - end, -tile) + 1).astype(f32))


def prepare_kernel(
    total_len, bits, me_ref, lengths_ref, embed_ref, history_ref, decay_ref,
    columns_ref, states_ref, rates_ref,
    entries, pieces, wide, load_sem, piece_sem, rate_sem, store_sem,
):
    count, _, block = columns_ref.shape
    team = count // 2
    chips = team // 2
    seqs, tile, _ = history_ref.shape
    me = me_ref[0]

    def piece_copies(spot):
        low = low_bits(me, spot < chips // 2)
        start = (4 * reversed_int(spot % (chips // 2), bits - 1) + low) * block
        at = pl.ds(pl.multiple_of(start, block), block)
        return (
            pltpu.make_async_copy(history_ref.at[:, :, at], pieces.at[spot], piece_sem.at[spot]),
            pltpu.make_async_copy(decay_ref.at[:, at], rates_ref.at[spot], rate_sem.at[spot]),
        )

    load = pltpu.make_async_copy(embed_ref, entries, load_sem)
    load.start()
    for spot in range(chips):
        for copy in piece_copies(spot):
            copy.start()
    stores = [
        pltpu.make_async_copy(entries.at[:, pl.ds(p % team * block, block)], columns_ref.at[p], store_sem.at[p])
        for p in range(count)
    ]
    load.wait()
    for copy in stores:
        copy.start()

    @pl.loop(0, chips)
    def _(spot):
        for source, target, sem in ((history_ref, pieces, piece_sem), (decay_ref, rates_ref, rate_sem)):
            origin = source.at[:, :, pl.ds(0, block)] if len(source.shape) == 3 else source.at[:, pl.ds(0, block)]
            pltpu.make_async_copy(origin, target.at[spot], sem.at[spot]).wait()
        rate = rates_ref[spot] / total_len
        rates_ref[spot] = rate
        keep = jnp.exp(-rate)
        for b in range(seqs):
            wide[b] = masked(pieces[spot, b], lengths_ref[b], me * tile)
        sums = horner(keep, lambda b, s: wide[b, pl.ds(s, 1), :], seqs, tile)
        for b in range(seqs):
            states_ref[spot, b] = sums[b] * lift(rate, lengths_ref[b], (me + 1) * tile, tile)

    for copy in stores:
        copy.wait()


def partner_kernel(flip, bits, me_ref, lengths_ref, other_ref, states_ref, rates_ref, out_ref, wide):
    seqs, tile, _ = other_ref.shape
    half, _, _, block = out_ref.shape
    me = me_ref[0]
    partner = me + 1 - 2 * lax.rem(me, 2)
    base = 0 if flip else half

    @pl.loop(0, half)
    def _(spot):
        start = (4 * reverse_bits(spot, bits - 1) + low_bits(me, flip)) * block
        at = pl.ds(pl.multiple_of(start, block), block)
        rate = rates_ref[base + spot]
        keep = jnp.exp(-rate)
        for b in range(seqs):
            wide[b] = masked(other_ref[b, :, at], lengths_ref[b], partner * tile)
        sums = horner(keep, lambda b, s: wide[b, pl.ds(s, 1), :], seqs, tile)
        for b in range(seqs):
            out_ref[spot, b] = states_ref[base + spot, b] + sums[b] * lift(
                rate, lengths_ref[b], (partner + 1) * tile, tile
            )


def tables_kernel(total_len, team, span, me_ref, decay_ref, residue_ref, skip_ref, weights_ref, taps_ref, keeps_ref, ages_ref):
    modes, block = decay_ref.shape
    rate = decay_ref[...] / total_len
    residue = residue_ref[...]
    taps = []
    for i in range(CHUNK):
        weight = residue * jnp.exp(-rate * float(i))
        weights_ref[i] = weight
        taps.append(fold(weight))
    for start in range(0, CHUNK, ROWS):
        taps_ref[start : start + ROWS] = merge_rows(taps[start : start + ROWS])
    taps_ref[0:1] = taps_ref[0:1] + skip_ref[...]
    keeps_ref[0] = jnp.exp(-rate)
    keeps_ref[1] = jnp.exp(-rate * float(CHUNK))
    keeps_ref[2] = rate
    chunks = span // CHUNK
    begin = (lax.div(me_ref[0], team) * span).astype(f32)
    times = begin + float(CHUNK) * lax.broadcasted_iota(jnp.int32, (chunks, block), 0).astype(f32)

    @pl.loop(0, modes)
    def _(k):
        ages_ref[k] = jnp.exp(-keeps_ref[2, pl.ds(k, 1), :] * times)


def chunk_rows(group, offset):
    return pl.ds(group * ROWS * CHUNK + offset, ROWS, stride=CHUNK)


def fresh_kernel(team, me_ref, chosen_ref, table_ref, taps_ref, keeps_ref, conv_ref, carry_ref, fresh, ends):
    seqs, _, _ = chosen_ref.shape
    tiles, span = conv_ref.shape[1:3]
    modes = keeps_ref.shape[1]
    chunks = span // CHUNK
    late = lax.div(me_ref[0], team)
    strips = [(b, t) for t in range(tiles) for b in range(seqs)]

    def look_up(begin):
        for b in range(seqs):
            rows = chosen_ref[b, pl.ds(pl.multiple_of(begin, span), span), :]
            found = jnp.dot(rows, table_ref[...], preferred_element_type=f32)
            for t in range(tiles):
                fresh[b, t] = found[:, t * LANES : (t + 1) * LANES]

    def lanes(t):
        return slice(t * LANES, (t + 1) * LANES)

    def finish_chunks(values, b, t, group):
        for k in range(modes):
            keep = jnp.broadcast_to(keeps_ref[0, k : k + 1, lanes(t)], (ROWS, LANES))
            total = keep * values[0]
            for value in values[1:]:
                total = keep * (total + value)
            ends[b, t, chunk_rows(group, k), :] = total

    def values_of(b, t, group):
        return [fresh[b, t, chunk_rows(group, i), :] for i in range(CHUNK)]

    def rows_of(chunk):
        return pl.ds(pl.multiple_of(chunk * modes, modes), modes)

    for b, t in strips:
        carry_ref[b, t, 0:modes, :] = jnp.zeros((modes, LANES), f32)

    @pl.when(late == 1)
    def _():
        look_up(0)

        @pl.loop(0, chunks // ROWS)
        def _(group):
            for b, t in strips:
                finish_chunks(values_of(b, t, group), b, t, group)

        def advance(chunk, carries):
            return tuple(
                keeps_ref[1, :, lanes(t)] * carry + ends[b, t, rows_of(chunk), :] for (b, t), carry in zip(strips, carries)
            )

        carries = lax.fori_loop(0, chunks, advance, (jnp.zeros((modes, LANES), f32),) * len(strips))
        for (b, t), carry in zip(strips, carries):
            carry_ref[b, t, 0:modes, :] = carry

    look_up(late * span)

    @pl.loop(0, chunks // ROWS)
    def _(group):
        for b, t in strips:
            values = values_of(b, t, group)
            taps = [jnp.broadcast_to(taps_ref[d : d + 1, lanes(t)], (ROWS, LANES)) for d in range(CHUNK)]
            for i in range(CHUNK):
                total = taps[0] * values[i]
                for d in range(1, i + 1):
                    total = total + taps[d] * values[i - d]
                conv_ref[b, t, chunk_rows(group, i), :] = total
            finish_chunks(values, b, t, group)

    @pl.loop(1, chunks)
    def _(chunk):
        for b, t in strips:
            old, new = rows_of(chunk - 1), rows_of(chunk)
            carry_ref[b, t, new, :] = keeps_ref[1, :, lanes(t)] * carry_ref[b, t, old, :] + ends[b, t, old, :]


def mix_kernel(near_ref, far_ref, conv_ref, carry_ref, weights_ref, ages_ref, out_ref, state, total_ref):
    seqs, tiles, span, _ = conv_ref.shape
    modes = near_ref.shape[1]
    chunks = span // CHUNK
    for b in range(seqs):
        state[b] = near_ref[b] + far_ref[b]

    @pl.loop(0, chunks // ROWS)
    def _(group):
        old = pl.ds(pl.multiple_of(group * ROWS, ROWS), ROWS)
        for t in range(tiles):
            at = slice(t * LANES, (t + 1) * LANES)
            begun = [
                [
                    carry_ref[b, t, chunk_rows(group, k), :] + ages_ref[k, old, at] * state[b, k : k + 1, at]
                    for k in range(modes)
                ]
                for b in range(seqs)
            ]
            for i in range(CHUNK):
                weights = [weights_ref[i, k : k + 1, at] for k in range(modes)]
                for b in range(seqs):
                    total = conv_ref[b, t, chunk_rows(group, i), :]
                    other = weights[0] * begun[b][0]
                    for k in range(1, modes):
                        if k % 2:
                            total = total + weights[k] * begun[b][k]
                        else:
                            other = other + weights[k] * begun[b][k]
                    total_ref[b, t, chunk_rows(0, i), :] = total + other
        for chunk in range(ROWS):
            first = pl.multiple_of((group * ROWS + chunk) * CHUNK, CHUNK)
            for b, t in ((b, t) for b in range(seqs) for t in range(tiles)):
                at = slice(t * LANES, (t + 1) * LANES)
                mixed = total_ref[b, t, chunk * CHUNK : (chunk + 1) * CHUNK, :].astype(jnp.bfloat16)
                if len(out_ref.shape) == 4:
                    own = out_ref.shape[2]
                    spot = pl.ds(pl.multiple_of(lax.rem(first, own), CHUNK), CHUNK)
                    out_ref[lax.div(first, own), b, spot, at] = mixed
                else:
                    out_ref[b, pl.ds(first, CHUNK), at] = mixed


def join_kernel(mixed_ref, out_ref):
    count, seqs, _, block = mixed_ref.shape
    for p in range(count):
        for b in range(seqs):
            out_ref[b, :, p * block : (p + 1) * block] = mixed_ref[p, b]


def call(kernel, grid, scalars, in_specs, out_specs, out_shape, flops, moved, scratch=()):
    return pl.pallas_call(
        kernel,
        grid_spec=pltpu.PrefetchScalarGridSpec(
            num_scalar_prefetch=scalars,
            grid=grid,
            in_specs=in_specs,
            out_specs=out_specs,
            scratch_shapes=scratch,
        ),
        out_shape=out_shape,
        cost_estimate=pl.CostEstimate(flops=flops, bytes_accessed=moved, transcendentals=0),
        compiler_params=pltpu.CompilerParams(vmem_limit_bytes=VMEM),
    )


def body(history, lengths, token_ids, embed, residue, decay, skip):
    devices = lax.axis_size("ctx")
    me = lax.axis_index("ctx")
    seqs, tile, width = history.shape
    modes = decay.shape[0]
    rows = embed.shape[0]
    gen = token_ids.shape[1]
    total_len = float(tile * devices)
    team = devices // 2
    chips = team // 2
    bits = chips.bit_length() - 1
    assert devices == 4 * 2**bits
    block = width // team
    span = gen // 2
    chunks = span // CHUNK
    tiles = block // LANES
    assert block % LANES == 0 and span % (ROWS * CHUNK) == 0
    own = gen // devices
    place = me.astype(jnp.int32).reshape(1)
    history, embed, residue, decay, skip, lengths = (
        pltpu.with_memory_space_constraint(x, pltpu.HBM)
        for x in (history, embed, residue, decay, skip.reshape(1, width), lengths)
    )
    chip = lax.rem(me, team) // 2
    opposite = [(j, (j + team) % devices) for j in range(devices)]
    shape = jax.ShapeDtypeStruct

    def paired(x, distance):
        return lax.ppermute(x, "ctx", [(j, j ^ distance) for j in range(devices)])

    swapped = pltpu.with_memory_space_constraint(paired(history, 1), pltpu.VMEM)

    hbm = pl.BlockSpec(memory_space=pltpu.HBM)
    vmem = pl.BlockSpec(memory_space=pltpu.VMEM)
    columns, states, rates = call(
        lambda *refs: prepare_kernel(total_len, bits, *refs),
        (1,),
        2,
        [hbm] * 3,
        [hbm, vmem, vmem],
        [
            shape((devices, rows, block), jnp.bfloat16),
            shape((chips, seqs, modes, block), f32),
            shape((chips, modes, block), f32),
        ],
        2 * seqs * tile * modes * block * chips,
        2**20,
        [
            pltpu.VMEM((rows, width), jnp.bfloat16),
            pltpu.VMEM((chips, seqs, tile, block), jnp.bfloat16),
            pltpu.VMEM((seqs, tile, block), f32),
            pltpu.SemaphoreType.DMA(()),
            pltpu.SemaphoreType.DMA((chips,)),
            pltpu.SemaphoreType.DMA((chips,)),
            pltpu.SemaphoreType.DMA((devices,)),
        ],
    )(place, lengths, embed, history, decay)
    table = lax.all_to_all(columns, "ctx", 0, 0, tiled=True)
    table = table.reshape(devices * rows, block)

    def finish(flip):
        return call(
            lambda *refs: partner_kernel(flip, bits, *refs),
            (1,),
            2,
            [vmem] * 3,
            vmem,
            shape((chips // 2, seqs, modes, block), f32),
            seqs * tile * modes * block * chips,
            2**20,
            [pltpu.VMEM((seqs, tile, block), f32)],
        )(place, lengths, swapped, states, rates)

    sent = finish(True)
    came = paired(sent, 2)
    mine = finish(False) + came
    done = 1
    while done < bits:
        now = min(2, bits - done)
        ways, size = 2**now, mine.shape[0] // 2**now
        digit = lax.rem(lax.div(chip, 2**done), ways)
        take = lambda x, d: lax.dynamic_slice_in_dim(x, reverse_bits(d, now) * size, size, 0)
        total = take(mine, digit)
        for d in range(1, ways):
            flipped = digit ^ d
            total = total + paired(take(mine, flipped), d << (done + 1))
        mine = total
        done += now
    near = mine[0]
    far = lax.ppermute(near, "ctx", opposite)

    entry = lax.broadcasted_iota(jnp.int32, (seqs, gen, devices * rows), 2)
    chosen = (token_ids[:, :, None] == entry).astype(jnp.bfloat16)
    strip = lambda g, at: (0, lax.rem(at[0], team))
    weights, taps, keeps, ages = call(
        lambda *refs: tables_kernel(total_len, team, span, *refs),
        (1,),
        1,
        [pl.BlockSpec((modes, block), strip)] * 2 + [pl.BlockSpec((1, block), strip)],
        [vmem] * 4,
        [
            shape((CHUNK, modes, block), f32),
            shape((CHUNK, block), f32),
            shape((3, modes, block), f32),
            shape((modes, chunks, block), f32),
        ],
        10**6,
        2**20,
    )(place, decay, residue, skip)
    conv, carry = call(
        lambda *refs: fresh_kernel(team, *refs),
        (1,),
        1,
        [vmem] * 4,
        [vmem] * 2,
        [shape((seqs, tiles, span, LANES), f32), shape((seqs, tiles, chunks * modes, LANES), f32)],
        6 * seqs * span * modes * block,
        2**21,
        [pltpu.VMEM((seqs, tiles, span, LANES), f32), pltpu.VMEM((seqs, tiles, chunks * modes, LANES), f32)],
    )(place, chosen, table, taps, keeps)

    direct = own % CHUNK == 0
    mixed = call(
        mix_kernel,
        (1,),
        0,
        [vmem] * 6,
        vmem,
        shape((team, seqs, own, block) if direct else (seqs, span, block), jnp.bfloat16),
        3 * seqs * span * modes * block,
        2**21,
        [pltpu.VMEM((seqs, modes, block), f32), pltpu.VMEM((seqs, tiles, ROWS * CHUNK, LANES), f32)],
    )(near, far, conv, carry, weights, ages)
    if not direct:
        mixed = mixed.reshape(seqs, team, own, block).transpose(1, 0, 2, 3)
    halves = [[h * team + p for p in range(team)] for h in range(2)]
    result = lax.all_to_all(mixed, "ctx", 0, 0, tiled=True, axis_index_groups=halves)
    parts = 4
    return call(
        join_kernel,
        (parts,),
        0,
        [pl.BlockSpec((team // parts, seqs, own, block), lambda g: (g, 0, 0, 0))],
        pl.BlockSpec((seqs, own, width // parts), lambda g: (0, 0, g)),
        shape((seqs, own, width), jnp.bfloat16),
        10**5,
        2**20,
    )(result)


def solution(mesh):
    placed = (P("group", "ctx", None), P("group"), P("group", None), P("ctx", None), P(), P(), P())
    return jax.shard_map(body, mesh=mesh, in_specs=placed, out_specs=P("group", "ctx", None), check_vma=False)
```

time: 58.4 us -> 56.8 us (0.973)
  Pallas kernels: 16.1 us -> 13.6 us
  waiting for transfers between devices: 12.4 us -> 13.4 us
    pallas_call x3 -> x4, Pallas kernels: 11.9 us -> 9.37 us  [the longest x1 3.94 us: body(): call(lambda *refs: prepare_kernel(total_len, bits, *refs), (1,), 2, [hbm]...]
    ppermute x5, waiting for transfers between devices: 12.3 us -> 13.4 us  [paired(): return lax.ppermute(x, 'ctx', [(j, j ^ distance) for j in range(devices)])]
  transfers between devices with their start and end apart: 7 -> 7, of which waited for: 4 -> 4; matrix products, arithmetic and copies ran while one was open for 1% -> 1% of each run, Pallas kernels for 21% -> 19%
where the time goes in v6:
time: 56.8 us; the launch traced here: 56.4 us
  starting transfers between devices  15.8 us (28%)
  Pallas kernels  13.6 us (24%)
  waiting for transfers between devices  13.4 us (24%)
  blocking collectives  13.1 us (23%)
    ppermute x5, waiting for transfers between devices, paired(): return lax.ppermute(x, 'ctx', [(j, j ^ distance) for j in range(devices)])  13.4 us
    all_to_all x1, blocking collectives, body(): lax.all_to_all(mixed, 'ctx', 0, 0, tiled=True, axis_index_groups=halves)  13.1 us
    all_to_all x1, starting transfers between devices, body(): table = lax.all_to_all(columns, 'ctx', 0, 0, tiled=True)  6.95 us
    ppermute x5, starting transfers between devices, paired(): return lax.ppermute(x, 'ctx', [(j, j ^ distance) for j in range(devices)])  5.88 us
    pallas_call x1, Pallas kernels, body(): call(lambda *refs: prepare_kernel(total_len, bits, *refs), (1,), 2, [hbm]...  3.94 us
    ppermute x1, starting transfers between devices, body(): far = lax.ppermute(near, 'ctx', opposite)  3 us
    pallas_call x2, Pallas kernels, finish(): call(lambda *refs: partner_kernel(flip, bits, *refs), (1,), 2, [vmem] * 3...  2.85 us
    pallas_call x1, Pallas kernels, body(): call(lambda *refs: fresh_kernel(team, *refs), (1,), 1, [vmem] * 4, [vmem]...  2.51 us
  transfers between devices with their start and end apart: 7, of which 4 were waited for; matrix products, arithmetic and copies ran while one was open for 1% of the time, Pallas kernels for 19%

profile of v6, /device:TPU:0, one launch (start us, length us, event | category | flops | bytes accessed | tf_op | source)
XLA Modules:
  0.0 56.4 jit_solution(4458467256240880916)
XLA Ops:
  0.0 0.5 collective-permute-start
  0.5 3.9 %shard_map.73 = (bf16[32,16,512]{2,1,0:T(8,128)(2,1)}, f32[8,2,16,512]{3,2,1,0:T(8,128)S(1)}, f32[8,16,512]{2,1,0:T(8,128)S(1)}) custom-call(s32[1]{0:T(128)} %bitcast.refs_0_, s32[2]{0:T(128)} %refs_1_.6, bf16[16,8192]{1,0:T(8,128)(2,1)} %refs_2_.2, bf16[2,32,8192]{2,1,0:T(8,128)(2,1)} %refs_3_.1, f32[16,8192]{1,0:T(8,128)} %refs_1_.7), custom_call_target="tpu_custom_call" | custom-call | flops 8388608 | bytes 1048576 | tf_op jit(solution)/shard_map/pallas_call | solution.py:346
  4.4 7.0 %all-to-all-start = ((bf16[32,16,512]{2,1,0:T(8,128)(2,1)}), bf16[32,16,512]{2,1,0:T(8,128)(2,1)S(1)}, u32[]{:S(2)}, u32[]{:S(2)}) async-start(bf16[32,16,512]{2,1,0:T(8,128)(2,1)} %get-tuple-element.16), calls=%async_computation | async-start | bytes 1048576 | tf_op jit(solution)/shard_map/all_to_all | solution.py:369
  11.4 0.0 collective-permute-done.refs_2_
  11.4 1.4 %shard_map.75 = f32[4,2,16,512]{3,2,1,0:T(8,128)S(1)} custom-call(s32[1]{0:T(128)} %bitcast.refs_0_, s32[2]{0:T(128)} %refs_1_.6, bf16[2,32,8192]{2,1,0:T(8,128)(2,1)S(1)} %collective-permute-done.refs_2_, f32[8,2,16,512]{3,2,1,0:T(8,128)S(1)} %get-tuple-element.14.refs_3_, f32[8,16,512]{2,1,0:T(8,128)S(1)} %get-tuple-element.15.refs_4_), custom_call_target="tpu_custom_call" | custom-call | flops 4194304 | bytes 1048576 | tf_op jit(solution)/shard_map/pallas_call | solution.py:373
  12.9 1.8 %collective-permute-start.1 = (f32[4,2,16,512]{3,2,1,0:T(8,128)S(1)}, f32[4,2,16,512]{3,2,1,0:T(8,128)S(1)}, u32[]{:S(2)}, u32[]{:S(2)}) collective-permute-start(f32[4,2,16,512]{3,2,1,0:T(8,128)S(1)} %shard_map.75), channel_id=1, source_target_pairs={{0,2},{1,3},{2,0},{3,1},{4,6},{5,7},{6,4},{7,5},{8,10},{9,11},{10,... | collective-permute-start | bytes 786440 | tf_op jit(solution)/shard_map/ppermute | solution.py:340
  14.7 1.4 %shard_map.74 = f32[4,2,16,512]{3,2,1,0:T(8,128)S(1)} custom-call(s32[1]{0:T(128)} %bitcast.refs_0_, s32[2]{0:T(128)} %refs_1_.6, bf16[2,32,8192]{2,1,0:T(8,128)(2,1)S(1)} %collective-permute-done.refs_2_, f32[8,2,16,512]{3,2,1,0:T(8,128)S(1)} %get-tuple-element.14.refs_3_, f32[8,16,512]{2,1,0:T(8,128)S(1)} %get-tuple-element.15.refs_4_), custom_call_target="tpu_custom_call" | custom-call | flops 4194304 | bytes 1048576 | tf_op jit(solution)/shard_map/pallas_call | solution.py:373
  16.1 0.0 copy-start
  16.1 8.9 %collective-permute-done.1 = f32[4,2,16,512]{3,2,1,0:T(8,128)S(1)} collective-permute-done((f32[4,2,16,512]{3,2,1,0:T(8,128)S(1)}, f32[4,2,16,512]{3,2,1,0:T(8,128)S(1)}, u32[]{:S(2)}, u32[]{:S(2)}) %collective-permute-start.1) | collective-permute-done | bytes 262176 | tf_op jit(solution)/shard_map/ppermute | solution.py:340
  25.1 1.3 %collective-permute-start.2 = (f32[1,2,16,512]{3,2,1,0:T(8,128)S(1)}, f32[1,2,16,512]{3,2,1,0:T(8,128)S(1)}, u32[]{:S(2)}, u32[]{:S(2)}) collective-permute-start(f32[1,2,16,512]{3,2,1,0:T(8,128)S(1)} %get-tuple-element.23), channel_id=1, source_target_pairs={{0,4},{1,5},{2,6},{3,7},{4,0},{5,1},{6,2},{7,3},{8,12},{9,13},{10,... | collective-permute-start | bytes 196616 | tf_op jit(solution)/shard_map/ppermute | solution.py:340
  26.4 1.6 %collective-permute-start.3 = (f32[1,2,16,512]{3,2,1,0:T(8,128)S(1)}, f32[1,2,16,512]{3,2,1,0:T(8,128)S(1)}, u32[]{:S(2)}, u32[]{:S(2)}) collective-permute-start(f32[1,2,16,512]{3,2,1,0:T(8,128)S(1)} %get-tuple-element.25), channel_id=1, source_target_pairs={{0,8},{1,9},{2,10},{3,11},{4,12},{5,13},{6,14},{7,15},{8,0},{9,1},... | collective-permute-start | bytes 196616 | tf_op jit(solution)/shard_map/ppermute | solution.py:340
  28.0 0.6 %collective-permute-start.4 = (f32[1,2,16,512]{3,2,1,0:T(8,128)S(1)}, f32[1,2,16,512]{3,2,1,0:T(8,128)S(1)}, u32[]{:S(2)}, u32[]{:S(2)}) collective-permute-start(f32[1,2,16,512]{3,2,1,0:T(8,128)S(1)} %get-tuple-element.24), channel_id=1, source_target_pairs={{0,12},{1,13},{2,14},{3,15},{4,8},{5,9},{6,10},{7,11},{8,4},{9,5},... | collective-permute-start | bytes 196616 | tf_op jit(solution)/shard_map/ppermute | solution.py:340
  28.7 0.8 %collective-permute-done.2 = f32[1,2,16,512]{3,2,1,0:T(8,128)S(1)} collective-permute-done((f32[1,2,16,512]{3,2,1,0:T(8,128)S(1)}, f32[1,2,16,512]{3,2,1,0:T(8,128)S(1)}, u32[]{:S(2)}, u32[]{:S(2)}) %collective-permute-start.2) | collective-permute-done | bytes 65568 | tf_op jit(solution)/shard_map/ppermute | solution.py:340
  29.4 1.7 %collective-permute-done.3 = f32[1,2,16,512]{3,2,1,0:T(8,128)S(1)} collective-permute-done((f32[1,2,16,512]{3,2,1,0:T(8,128)S(1)}, f32[1,2,16,512]{3,2,1,0:T(8,128)S(1)}, u32[]{:S(2)}, u32[]{:S(2)}) %collective-permute-start.3) | collective-permute-done | bytes 65568 | tf_op jit(solution)/shard_map/ppermute | solution.py:340
  31.1 2.1 %collective-permute-done.4 = f32[1,2,16,512]{3,2,1,0:T(8,128)S(1)} collective-permute-done((f32[1,2,16,512]{3,2,1,0:T(8,128)S(1)}, f32[1,2,16,512]{3,2,1,0:T(8,128)S(1)}, u32[]{:S(2)}, u32[]{:S(2)}) %collective-permute-start.4) | collective-permute-done | bytes 65568 | tf_op jit(solution)/shard_map/ppermute | solution.py:340
  33.2 3.0 %collective-permute-start.5 = (f32[2,16,512]{2,1,0:T(8,128)S(1)}, f32[2,16,512]{2,1,0:T(8,128)S(1)}, u32[]{:S(2)}, u32[]{:S(2)}) collective-permute-start(f32[2,16,512]{2,1,0:T(8,128)S(1)} %add_bitcast_fusion.near_ref), channel_id=1, source_target_pairs={{0,16},{1,17},{2,18},{3,19},{4,20},{5,21},{6,22},{7,23},{8,24},{9,... | collective-permute-start | bytes 196616 | tf_op jit(solution)/shard_map/ppermute | solution.py:401
  36.2 0.0 copy-done
  36.2 0.2 fusion.refs_1_
  36.4 1.2 %shard_map.76 = (f32[16,16,512]{2,1,0:T(8,128)S(1)}, f32[16,512]{1,0:T(8,128)S(1)}, f32[3,16,512]{2,1,0:T(8,128)S(1)}, f32[16,16,512]{2,1,0:T(8,128)S(1)}) custom-call(s32[1]{0:T(128)} %bitcast.refs_0_, f32[16,8192]{1,0:T(8,128)} %refs_1_.7, f32[16,8192]{1,0:T(8,128)} %refs_2_.3, f32[1,8192]{1,0:T(1,128)} %bitcast.6), custom_call_target="tpu_custom_call" | custom-call | flops 1000000 | bytes 1048576 | tf_op jit(solution)/shard_map/pallas_call | solution.py:406
  37.6 0.0 all-to-all-done
  37.6 2.5 %shard_map.77 = (f32[2,4,256,128]{3,2,1,0:T(8,128)S(1)}, f32[2,4,256,128]{3,2,1,0:T(8,128)S(1)}) custom-call(s32[1]{0:T(128)} %bitcast.refs_0_, bf16[2,512,512]{2,1,0:T(8,128)(2,1)S(1)} %fusion.refs_1_, bf16[512,512]{1,0:T(8,128)(2,1)S(1)} %bitcast.5, f32[16,512]{1,0:T(8,128)S(1)} %get-tuple-element.17.refs_3_, f32[3,16,512]{2,1,0:T(8,128)S(1)} %get-tuple-element.18.refs_4_), custom_call_target="tpu_custom_call" | custom-call | flops 25165824 | bytes 2097152 | tf_op jit(solution)/shard_map/pallas_call | solution.py:421
  40.1 0.0 collective-permute-done.5.far_ref
  40.1 1.8 %shard_map.78 = bf16[16,2,16,512]{3,2,1,0:T(8,128)(2,1)S(1)} custom-call(f32[2,16,512]{2,1,0:T(8,128)S(1)} %add_bitcast_fusion.near_ref, f32[2,16,512]{2,1,0:T(8,128)S(1)} %collective-permute-done.5.far_ref, f32[2,4,256,128]{3,2,1,0:T(8,128)S(1)} %get-tuple-element.19.conv_ref, f32[2,4,256,128]{3,2,1,0:T(8,128)S(1)} %get-tuple-element.20.carry_ref, ...), custom_call_target="tpu_custom_call" | custom-call | flops 12582912 | bytes 2097152 | tf_op jit(solution)/shard_map/pallas_call | solution.py:434
  41.9 13.1 %all_to_all.10.mixed_ref = bf16[16,2,16,512]{3,2,1,0:T(8,128)(2,1)S(1)} all-to-all(bf16[16,2,16,512]{3,2,1,0:T(8,128)(2,1)S(1)} %shard_map.78), channel_id=1, replica_groups={{0,1,2,3,4,5,6,7,8,9,10,11,12,13,14,15},{16,17,18,19,20,21,22,23,24,25,..., dimensions={0} | all-to-all | bytes 1048576 | tf_op jit(solution)/shard_map/all_to_all | solution.py:448
  55.1 1.4 %shard_map.79 = bf16[2,16,8192]{2,1,0:T(8,128)(2,1)} custom-call(bf16[16,2,16,512]{3,2,1,0:T(8,128)(2,1)S(1)} %all_to_all.10.mixed_ref), custom_call_target="tpu_custom_call" | custom-call | flops 100000 | bytes 1048576 | tf_op jit(solution)/shard_map/pallas_call | solution.py:450
  (3 shorter events, 0.1 us)
Async XLA Ops:
  0.0 11.4 %collective-permute-start = (bf16[2,32,8192]{2,1,0:T(8,128)(2,1)}, bf16[2,32,8192]{2,1,0:T(8,128)(2,1)S(1)}, u32[]{:S(2)}, u32[]{:S(2)}) collective-permute-start(bf16[2,32,8192]{2,1,0:T(8,128)(2,1)} %refs_3_.1), channel_id=1, source_target_pairs={{0,1},{1,0},{2,3},{3,2},{4,5},{5,4},{6,7},{7,6},{8,9},{9,8},{10,11... | collective-permute-start | bytes 3145736 | tf_op jit(solution)/shard_map/ppermute | solution.py:340
  4.4 33.2 %all-to-all-start = ((bf16[32,16,512]{2,1,0:T(8,128)(2,1)}), bf16[32,16,512]{2,1,0:T(8,128)(2,1)S(1)}, u32[]{:S(2)}, u32[]{:S(2)}) async-start(bf16[32,16,512]{2,1,0:T(8,128)(2,1)} %get-tuple-element.16), calls=%async_computation | async-start | bytes 1048576 | tf_op jit(solution)/shard_map/all_to_all | solution.py:369
  12.9 12.2 %collective-permute-start.1 = (f32[4,2,16,512]{3,2,1,0:T(8,128)S(1)}, f32[4,2,16,512]{3,2,1,0:T(8,128)S(1)}, u32[]{:S(2)}, u32[]{:S(2)}) collective-permute-start(f32[4,2,16,512]{3,2,1,0:T(8,128)S(1)} %shard_map.75), channel_id=1, source_target_pairs={{0,2},{1,3},{2,0},{3,1},{4,6},{5,7},{6,4},{7,5},{8,10},{9,11},{10,... | collective-permute-start | bytes 786440 | tf_op jit(solution)/shard_map/ppermute | solution.py:340
  16.1 20.1 %copy-start = (s32[2,512]{1,0:T(2,128)S(1)}, s32[2,512]{1,0:T(2,128)}, u32[]{:S(2)}) copy-start(s32[2,512]{1,0:T(2,128)} %param.9) | copy-start | bytes 12292
  25.1 4.3 %collective-permute-start.2 = (f32[1,2,16,512]{3,2,1,0:T(8,128)S(1)}, f32[1,2,16,512]{3,2,1,0:T(8,128)S(1)}, u32[]{:S(2)}, u32[]{:S(2)}) collective-permute-start(f32[1,2,16,512]{3,2,1,0:T(8,128)S(1)} %get-tuple-element.23), channel_id=1, source_target_pairs={{0,4},{1,5},{2,6},{3,7},{4,0},{5,1},{6,2},{7,3},{8,12},{9,13},{10,... | collective-permute-start | bytes 196616 | tf_op jit(solution)/shard_map/ppermute | solution.py:340
  26.4 4.7 %collective-permute-start.3 = (f32[1,2,16,512]{3,2,1,0:T(8,128)S(1)}, f32[1,2,16,512]{3,2,1,0:T(8,128)S(1)}, u32[]{:S(2)}, u32[]{:S(2)}) collective-permute-start(f32[1,2,16,512]{3,2,1,0:T(8,128)S(1)} %get-tuple-element.25), channel_id=1, source_target_pairs={{0,8},{1,9},{2,10},{3,11},{4,12},{5,13},{6,14},{7,15},{8,0},{9,1},... | collective-permute-start | bytes 196616 | tf_op jit(solution)/shard_map/ppermute | solution.py:340
  28.0 5.2 %collective-permute-start.4 = (f32[1,2,16,512]{3,2,1,0:T(8,128)S(1)}, f32[1,2,16,512]{3,2,1,0:T(8,128)S(1)}, u32[]{:S(2)}, u32[]{:S(2)}) collective-permute-start(f32[1,2,16,512]{3,2,1,0:T(8,128)S(1)} %get-tuple-element.24), channel_id=1, source_target_pairs={{0,12},{1,13},{2,14},{3,15},{4,8},{5,9},{6,10},{7,11},{8,4},{9,5},... | collective-permute-start | bytes 196616 | tf_op jit(solution)/shard_map/ppermute | solution.py:340
  33.2 6.9 %collective-permute-start.5 = (f32[2,16,512]{2,1,0:T(8,128)S(1)}, f32[2,16,512]{2,1,0:T(8,128)S(1)}, u32[]{:S(2)}, u32[]{:S(2)}) collective-permute-start(f32[2,16,512]{2,1,0:T(8,128)S(1)} %add_bitcast_fusion.near_ref), channel_id=1, source_target_pairs={{0,16},{1,17},{2,18},{3,19},{4,20},{5,21},{6,22},{7,23},{8,24},{9,... | collective-permute-start | bytes 196616 | tf_op jit(solution)/shard_map/ppermute | solution.py:401

commit v7 on v6

--- a/solution.py
+++ b/solution.py
@@ -17,10 +17,6 @@
     for k in range(bits):
         result = result + lax.rem(lax.div(value, 2**k), 2) * 2 ** (bits - 1 - k)
     return result
-
-
-def reversed_int(value, bits):
-    return sum((value >> k & 1) << (bits - 1 - k) for k in range(bits))
 
 
 def merge_rows(parts):
@@ -54,9 +50,12 @@
     return lax.fori_loop(0, tile, step, (jnp.zeros(keep.shape, f32),) * count, unroll=16)
 
 
-def low_bits(me, flip):
-    low = lax.rem(me, 4)
-    return lax.rem(low + 2, 4) if flip else low
+def block_of(me, spot, give, bits):
+    core = lax.rem(me, 2)
+    top = lax.rem(lax.div(me, 2**bits), 2)
+    if give:
+        top = 1 - top
+    return 2 * (top * 2 ** (bits - 1) + reverse_bits(spot, bits - 1)) + core
 
 
 def masked(value, length, start):
@@ -70,29 +69,29 @@
 
 def prepare_kernel(
     total_len, bits, me_ref, lengths_ref, embed_ref, history_ref, decay_ref,
-    columns_ref, states_ref, rates_ref,
+    columns_ref, states_ref, decays_ref, held_ref,
     entries, pieces, wide, load_sem, piece_sem, rate_sem, store_sem,
 ):
     count, _, block = columns_ref.shape
+    half, seqs, tile, _ = pieces.shape
     team = count // 2
-    chips = team // 2
-    seqs, tile, _ = history_ref.shape
     me = me_ref[0]
 
-    def piece_copies(spot):
-        low = low_bits(me, spot < chips // 2)
-        start = (4 * reversed_int(spot % (chips // 2), bits - 1) + low) * block
-        at = pl.ds(pl.multiple_of(start, block), block)
+    def fetch(spot, give):
+        start = pl.multiple_of(block_of(me, spot, give, bits) * block, block)
+        target, index = (pieces, spot) if give else (held_ref, spot + half)
         return (
-            pltpu.make_async_copy(history_ref.at[:, :, at], pieces.at[spot], piece_sem.at[spot]),
-            pltpu.make_async_copy(decay_ref.at[:, at], rates_ref.at[spot], rate_sem.at[spot]),
+            pltpu.make_async_copy(decay_ref.at[:, pl.ds(start, block)], decays_ref.at[index], rate_sem.at[index]),
+            pltpu.make_async_copy(history_ref.at[:, :, pl.ds(start, block)], target.at[spot], piece_sem.at[index]),
         )
 
+    copies = [copy for give in (True, False) for spot in range(half) for copy in fetch(spot, give)]
     load = pltpu.make_async_copy(embed_ref, entries, load_sem)
+    for copy in copies[: 2 * half]:
+        copy.start()
     load.start()
-    for spot in range(chips):
-        for copy in piece_copies(spot):
-            copy.start()
+    for copy in copies[2 * half :]:
+        copy.start()
     stores = [
         pltpu.make_async_copy(entries.at[:, pl.ds(p % team * block, block)], columns_ref.at[p], store_sem.at[p])
         for p in range(count)
@@ -100,45 +99,57 @@
     load.wait()
     for copy in stores:
         copy.start()
-
-    @pl.loop(0, chips)
+    for copy in copies[: 2 * half]:
+        copy.wait()
+
+    @pl.loop(0, half)
     def _(spot):
-        for source, target, sem in ((history_ref, pieces, piece_sem), (decay_ref, rates_ref, rate_sem)):
-            origin = source.at[:, :, pl.ds(0, block)] if len(source.shape) == 3 else source.at[:, pl.ds(0, block)]
-            pltpu.make_async_copy(origin, target.at[spot], sem.at[spot]).wait()
-        rate = rates_ref[spot] / total_len
-        rates_ref[spot] = rate
-        keep = jnp.exp(-rate)
+        rate = decays_ref[spot] / total_len
+        sums = partial_states(rate, lambda b: pieces[spot, b], wide, lengths_ref, me * tile)
         for b in range(seqs):
-            wide[b] = masked(pieces[spot, b], lengths_ref[b], me * tile)
-        sums = horner(keep, lambda b, s: wide[b, pl.ds(s, 1), :], seqs, tile)
-        for b in range(seqs):
-            states_ref[spot, b] = sums[b] * lift(rate, lengths_ref[b], (me + 1) * tile, tile)
-
-    for copy in stores:
+            states_ref[spot, b] = sums[b]
+
+    for copy in copies[2 * half :] + stores:
         copy.wait()
 
 
-def partner_kernel(flip, bits, me_ref, lengths_ref, other_ref, states_ref, rates_ref, out_ref, wide):
-    seqs, tile, _ = other_ref.shape
-    half, _, _, block = out_ref.shape
+def partial_states(rate, tile_of, wide, lengths_ref, start):
+    seqs, tile, _ = wide.shape
+    keep = jnp.exp(-rate)
+    for b in range(seqs):
+        wide[b] = masked(tile_of(b), lengths_ref[b], start)
+    sums = horner(keep, lambda b, s: wide[b, pl.ds(s, 1), :], seqs, tile)
+    return [sums[b] * lift(rate, lengths_ref[b], start + tile, tile) for b in range(seqs)]
+
+
+def give_kernel(total_len, bits, me_ref, lengths_ref, other_ref, states_ref, decays_ref, out_ref, wide):
+    seqs, tile, block = wide.shape
     me = me_ref[0]
     partner = me + 1 - 2 * lax.rem(me, 2)
-    base = 0 if flip else half
+
+    @pl.loop(0, out_ref.shape[0])
+    def _(spot):
+        at = pl.ds(pl.multiple_of(block_of(me, spot, True, bits) * block, block), block)
+        rate = decays_ref[spot] / total_len
+        sums = partial_states(rate, lambda b: other_ref[b, :, at], wide, lengths_ref, partner * tile)
+        for b in range(seqs):
+            out_ref[spot, b] = states_ref[spot, b] + sums[b]
+
+
+def keep_kernel(total_len, bits, me_ref, lengths_ref, other_ref, held_ref, decays_ref, out_ref, wide):
+    seqs, tile, block = wide.shape
+    half = out_ref.shape[0]
+    me = me_ref[0]
+    partner = me + 1 - 2 * lax.rem(me, 2)
 
     @pl.loop(0, half)
     def _(spot):
-        start = (4 * reverse_bits(spot, bits - 1) + low_bits(me, flip)) * block
-        at = pl.ds(pl.multiple_of(start, block), block)
-        rate = rates_ref[base + spot]
-        keep = jnp.exp(-rate)
+        at = pl.ds(pl.multiple_of(block_of(me, spot, False, bits) * block, block), block)
+        rate = decays_ref[spot + half] / total_len
+        own = partial_states(rate, lambda b: held_ref[spot, b], wide, lengths_ref, me * tile)
+        sums = partial_states(rate, lambda b: other_ref[b, :, at], wide, lengths_ref, partner * tile)
         for b in range(seqs):
-            wide[b] = masked(other_ref[b, :, at], lengths_ref[b], partner * tile)
-        sums = horner(keep, lambda b, s: wide[b, pl.ds(s, 1), :], seqs, tile)
-        for b in range(seqs):
-            out_ref[spot, b] = states_ref[base + spot, b] + sums[b] * lift(
-                rate, lengths_ref[b], (partner + 1) * tile, tile
-            )
+            out_ref[spot, b] = own[b] + sums[b]
 
 
 def tables_kernel(total_len, team, span, me_ref, decay_ref, residue_ref, skip_ref, weights_ref, taps_ref, keeps_ref, ages_ref):
@@ -286,11 +297,19 @@
                     out_ref[b, pl.ds(first, CHUNK), at] = mixed
 
 
-def join_kernel(mixed_ref, out_ref):
+def join_kernel(mixed_ref, out_ref, sem):
     count, seqs, _, block = mixed_ref.shape
-    for p in range(count):
-        for b in range(seqs):
-            out_ref[b, :, p * block : (p + 1) * block] = mixed_ref[p, b]
+    copies = [
+        pltpu.make_async_copy(
+            mixed_ref.at[p, b], out_ref.at[b, :, pl.ds(p * block, block)], sem.at[p, b]
+        )
+        for p in range(count)
+        for b in range(seqs)
+    ]
+    for copy in copies:
+        copy.start()
+    for copy in copies:
+        copy.wait()
 
 
 def call(kernel, grid, scalars, in_specs, out_specs, out_shape, flops, moved, scratch=()):
@@ -343,22 +362,24 @@
 
     hbm = pl.BlockSpec(memory_space=pltpu.HBM)
     vmem = pl.BlockSpec(memory_space=pltpu.VMEM)
-    columns, states, rates = call(
+    half = chips // 2
+    columns, states, decays, held = call(
         lambda *refs: prepare_kernel(total_len, bits, *refs),
         (1,),
         2,
         [hbm] * 3,
-        [hbm, vmem, vmem],
+        [hbm, vmem, vmem, vmem],
         [
             shape((devices, rows, block), jnp.bfloat16),
-            shape((chips, seqs, modes, block), f32),
+            shape((half, seqs, modes, block), f32),
             shape((chips, modes, block), f32),
+            shape((half, seqs, tile, block), jnp.bfloat16),
         ],
-        2 * seqs * tile * modes * block * chips,
+        2 * seqs * tile * modes * block * half,
         2**20,
         [
             pltpu.VMEM((rows, width), jnp.bfloat16),
-            pltpu.VMEM((chips, seqs, tile, block), jnp.bfloat16),
+            pltpu.VMEM((half, seqs, tile, block), jnp.bfloat16),
             pltpu.VMEM((seqs, tile, block), f32),
             pltpu.SemaphoreType.DMA(()),
             pltpu.SemaphoreType.DMA((chips,)),
@@ -369,25 +390,26 @@
     table = lax.all_to_all(columns, "ctx", 0, 0, tiled=True)
     table = table.reshape(devices * rows, block)
 
-    def finish(flip):
+    def finish(kernel, operand, flops):
         return call(
-            lambda *refs: partner_kernel(flip, bits, *refs),
+            lambda *refs: kernel(total_len, bits, *refs),
             (1,),
             2,
             [vmem] * 3,
             vmem,
-            shape((chips // 2, seqs, modes, block), f32),
-            seqs * tile * modes * block * chips,
+            shape((half, seqs, modes, block), f32),
+            flops,
             2**20,
             [pltpu.VMEM((seqs, tile, block), f32)],
-        )(place, lengths, swapped, states, rates)
-
-    sent = finish(True)
-    came = paired(sent, 2)
-    mine = finish(False) + came
-    done = 1
-    while done < bits:
-        now = min(2, bits - done)
+        )(place, lengths, swapped, operand, decays)
+
+    work = 2 * seqs * tile * modes * block * half
+    sent = finish(give_kernel, states, work)
+    came = paired(sent, 2**bits)
+    mine = finish(keep_kernel, held, 2 * work) + came
+    done = 0
+    while done < bits - 1:
+        now = min(2, bits - 1 - done)
         ways, size = 2**now, mine.shape[0] // 2**now
         digit = lax.rem(lax.div(chip, 2**done), ways)
         take = lambda x, d: lax.dynamic_slice_in_dim(x, reverse_bits(d, now) * size, size, 0)
@@ -446,16 +468,16 @@
         mixed = mixed.reshape(seqs, team, own, block).transpose(1, 0, 2, 3)
     halves = [[h * team + p for p in range(team)] for h in range(2)]
     result = lax.all_to_all(mixed, "ctx", 0, 0, tiled=True, axis_index_groups=halves)
-    parts = 4
     return call(
         join_kernel,
-        (parts,),
+        (1,),
         0,
-        [pl.BlockSpec((team // parts, seqs, own, block), lambda g: (g, 0, 0, 0))],
-        pl.BlockSpec((seqs, own, width // parts), lambda g: (0, 0, g)),
+        [vmem],
+        hbm,
         shape((seqs, own, width), jnp.bfloat16),
         10**5,
         2**20,
+        [pltpu.SemaphoreType.DMA((team, seqs))],
     )(result)
 
 

time: 56.8 us -> 57.8 us (1.018)
  waiting for transfers between devices: 13.4 us -> 15.3 us
    ppermute x5, waiting for transfers between devices: 13.4 us -> 15.3 us  [paired(): return lax.ppermute(x, 'ctx', [(j, j ^ distance) for j in range(devices)])]
    pallas_call x1, Pallas kernels: 3.94 us -> 3.21 us  [body(): call(lambda *refs: prepare_kernel(total_len, bits, *refs), (1,), 2, [hbm]...]
  transfers between devices with their start and end apart: 7 -> 7, of which waited for: 4 -> 4; matrix products, arithmetic and copies ran while one was open for 1% -> 1% of each run, Pallas kernels for 19% -> 18%
where the time goes in v7:
time: 57.8 us; the launch traced here: 57.5 us
  starting transfers between devices  15.3 us (26%)
  waiting for transfers between devices  15.3 us (26%)
  Pallas kernels  13.2 us (23%)
  blocking collectives  13.2 us (23%)
    ppermute x5, waiting for transfers between devices, paired(): return lax.ppermute(x, 'ctx', [(j, j ^ distance) for j in range(devices)])  15.3 us
    all_to_all x1, blocking collectives, body(): lax.all_to_all(mixed, 'ctx', 0, 0, tiled=True, axis_index_groups=halves)  13.2 us
    all_to_all x1, starting transfers between devices, body(): table = lax.all_to_all(columns, 'ctx', 0, 0, tiled=True)  6.95 us
    ppermute x5, starting transfers between devices, paired(): return lax.ppermute(x, 'ctx', [(j, j ^ distance) for j in range(devices)])  5.88 us
    pallas_call x2, Pallas kernels, finish(): call(lambda *refs: kernel(total_len, bits, *refs), (1,), 2, [vmem] * 3, v...  3.54 us
    pallas_call x1, Pallas kernels, body(): call(lambda *refs: prepare_kernel(total_len, bits, *refs), (1,), 2, [hbm]...  3.21 us
    pallas_call x1, Pallas kernels, body(): call(lambda *refs: fresh_kernel(team, *refs), (1,), 1, [vmem] * 4, [vmem]...  2.51 us
    ppermute x1, starting transfers between devices, body(): far = lax.ppermute(near, 'ctx', opposite)  2.5 us
  transfers between devices with their start and end apart: 7, of which 4 were waited for; matrix products, arithmetic and copies ran while one was open for 1% of the time, Pallas kernels for 18%

profile of v7, /device:TPU:0, one launch (start us, length us, event | category | flops | bytes accessed | tf_op | source)
XLA Modules:
  0.0 57.5 jit_solution(16910460149164013081)
XLA Ops:
  0.0 0.5 collective-permute-start
  0.5 3.2 %shard_map.73 = (bf16[32,16,512]{2,1,0:T(8,128)(2,1)}, f32[4,2,16,512]{3,2,1,0:T(8,128)S(1)}, f32[8,16,512]{2,1,0:T(8,128)S(1)}, bf16[4,2,32,512]{3,2,1,0:T(8,128)(2,1)S(1)}) custom-call(s32[1]{0:T(128)} %bitcast.refs_0_, s32[2]{0:T(128)} %refs_1_.6, bf16[16,8192]{1,0:T(8,128)(2,1)} %refs_2_.2, bf16[2,32,8192]{2,1,0:T(8,128)(2,1)} %refs_3_.1, f32[16,8192]{1,0:T(8,128)} %refs_1_.7), custom_call_target="tpu_custom_call" | custom-call | flops 4194304 | bytes 1048576 | tf_op jit(solution)/shard_map/pallas_call | solution.py:366
  3.7 7.0 %all-to-all-start = ((bf16[32,16,512]{2,1,0:T(8,128)(2,1)}), bf16[32,16,512]{2,1,0:T(8,128)(2,1)S(1)}, u32[]{:S(2)}, u32[]{:S(2)}) async-start(bf16[32,16,512]{2,1,0:T(8,128)(2,1)} %get-tuple-element.18), calls=%async_computation | async-start | bytes 1048576 | tf_op jit(solution)/shard_map/all_to_all | solution.py:390
  10.7 0.0 collective-permute-done.refs_2_
  10.7 1.4 %shard_map.75 = f32[4,2,16,512]{3,2,1,0:T(8,128)S(1)} custom-call(s32[1]{0:T(128)} %bitcast.refs_0_, s32[2]{0:T(128)} %refs_1_.6, bf16[2,32,8192]{2,1,0:T(8,128)(2,1)S(1)} %collective-permute-done.refs_2_, f32[4,2,16,512]{3,2,1,0:T(8,128)S(1)} %get-tuple-element.17.refs_3_, f32[8,16,512]{2,1,0:T(8,128)S(1)} %get-tuple-element.16.refs_4_), custom_call_target="tpu_custom_call" | custom-call | flops 4194304 | bytes 1048576 | tf_op jit(solution)/shard_map/pallas_call | solution.py:394
  12.1 1.8 %collective-permute-start.1 = (f32[4,2,16,512]{3,2,1,0:T(8,128)S(1)}, f32[4,2,16,512]{3,2,1,0:T(8,128)S(1)}, u32[]{:S(2)}, u32[]{:S(2)}) collective-permute-start(f32[4,2,16,512]{3,2,1,0:T(8,128)S(1)} %shard_map.75), channel_id=1, source_target_pairs={{0,8},{1,9},{2,10},{3,11},{4,12},{5,13},{6,14},{7,15},{8,0},{9,1},... | collective-permute-start | bytes 786440 | tf_op jit(solution)/shard_map/ppermute | solution.py:359
  14.0 2.1 %shard_map.74 = f32[4,2,16,512]{3,2,1,0:T(8,128)S(1)} custom-call(s32[1]{0:T(128)} %bitcast.refs_0_, s32[2]{0:T(128)} %refs_1_.6, bf16[2,32,8192]{2,1,0:T(8,128)(2,1)S(1)} %collective-permute-done.refs_2_, bf16[4,2,32,512]{3,2,1,0:T(8,128)(2,1)S(1)} %get-tuple-element.15.refs_3_, f32[8,16,512]{2,1,0:T(8,128)S(1)} %get-tuple-element.16.refs_4_), custom_call_target="tpu_custom_call" | custom-call | flops 8388608 | bytes 1048576 | tf_op jit(solution)/shard_map/pallas_call | solution.py:394
  16.1 0.0 copy-start
  16.1 11.5 %collective-permute-done.1 = f32[4,2,16,512]{3,2,1,0:T(8,128)S(1)} collective-permute-done((f32[4,2,16,512]{3,2,1,0:T(8,128)S(1)}, f32[4,2,16,512]{3,2,1,0:T(8,128)S(1)}, u32[]{:S(2)}, u32[]{:S(2)}) %collective-permute-start.1) | collective-permute-done | bytes 262176 | tf_op jit(solution)/shard_map/ppermute | solution.py:359
  27.6 1.5 %collective-permute-start.2 = (f32[1,2,16,512]{3,2,1,0:T(8,128)S(1)}, f32[1,2,16,512]{3,2,1,0:T(8,128)S(1)}, u32[]{:S(2)}, u32[]{:S(2)}) collective-permute-start(f32[1,2,16,512]{3,2,1,0:T(8,128)S(1)} %get-tuple-element.25), channel_id=1, source_target_pairs={{0,2},{1,3},{2,0},{3,1},{4,6},{5,7},{6,4},{7,5},{8,10},{9,11},{10,... | collective-permute-start | bytes 196616 | tf_op jit(solution)/shard_map/ppermute | solution.py:359
  29.2 1.5 %collective-permute-start.4 = (f32[1,2,16,512]{3,2,1,0:T(8,128)S(1)}, f32[1,2,16,512]{3,2,1,0:T(8,128)S(1)}, u32[]{:S(2)}, u32[]{:S(2)}) collective-permute-start(f32[1,2,16,512]{3,2,1,0:T(8,128)S(1)} %get-tuple-element.26), channel_id=1, source_target_pairs={{0,6},{1,7},{2,4},{3,5},{4,2},{5,3},{6,0},{7,1},{8,14},{9,15},{10,... | collective-permute-start | bytes 196616 | tf_op jit(solution)/shard_map/ppermute | solution.py:359
  30.6 0.6 collective-permute-start.3
  31.2 0.8 %collective-permute-done.2 = f32[1,2,16,512]{3,2,1,0:T(8,128)S(1)} collective-permute-done((f32[1,2,16,512]{3,2,1,0:T(8,128)S(1)}, f32[1,2,16,512]{3,2,1,0:T(8,128)S(1)}, u32[]{:S(2)}, u32[]{:S(2)}) %collective-permute-start.2) | collective-permute-done | bytes 65568 | tf_op jit(solution)/shard_map/ppermute | solution.py:359
  32.0 2.3 %collective-permute-done.4 = f32[1,2,16,512]{3,2,1,0:T(8,128)S(1)} collective-permute-done((f32[1,2,16,512]{3,2,1,0:T(8,128)S(1)}, f32[1,2,16,512]{3,2,1,0:T(8,128)S(1)}, u32[]{:S(2)}, u32[]{:S(2)}) %collective-permute-start.4) | collective-permute-done | bytes 65568 | tf_op jit(solution)/shard_map/ppermute | solution.py:359
  34.3 0.7 %collective-permute-done.3 = f32[1,2,16,512]{3,2,1,0:T(8,128)S(1)} collective-permute-done((f32[1,2,16,512]{3,2,1,0:T(8,128)S(1)}, f32[1,2,16,512]{3,2,1,0:T(8,128)S(1)}, u32[]{:S(2)}, u32[]{:S(2)}) %collective-permute-start.3) | collective-permute-done | bytes 65568 | tf_op jit(solution)/shard_map/ppermute | solution.py:359
  35.0 2.5 %collective-permute-start.5 = (f32[2,16,512]{2,1,0:T(8,128)S(1)}, f32[2,16,512]{2,1,0:T(8,128)S(1)}, u32[]{:S(2)}, u32[]{:S(2)}) collective-permute-start(f32[2,16,512]{2,1,0:T(8,128)S(1)} %add_bitcast_fusion.near_ref), channel_id=1, source_target_pairs={{0,16},{1,17},{2,18},{3,19},{4,20},{5,21},{6,22},{7,23},{8,24},{9,... | collective-permute-start | bytes 196616 | tf_op jit(solution)/shard_map/ppermute | solution.py:423
  37.5 0.0 copy-done
  37.5 0.2 fusion.refs_1_
  37.8 1.2 %shard_map.76 = (f32[16,16,512]{2,1,0:T(8,128)S(1)}, f32[16,512]{1,0:T(8,128)S(1)}, f32[3,16,512]{2,1,0:T(8,128)S(1)}, f32[16,16,512]{2,1,0:T(8,128)S(1)}) custom-call(s32[1]{0:T(128)} %bitcast.refs_0_, f32[16,8192]{1,0:T(8,128)} %refs_1_.7, f32[16,8192]{1,0:T(8,128)} %refs_2_.3, f32[1,8192]{1,0:T(1,128)} %bitcast.6), custom_call_target="tpu_custom_call" | custom-call | flops 1000000 | bytes 1048576 | tf_op jit(solution)/shard_map/pallas_call | solution.py:428
  39.0 0.0 all-to-all-done
  39.0 2.5 %shard_map.77 = (f32[2,4,256,128]{3,2,1,0:T(8,128)S(1)}, f32[2,4,256,128]{3,2,1,0:T(8,128)S(1)}) custom-call(s32[1]{0:T(128)} %bitcast.refs_0_, bf16[2,512,512]{2,1,0:T(8,128)(2,1)S(1)} %fusion.refs_1_, bf16[512,512]{1,0:T(8,128)(2,1)S(1)} %bitcast.5, f32[16,512]{1,0:T(8,128)S(1)} %get-tuple-element.19.refs_3_, f32[3,16,512]{2,1,0:T(8,128)S(1)} %get-tuple-element.20.refs_4_), custom_call_target="tpu_custom_call" | custom-call | flops 25165824 | bytes 2097152 | tf_op jit(solution)/shard_map/pallas_call | solution.py:443
  41.5 0.0 collective-permute-done.5.far_ref
  41.5 1.8 %shard_map.78 = bf16[16,2,16,512]{3,2,1,0:T(8,128)(2,1)S(1)} custom-call(f32[2,16,512]{2,1,0:T(8,128)S(1)} %add_bitcast_fusion.near_ref, f32[2,16,512]{2,1,0:T(8,128)S(1)} %collective-permute-done.5.far_ref, f32[2,4,256,128]{3,2,1,0:T(8,128)S(1)} %get-tuple-element.21.conv_ref, f32[2,4,256,128]{3,2,1,0:T(8,128)S(1)} %get-tuple-element.22.carry_ref, ...), custom_call_target="tpu_custom_call" | custom-call | flops 12582912 | bytes 2097152 | tf_op jit(solution)/shard_map/pallas_call | solution.py:456
  43.3 13.2 %all_to_all.10.mixed_ref = bf16[16,2,16,512]{3,2,1,0:T(8,128)(2,1)S(1)} all-to-all(bf16[16,2,16,512]{3,2,1,0:T(8,128)(2,1)S(1)} %shard_map.78), channel_id=1, replica_groups={{0,1,2,3,4,5,6,7,8,9,10,11,12,13,14,15},{16,17,18,19,20,21,22,23,24,25,..., dimensions={0} | all-to-all | bytes 1048576 | tf_op jit(solution)/shard_map/all_to_all | solution.py:470
  56.5 1.1 %shard_map.79 = bf16[2,16,8192]{2,1,0:T(8,128)(2,1)} custom-call(bf16[16,2,16,512]{3,2,1,0:T(8,128)(2,1)S(1)} %all_to_all.10.mixed_ref), custom_call_target="tpu_custom_call" | custom-call | flops 100000 | bytes 1048576 | tf_op jit(solution)/shard_map/pallas_call | solution.py:471
  (3 shorter events, 0.1 us)
Async XLA Ops:
  0.0 10.7 %collective-permute-start = (bf16[2,32,8192]{2,1,0:T(8,128)(2,1)}, bf16[2,32,8192]{2,1,0:T(8,128)(2,1)S(1)}, u32[]{:S(2)}, u32[]{:S(2)}) collective-permute-start(bf16[2,32,8192]{2,1,0:T(8,128)(2,1)} %refs_3_.1), channel_id=1, source_target_pairs={{0,1},{1,0},{2,3},{3,2},{4,5},{5,4},{6,7},{7,6},{8,9},{9,8},{10,11... | collective-permute-start | bytes 3145736 | tf_op jit(solution)/shard_map/ppermute | solution.py:359
  3.7 35.2 %all-to-all-start = ((bf16[32,16,512]{2,1,0:T(8,128)(2,1)}), bf16[32,16,512]{2,1,0:T(8,128)(2,1)S(1)}, u32[]{:S(2)}, u32[]{:S(2)}) async-start(bf16[32,16,512]{2,1,0:T(8,128)(2,1)} %get-tuple-element.18), calls=%async_computation | async-start | bytes 1048576 | tf_op jit(solution)/shard_map/all_to_all | solution.py:390
  12.1 15.4 %collective-permute-start.1 = (f32[4,2,16,512]{3,2,1,0:T(8,128)S(1)}, f32[4,2,16,512]{3,2,1,0:T(8,128)S(1)}, u32[]{:S(2)}, u32[]{:S(2)}) collective-permute-start(f32[4,2,16,512]{3,2,1,0:T(8,128)S(1)} %shard_map.75), channel_id=1, source_target_pairs={{0,8},{1,9},{2,10},{3,11},{4,12},{5,13},{6,14},{7,15},{8,0},{9,1},... | collective-permute-start | bytes 786440 | tf_op jit(solution)/shard_map/ppermute | solution.py:359
  16.1 21.5 %copy-start = (s32[2,512]{1,0:T(2,128)S(1)}, s32[2,512]{1,0:T(2,128)}, u32[]{:S(2)}) copy-start(s32[2,512]{1,0:T(2,128)} %param.9) | copy-start | bytes 12292
  27.6 4.4 %collective-permute-start.2 = (f32[1,2,16,512]{3,2,1,0:T(8,128)S(1)}, f32[1,2,16,512]{3,2,1,0:T(8,128)S(1)}, u32[]{:S(2)}, u32[]{:S(2)}) collective-permute-start(f32[1,2,16,512]{3,2,1,0:T(8,128)S(1)} %get-tuple-element.25), channel_id=1, source_target_pairs={{0,2},{1,3},{2,0},{3,1},{4,6},{5,7},{6,4},{7,5},{8,10},{9,11},{10,... | collective-permute-start | bytes 196616 | tf_op jit(solution)/shard_map/ppermute | solution.py:359
  29.2 5.2 %collective-permute-start.4 = (f32[1,2,16,512]{3,2,1,0:T(8,128)S(1)}, f32[1,2,16,512]{3,2,1,0:T(8,128)S(1)}, u32[]{:S(2)}, u32[]{:S(2)}) collective-permute-start(f32[1,2,16,512]{3,2,1,0:T(8,128)S(1)} %get-tuple-element.26), channel_id=1, source_target_pairs={{0,6},{1,7},{2,4},{3,5},{4,2},{5,3},{6,0},{7,1},{8,14},{9,15},{10,... | collective-permute-start | bytes 196616 | tf_op jit(solution)/shard_map/ppermute | solution.py:359
  30.6 4.4 %collective-permute-start.3 = (f32[1,2,16,512]{3,2,1,0:T(8,128)S(1)}, f32[1,2,16,512]{3,2,1,0:T(8,128)S(1)}, u32[]{:S(2)}, u32[]{:S(2)}) collective-permute-start(f32[1,2,16,512]{3,2,1,0:T(8,128)S(1)} %get-tuple-element.27), channel_id=1, source_target_pairs={{0,4},{1,5},{2,6},{3,7},{4,0},{5,1},{6,2},{7,3},{8,12},{9,13},{10,... | collective-permute-start | bytes 196616 | tf_op jit(solution)/shard_map/ppermute | solution.py:359
  35.0 6.4 %collective-permute-start.5 = (f32[2,16,512]{2,1,0:T(8,128)S(1)}, f32[2,16,512]{2,1,0:T(8,128)S(1)}, u32[]{:S(2)}, u32[]{:S(2)}) collective-permute-start(f32[2,16,512]{2,1,0:T(8,128)S(1)} %add_bitcast_fusion.near_ref), channel_id=1, source_target_pairs={{0,16},{1,17},{2,18},{3,19},{4,20},{5,21},{6,22},{7,23},{8,24},{9,... | collective-permute-start | bytes 196616 | tf_op jit(solution)/shard_map/ppermute | solution.py:423
